TPU v7x, 256 devices: a whole 4x4x8 slice. The times are simulated.
256 devices in a mesh: branch: 2 (over y_lo), seq: 16 (over z, core), mp: 8 (over x, y_hi).
Axes of the slice: x: 4, y: 4 (y_hi: 2, y_lo: 2; y = y_hi * 2 + y_lo), z: 8, core: 2. Of those that a mesh axis runs over, the one named last changes fastest.
Arguments:
- queries: bfloat16 [2, 16, 2048, 2048], P('branch', 'mp', 'seq'), may hold values from -8 to 8
- keys: bfloat16 [2, 16, 2048, 2048], P('branch', 'mp', 'seq'), may hold values from -8 to 8
- values: bfloat16 [2, 16, 2048, 2048], P('branch', 'mp', 'seq'), may hold values from -6 to 6
- inject: float32 [2, 16], P('branch'), may hold values from 0.2 to 0.8
- keyframes: int32 [2], replicated, may hold values from 0 to 15, as said below
- key_mask: int32 [16, 2], replicated, may hold values 0 or 1
Outputs:
- attended: bfloat16 [2, 16, 2048, 2048], P('branch', 'mp', 'seq')
Inputs may be any that keep to these rules, and one draw needn't show every extreme that they name: The keyframes are distinct frames; one of them is the last frame.
All inputs are finite; a program needn't handle non-finite values.
Results may differ from a plain program's by a relative error of at most 0.0061.
Values may be sent and summed in bfloat16 or wider, within the bound.
No kernel may reach another device: no remote copies, remote signals or barrier semaphores. Data moves between devices by JAX's collectives and lax.ppermute only.
A program may use at most 64 MiB of HBM per device.

v0:
```python
import math

import jax
import jax.numpy as jnp
from jax import lax
from jax.sharding import PartitionSpec as P

HEAD = 128


NEG_FILL = -1e30


def swapped(value, axis, bit):
    mask = 2**bit
    pairs = [(source, source ^ mask) for source in range(lax.axis_size(axis))]
    return lax.ppermute(value, axis, pairs)


def from_root(block, axis, holder):
    block = jnp.where(lax.axis_index(axis) == holder, block, jnp.zeros_like(block))
    return lax.psum(block, axis)


def blend_pair(source, partner, strength):
    return (
        (1.0 - strength) * source.astype(jnp.float32) + strength * partner.astype(jnp.float32)
    ).astype(jnp.bfloat16)


def score_tile(query_block, key_tile):
    return jnp.einsum("qhd,khd->hqk", query_block, key_tile, preferred_element_type=jnp.float32) * (
        1.0 / math.sqrt(HEAD)
    )


def attend_frame(query_rows, key_own, value_own, key_extra, value_extra, mask_row):
    frame_rows = query_rows.shape[0]
    row_width = query_rows.shape[1]
    local_heads = row_width // HEAD
    rows_block = min(512, frame_rows)
    key_count = key_extra.shape[0]
    split_queries = query_rows.reshape(frame_rows // rows_block, rows_block, local_heads, HEAD)
    key_own = key_own.reshape(frame_rows, local_heads, HEAD)
    value_own = value_own.reshape(frame_rows, local_heads, HEAD)
    key_extra = key_extra.reshape(key_count, frame_rows, local_heads, HEAD)
    value_extra = value_extra.reshape(key_count, frame_rows, local_heads, HEAD)
    present = mask_row > 0
    valid_keys = jnp.concatenate(
        [jnp.ones((frame_rows,), jnp.bool_), jnp.repeat(present, frame_rows)]
    )
    key_whole = jnp.concatenate(
        [key_own, key_extra.reshape(key_count * frame_rows, local_heads, HEAD)], axis=0
    )
    value_whole = jnp.concatenate(
        [value_own, value_extra.reshape(key_count * frame_rows, local_heads, HEAD)], axis=0
    )

    def one_block(query_block):
        scores = score_tile(query_block, key_whole)
        scores = jnp.where(valid_keys[None, None, :], scores, NEG_FILL)
        row_max = jnp.max(scores, axis=2, keepdims=True)
        weights = jnp.where(valid_keys[None, None, :], jnp.exp(scores - row_max), 0.0)
        totals = jnp.sum(weights, axis=2)
        rounded = weights.astype(jnp.bfloat16)
        mixed_out = jnp.einsum(
            "hqk,khd->qhd", rounded, value_whole, preferred_element_type=jnp.float32
        )
        result = mixed_out / jnp.transpose(totals)[:, :, None]
        return result.reshape(rows_block, row_width).astype(jnp.bfloat16)

    return lax.map(one_block, split_queries).reshape(frame_rows, row_width)


def local(queries, keys, values, inject, keyframes, key_mask):
    frames_dev = queries.shape[1]
    total_heads = inject.shape[1]
    strength = jnp.repeat(inject[0], HEAD, total_repeat_length=total_heads * HEAD)
    partner_queries, partner_keys = swapped((queries, keys), "branch", 0)
    mixed_queries = blend_pair(queries, partner_queries, strength)
    mixed_keys = blend_pair(keys, partner_keys, strength)
    head_queries, head_keys, head_values = (
        lax.all_to_all(mixed_queries, "seq", split_axis=3, concat_axis=2, tiled=True),
        lax.all_to_all(mixed_keys, "seq", split_axis=3, concat_axis=2, tiled=True),
        lax.all_to_all(values, "seq", split_axis=3, concat_axis=2, tiled=True),
    )
    frame_keys = head_keys[0]
    frame_values = head_values[0]
    mp_index = lax.axis_index("mp")
    extra_keys = []
    extra_values = []
    for keyframe_slot in range(keyframes.shape[0]):
        chosen = keyframes[keyframe_slot]
        local_slot = chosen % frames_dev
        chosen_key = lax.dynamic_index_in_dim(frame_keys, local_slot, 0, keepdims=False)
        chosen_value = lax.dynamic_index_in_dim(frame_values, local_slot, 0, keepdims=False)
        got_key, got_value = (
            from_root(chosen_key, "mp", chosen // frames_dev),
            from_root(chosen_value, "mp", chosen // frames_dev),
        )
        extra_keys.append(got_key)
        extra_values.append(got_value)
    key_extra = jnp.stack(extra_keys)
    value_extra = jnp.stack(extra_values)
    outputs = []
    for local_frame in range(frames_dev):
        mask_row = lax.dynamic_index_in_dim(
            key_mask, mp_index * frames_dev + local_frame, 0, keepdims=False
        )
        outputs.append(
            attend_frame(
                head_queries[0, local_frame],
                frame_keys[local_frame],
                frame_values[local_frame],
                key_extra,
                value_extra,
                mask_row,
            )
        )
    attended = jnp.stack(outputs)[None]
    return lax.all_to_all(attended, "seq", split_axis=2, concat_axis=3, tiled=True)


def solution(mesh):
    return jax.shard_map(
        local,
        mesh=mesh,
        in_specs=(
            P("branch", "mp", "seq", None),
            P("branch", "mp", "seq", None),
            P("branch", "mp", "seq", None),
            P("branch", None),
            P(),
            P(),
        ),
        out_specs=P("branch", "mp", "seq", None),
        check_vma=False,
    )
```

profile of v0, /device:TPU:1, one launch (start us, length us, event | category | flops | bytes accessed | tf_op | source)
XLA Modules:
  0.0 387.3 jit_solution(7415376909329658251)
XLA Ops:
  6.5 3.7 copy.89
  10.2 10.0 %all-to-all-start.2 = ((bf16[1,2,128,2048]{2,1,0,3:T(2,128)(2,1)}), bf16[1,2,128,2048]{2,1,0,3:T(2,128)(2,1)S(1)}, u32[]{:S(2)}, u32[]{:S(2)}) async-start(bf16[1,2,128,2048]{2,1,0,3:T(2,128)(2,1)} %copy.89), calls=%async_computation.2 | async-start | bytes 2097152 | tf_op jit(solution)/shard_map/all_to_all | solution.py:85
  21.6 1.9 fusion.86
  23.6 4.3 %compare_select_fusion.1 = (f32[2048,1]{0,1:T(1,128)S(1)}, s32[2048,1]{0,1:T(1,128)S(1)}) fusion(f32[]{:T(128)} %bitcast.27, f32[]{:T(128)} %bitcast.28, f32[]{:T(128)} %bitcast.29, f32[]{:T(128)} %bitcast.30, f32[]{:T(128)} %bitcast.31, f32[]{:T(128)} %bitcast.33, f32[]{:T(128)} %bitcast.32, s32[2048,1]{0,1:T(1,128)S(1)} %bitcast.185, ...), kind=kLoop, calls=%fused_computation.65 | loop fusion | flops 28672 | bytes 32796 | tf_op jit(solution)/shard_map/jit(_take)/gather | solution.py:78
  28.1 5.7 %broadcast_subtract_fusion = (f32[2048]{0:T(1024)S(1)}, f32[2048]{0:T(1024)S(1)}) fusion(pred[2048]{0:T(1024)(128)(4,1)S(1)} %get-tuple-element.163, pred[2048]{0:T(1024)(128)(4,1)S(1)} %get-tuple-element.162, pred[2048]{0:T(1024)(128)(4,1)S(1)} %get-tuple-element.161, pred[2048]{0:T(1024)(128)(4,1)S(1)} %get-tuple-element.160, ...), kind=kLoop, calls=%fused_computation.76 | loop fusion | flops 38912 | bytes 43044 | tf_op jit(solution)/shard_map/sub | solution.py:27
  33.8 11.1 %collective-permute-done = bf16[1,2,128,2048]{3,2,1,0:T(8,128)(2,1)S(1)} collective-permute-done((bf16[1,2,128,2048]{3,2,1,0:T(8,128)(2,1)}, bf16[1,2,128,2048]{3,2,1,0:T(8,128)(2,1)S(1)}, u32[]{:S(2)}, u32[]{:S(2)}) %collective-permute-start) | collective-permute-done | bytes 1048608 | tf_op jit(solution)/shard_map/ppermute | solution.py:17
  44.9 22.5 %collective-permute-done.1 = bf16[1,2,128,2048]{3,2,1,0:T(8,128)(2,1)S(1)} collective-permute-done((bf16[1,2,128,2048]{3,2,1,0:T(8,128)(2,1)}, bf16[1,2,128,2048]{3,2,1,0:T(8,128)(2,1)S(1)}, u32[]{:S(2)}, u32[]{:S(2)}) %collective-permute-start.1) | collective-permute-done | bytes 1048608 | tf_op jit(solution)/shard_map/ppermute | solution.py:17
  67.4 2.4 add_convert_fusion
  69.8 2.0 copy.85
  71.8 7.9 %all-to-all-start.1 = ((bf16[1,2,128,2048]{2,1,0,3:T(2,128)(2,1)}), bf16[1,2,128,2048]{2,1,0,3:T(2,128)(2,1)S(1)}, u32[]{:S(2)}, u32[]{:S(2)}) async-start(bf16[1,2,128,2048]{2,1,0,3:T(2,128)(2,1)} %copy.85), calls=%async_computation.1 | async-start | bytes 2097152 | tf_op jit(solution)/shard_map/all_to_all | solution.py:84
  79.7 2.0 copy.83
  81.7 26.0 %all-to-all-done.1 = bf16[1,2,128,2048]{2,1,0,3:T(2,128)(2,1)S(1)} async-done(((bf16[1,2,128,2048]{2,1,0,3:T(2,128)(2,1)}), bf16[1,2,128,2048]{2,1,0,3:T(2,128)(2,1)S(1)}, u32[]{:S(2)}, u32[]{:S(2)}) %all-to-all-start.1) | async-done | bytes 1048608 | tf_op jit(solution)/shard_map/all_to_all | solution.py:84
  108.7 3.6 all-to-all-start
  122.4 2.9 dynamic-slice_select_fusion.1
  130.5 2.1 copy.87
  132.6 2.1 copy.94
  134.7 5.5 %all-to-all-done = bf16[1,2,128,2048]{2,1,0,3:T(2,128)(2,1)S(1)} async-done(((bf16[1,2,128,2048]{2,1,0,3:T(2,128)(2,1)}), bf16[1,2,128,2048]{2,1,0,3:T(2,128)(2,1)S(1)}, u32[]{:S(2)}, u32[]{:S(2)}) %all-to-all-start) | async-done | bytes 1048608 | tf_op jit(solution)/shard_map/all_to_all | solution.py:83
  142.1 97.8 %all-reduce.5.cloned.1.call-done = (bf16[1,2048,128]{2,1,0:T(8,128)(2,1)}, bf16[1,2048,128]{2,1,0:T(8,128)(2,1)}, bf16[1,2048,128]{2,1,0:T(8,128)(2,1)}, bf16[1,2048,128]{2,1,0:T(8,128)(2,1)}) async-done(((bf16[1,2048,128]{2,1,0:T(8,128)(2,1)}, bf16[1,2048,128]{2,1,0:T(8,128)(2,1)}, bf16[1,2048,128]{2,1,0:T(8,128)(2,1)}, bf16[1,2048,128]{2,1,0:T(8,128)(2,1)}), (bf16[1,2048,128]{2,1,0:T(8,128)(2,1)}, ...) | async-done | bytes 2097168 | tf_op jit(solution)/shard_map/psum | solution.py:22
  239.9 1.4 pad_maximum_fusion.5
  242.6 1.9 pad_maximum_fusion.3
  245.6 42.6 %while.21 = (s32[]{:T(128)}, bf16[4,512,128]{2,1,0:T(8,128)(2,1)}, pred[6144]{0:T(1024)(128)(4,1)S(1)}, bf16[4,512,1,128]{3,1,2,0:T(8,128)(2,1)}, bf16[6144,1,12...) while((s32[]{:T(128)}, bf16[4,512,128]{2,1,0:T(8,128)(2,1)}, ...), condition=%wide.region_7.8_spmd, body=%wide.region_4.7_spmd.sunk | while | flops 1651637248 | bytes 47477864 | solution.py:72
  245.6 3.0 fusion.99
  248.6 3.3 fusion.100
  251.9 4.3 %fusion.101 = bf16[4,512,128]{2,1,0:T(8,128)(2,1)} fusion(bf16[4,512,128]{2,1,0:T(8,128)(2,1)} %get-tuple-element.349, s32[]{:T(128)} %get-tuple-element.348, bf16[6144,1,128]{2,0,1:T(8,128)(2,1)S(1)} %copy-done.4, f32[512,6144]{1,0:T(8,128)S(1)} %get-tuple-element.310, f32[512]{0:T(512)S(1)} %get-tuple-element.311, ...), kind=kOutput, calls=%fused_computation.14.clone.1 | convolution fusion | flops 821166080 | bytes 14297600 | tf_op jit(solution)/shard_map/while/body/eval_jaxpr/hqk,khd->qhd/dot_general | solution.py:66
  256.2 3.0 fusion.99
  259.3 3.3 fusion.100
  262.6 4.3 %fusion.101 = bf16[4,512,128]{2,1,0:T(8,128)(2,1)} fusion(bf16[4,512,128]{2,1,0:T(8,128)(2,1)} %get-tuple-element.349, s32[]{:T(128)} %get-tuple-element.348, bf16[6144,1,128]{2,0,1:T(8,128)(2,1)S(1)} %copy-done.4, f32[512,6144]{1,0:T(8,128)S(1)} %get-tuple-element.310, f32[512]{0:T(512)S(1)} %get-tuple-element.311, ...), kind=kOutput, calls=%fused_computation.14.clone.1 | convolution fusion | flops 821166080 | bytes 14297600 | tf_op jit(solution)/shard_map/while/body/eval_jaxpr/hqk,khd->qhd/dot_general | solution.py:66
  266.9 3.0 fusion.99
  269.9 3.3 fusion.100
  273.2 4.3 %fusion.101 = bf16[4,512,128]{2,1,0:T(8,128)(2,1)} fusion(bf16[4,512,128]{2,1,0:T(8,128)(2,1)} %get-tuple-element.349, s32[]{:T(128)} %get-tuple-element.348, bf16[6144,1,128]{2,0,1:T(8,128)(2,1)S(1)} %copy-done.4, f32[512,6144]{1,0:T(8,128)S(1)} %get-tuple-element.310, f32[512]{0:T(512)S(1)} %get-tuple-element.311, ...), kind=kOutput, calls=%fused_computation.14.clone.1 | convolution fusion | flops 821166080 | bytes 14297600 | tf_op jit(solution)/shard_map/while/body/eval_jaxpr/hqk,khd->qhd/dot_general | solution.py:66
  277.5 3.0 fusion.99
  280.6 3.3 fusion.100
  283.9 4.3 %fusion.101 = bf16[4,512,128]{2,1,0:T(8,128)(2,1)} fusion(bf16[4,512,128]{2,1,0:T(8,128)(2,1)} %get-tuple-element.349, s32[]{:T(128)} %get-tuple-element.348, bf16[6144,1,128]{2,0,1:T(8,128)(2,1)S(1)} %copy-done.4, f32[512,6144]{1,0:T(8,128)S(1)} %get-tuple-element.310, f32[512]{0:T(512)S(1)} %get-tuple-element.311, ...), kind=kOutput, calls=%fused_computation.14.clone.1 | convolution fusion | flops 821166080 | bytes 14297600 | tf_op jit(solution)/shard_map/while/body/eval_jaxpr/hqk,khd->qhd/dot_general | solution.py:66
  288.3 40.7 %while.22 = (s32[]{:T(128)}, bf16[4,512,128]{2,1,0:T(8,128)(2,1)S(1)}, pred[6144]{0:T(1024)(128)(4,1)S(1)}, bf16[4,512,1,128]{3,1,2,0:T(8,128)(2,1)}, bf16[6144,...) while((s32[]{:T(128)}, bf16[4,512,128]{2,1,0:T(8,128)(2,1)S(1)}, ...), condition=%wide.region_11.12_spmd, body=%wide.region_8.11_spmd.sunk | while | flops 1651637248 | bytes 47477356 | solution.py:72
  288.5 3.0 fusion.104
  291.5 3.3 fusion.105
  294.8 3.8 fusion.106
  298.6 3.0 fusion.104
  301.6 3.3 fusion.105
  304.9 3.8 fusion.106
  308.7 3.0 fusion.104
  311.7 3.3 fusion.105
  315.0 3.8 fusion.106
  318.8 3.0 fusion.104
  321.9 3.3 fusion.105
  325.1 3.8 fusion.106
  330.1 8.7 %copy.97 = bf16[1,2,2048,128]{3,1,0,2:T(2,128)(2,1)S(1)} copy(bf16[1,2,2048,128]{3,2,1,0:T(8,128)(2,1)S(1)} %maximum_bitcast_fusion) | data formatting | bytes 2097152 | tf_op jit(solution)/shard_map/broadcast_in_dim | solution.py:120
  338.7 39.5 %all_to_all.66 = bf16[1,2,2048,128]{3,1,0,2:T(2,128)(2,1)S(1)} all-to-all(bf16[1,2,2048,128]{3,1,0,2:T(2,128)(2,1)S(1)} %copy.97), channel_id=1, replica_groups=mesh['branch'=2,'seq'=16,'mp'=8] {'seq'}, dimensions={2} | all-to-all | bytes 2097152 | tf_op jit(solution)/shard_map/all_to_all | solution.py:121
  (60 shorter events, 20.6 us)
Async XLA Ops:
  10.2 61.6 %all-to-all-start.2 = ((bf16[1,2,128,2048]{2,1,0,3:T(2,128)(2,1)}), bf16[1,2,128,2048]{2,1,0,3:T(2,128)(2,1)S(1)}, u32[]{:S(2)}, u32[]{:S(2)}) async-start(bf16[1,2,128,2048]{2,1,0,3:T(2,128)(2,1)} %copy.89), calls=%async_computation.2 | async-start | bytes 2097152 | tf_op jit(solution)/shard_map/all_to_all | solution.py:85
  20.2 24.7 %collective-permute-start = (bf16[1,2,128,2048]{3,2,1,0:T(8,128)(2,1)}, bf16[1,2,128,2048]{3,2,1,0:T(8,128)(2,1)S(1)}, u32[]{:S(2)}, u32[]{:S(2)}) collective-permute-start(bf16[1,2,128,2048]{3,2,1,0:T(8,128)(2,1)} %param.12), channel_id=1, source_target_pairs={{0,128},{128,0},{1,129},{129,1},{2,130},{130,2},{3,131},{131,3},{4... | collective-permute-start | bytes 3145736 | tf_op jit(solution)/shard_map/ppermute | solution.py:17
  21.5 45.9 %collective-permute-start.1 = (bf16[1,2,128,2048]{3,2,1,0:T(8,128)(2,1)}, bf16[1,2,128,2048]{3,2,1,0:T(8,128)(2,1)S(1)}, u32[]{:S(2)}, u32[]{:S(2)}) collective-permute-start(bf16[1,2,128,2048]{3,2,1,0:T(8,128)(2,1)} %param.13), channel_id=1, source_target_pairs={{0,128},{128,0},{1,129},{129,1},{2,130},{130,2},{3,131},{131,3},{4... | collective-permute-start | bytes 3145736 | tf_op jit(solution)/shard_map/ppermute | solution.py:17
  67.4 45.1 %copy-start.6 = (s32[2]{0:T(128)S(1)}, s32[2]{0:T(128)}, u32[]{:S(2)}) copy-start(s32[2]{0:T(128)} %param.16) | copy-start | bytes 28
  71.8 35.9 %all-to-all-start.1 = ((bf16[1,2,128,2048]{2,1,0,3:T(2,128)(2,1)}), bf16[1,2,128,2048]{2,1,0,3:T(2,128)(2,1)S(1)}, u32[]{:S(2)}, u32[]{:S(2)}) async-start(bf16[1,2,128,2048]{2,1,0,3:T(2,128)(2,1)} %copy.85), calls=%async_computation.1 | async-start | bytes 2097152 | tf_op jit(solution)/shard_map/all_to_all | solution.py:84
  107.7 1.0 copy-start
  108.7 31.4 %all-to-all-start = ((bf16[1,2,128,2048]{2,1,0,3:T(2,128)(2,1)}), bf16[1,2,128,2048]{2,1,0,3:T(2,128)(2,1)S(1)}, u32[]{:S(2)}, u32[]{:S(2)}) async-start(bf16[1,2,128,2048]{2,1,0,3:T(2,128)(2,1)} %copy.83), calls=%async_computation | async-start | bytes 2097152 | tf_op jit(solution)/shard_map/all_to_all | solution.py:83
  112.3 127.7 %all-reduce.5.cloned.1.call-start = ((), (), s32[]{:S(2)}) async-start(), calls=%async_computation.4 | async-start | bytes 4194304 | tf_op jit(solution)/shard_map/psum | solution.py:22
  118.3 7.0 %copy-start.5 = (s32[16,2]{0,1:T(2,128)S(1)}, s32[16,2]{0,1:T(2,128)}, u32[]{:S(2)}) copy-start(s32[16,2]{0,1:T(2,128)} %param.17) | copy-start | bytes 388
  239.9 4.6 %copy-start.1 = (bf16[1,1,16,128,128]{4,3,2,1,0:T(8,128)(2,1)S(1)}, bf16[1,1,16,128,128]{4,3,2,1,0:T(8,128)(2,1)}, u32[]{:S(2)}) copy-start(bf16[1,1,16,128,128]{4,3,2,1,0:T(8,128)(2,1)} %copy.87) | copy-start | bytes 1572868
  239.9 4.6 %copy-start.2 = (bf16[1,1,16,128,128]{4,3,2,1,0:T(8,128)(2,1)S(1)}, bf16[1,1,16,128,128]{4,3,2,1,0:T(8,128)(2,1)}, u32[]{:S(2)}) copy-start(bf16[1,1,16,128,128]{4,3,2,1,0:T(8,128)(2,1)} %copy.94) | copy-start | bytes 1572868
  248.6 3.3 copy-start.4
  259.3 3.3 copy-start.4
  269.9 3.3 copy-start.4
  280.6 3.3 copy-start.4
  291.5 3.3 copy-start.3
  301.6 3.3 copy-start.3
  311.7 3.3 copy-start.3
  321.8 3.3 copy-start.3
Sparse Core Ops, SparseCore 0:
  125.4 114.4 all-reduce.4
where the time goes:
time: 388 us; the launch traced here: 387 us
  waiting for transfers between devices  163 us (42%)
  matrix products  56.5 us (15%)
  other arithmetic  47.9 us (12%)
  blocking collectives  39.5 us (10%)
  local copies, waits for them, and re-layouts  38.3 us (10%)
  starting transfers between devices  23.1 us (6%)
  between operations  18.6 us (5%)
    psum x1, waiting for transfers between devices, from_root(): return lax.psum(block, axis)  97.8 us
    all_to_all x1, blocking collectives, local(): lax.all_to_all(attended, 'seq', split_axis=2, concat_axis=3, tiled=True)  39.5 us
    ppermute x2, waiting for transfers between devices, swapped(): return lax.ppermute(value, axis, pairs)  33.6 us
    dot_general x8, matrix products, one_block(): jnp.einsum('hqk,khd->qhd', rounded, value_whole, preferred_element_type=j...  32.3 us
    reduce_sum x8, other arithmetic, one_block(): totals = jnp.sum(weights, axis=2)  26.3 us
    all_to_all x1, waiting for transfers between devices, local(): lax.all_to_all(mixed_keys, 'seq', split_axis=3, concat_axis=2, tiled=True)  26 us
    dot_general x8, matrix products, score_tile(): jnp.einsum('qhd,khd->hqk', query_block, key_tile, preferred_element_type=...  24.2 us
    all_to_all x1, starting transfers between devices, local(): lax.all_to_all(values, 'seq', split_axis=3, concat_axis=2, tiled=True)  9.97 us
  transfers between devices with their start and end apart: 6, of which 5 were waited for; matrix products, arithmetic and copies ran while one was open for 10% of the time, Pallas kernels for 0%

commit v1 on v0

v1 whole, which is shorter than its diff:
```python
import functools
import math

import jax
import jax.numpy as jnp
from jax import lax
from jax.experimental import pallas as pl
from jax.experimental.pallas import tpu as pltpu
from jax.sharding import PartitionSpec as P


HEAD = 128
SCALE = math.log2(math.e) / math.sqrt(HEAD)
SAFE = 100.0
BF16 = jnp.bfloat16
F32 = jnp.float32


def blend_kernel(strength_ref, own_ref, partner_ref, *out_refs, heads):
    first = pl.program_id(0) * heads
    for head in range(heads):
        share = strength_ref[0, first + head]
        lanes = slice(head * HEAD, (head + 1) * HEAD)
        mixed = (
            (1.0 - share) * own_ref[:, :, lanes].astype(F32)
            + share * partner_ref[:, :, lanes].astype(F32)
        ).astype(BF16)
        if len(out_refs) == 1:
            out_refs[0][head] = mixed
        else:
            for frame, out_ref in enumerate(out_refs):
                out_ref[head] = mixed[frame]


def blend_heads(strength, own, partner, per_frame, steps=4):
    frames, rows, width = own.shape
    heads = width // HEAD
    group = heads // steps
    block = pl.BlockSpec((frames, rows, group * HEAD), lambda h: (0, 0, h))
    if per_frame:
        out_specs = [pl.BlockSpec((group, rows, HEAD), lambda h: (h, 0, 0))] * frames
        out_shape = [jax.ShapeDtypeStruct((heads, rows, HEAD), BF16)] * frames
    else:
        out_specs = [pl.BlockSpec((group, frames, rows, HEAD), lambda h: (h, 0, 0, 0))]
        out_shape = [jax.ShapeDtypeStruct((heads, frames, rows, HEAD), BF16)]
    return pl.pallas_call(
        functools.partial(blend_kernel, heads=group),
        grid=(steps,),
        in_specs=[pl.BlockSpec(memory_space=pltpu.SMEM), block, block],
        out_specs=out_specs,
        out_shape=out_shape,
        cost_estimate=pl.CostEstimate(
            flops=3 * own.size, bytes_accessed=6 * own.size, transcendentals=0
        ),
        name="blend",
    )(strength, own, partner)


def dot_nt(a, b):
    return lax.dot_general(a, b, (((1,), (1,)), ((), ())), preferred_element_type=F32)


def scaled_split(query):
    scaled = query.astype(F32) * SCALE
    high = scaled.astype(BF16)
    low = (scaled - high.astype(F32)).astype(BF16)
    return jnp.concatenate([high, low], axis=1)


def score_tile(query_pair, key):
    return dot_nt(query_pair, jnp.concatenate([key, key], axis=1))


def with_ones(value):
    return jnp.concatenate([value, jnp.ones_like(value)], axis=1)


def weighted(weights, value):
    return jnp.dot(weights.astype(BF16), with_ones(value), preferred_element_type=F32)


def norm_max(block):
    as_float = block.astype(F32)
    return jnp.max(jnp.sum(as_float * as_float, axis=1))


def is_safe(query_norm, key_norm):
    return query_norm * key_norm * (SCALE * SCALE) <= SAFE * SAFE


def tiles_of(ref, lead, tile):
    blocks, rows = ref.shape[-3], ref.shape[-2]
    step = max(1, tile // rows)
    for start in range(0, blocks, step):
        stop = min(blocks, start + step)
        yield lambda start=start, stop=stop: ref[lead + (slice(start, stop),)].reshape(
            (stop - start) * rows, HEAD
        )


def pairs_of(key_refs, value_refs, lead, tile):
    for key_ref, value_ref in zip(key_refs, value_refs):
        yield from zip(tiles_of(key_ref, lead, tile), tiles_of(value_ref, lead, tile))


def own_kernel(query_ref, key_ref, value_ref, acc_ref, norm_ref, *, tile):
    @pl.when(pl.program_id(0) == 0)
    def _():
        norm_ref[0] = norm_max(key_ref[...].reshape(-1, HEAD))

    query = query_ref[...].reshape(-1, HEAD)

    @pl.when(is_safe(norm_max(query), norm_ref[0]))
    def _():
        pair = scaled_split(query)
        for index, (key, value) in enumerate(pairs_of([key_ref], [value_ref], (), tile)):
            part = weighted(jnp.exp2(score_tile(pair, key())), value())
            acc_ref[...] = part if index == 0 else acc_ref[...] + part


def extra_kernel(
    valid_ref, query_ref, key_ref, value_ref, *refs, tile, pieces, extras
):
    key_extra = refs[:pieces]
    value_extra = refs[pieces : 2 * pieces]
    *acc_in, out_ref, norm_ref, acc_ref, max_ref = refs[2 * pieces :]
    blocks, rows = query_ref.shape[0], query_ref.shape[1]

    @pl.when(pl.program_id(0) == 0)
    def _():
        norm = norm_max(key_ref[...].reshape(-1, HEAD))
        for ref in key_extra:
            norm = jnp.maximum(norm, norm_max(ref[...].reshape(-1, HEAD)))
        norm_ref[0] = norm

    query = query_ref[...].reshape(-1, HEAD)
    safe = is_safe(norm_max(query), norm_ref[0])

    @pl.when(safe)
    def _():
        pair = scaled_split(query)
        if acc_in:
            acc_ref[...] = acc_in[0][...]
        else:
            for index, (key, value) in enumerate(pairs_of([key_ref], [value_ref], (), tile)):
                part = weighted(jnp.exp2(score_tile(pair, key())), value())
                acc_ref[...] = part if index == 0 else acc_ref[...] + part

        def one_extra(slot, carry):
            @pl.when(valid_ref[slot] > 0)
            def _():
                for key, value in pairs_of(key_extra, value_extra, (slot,), tile):
                    acc_ref[...] += weighted(jnp.exp2(score_tile(pair, key())), value())

            return carry

        lax.fori_loop(0, extras, one_extra, 0)
        acc = acc_ref[...]
        out_ref[...] = (acc[:, :HEAD] / acc[:, HEAD:]).astype(BF16).reshape(out_ref.shape)

    @pl.when(jnp.logical_not(safe))
    def _():
        def one_block(block, carry):
            pair = scaled_split(query_ref[block])
            acc_slow = acc_ref.at[pl.ds(0, rows)]

            def step(key, value, first):
                scores = score_tile(pair, key)
                top = jnp.max(scores, axis=1, keepdims=True)
                if first:
                    new_max = top
                else:
                    old_max = max_ref[:, :1]
                    new_max = jnp.maximum(old_max, top)
                part = weighted(jnp.exp2(scores - new_max), value)
                if first:
                    acc_slow[...] = part
                else:
                    acc_slow[...] = acc_slow[...] * jnp.exp2(old_max - new_max) + part
                max_ref[...] = jnp.broadcast_to(new_max, max_ref.shape)

            for index, (key, value) in enumerate(pairs_of([key_ref], [value_ref], (), 512)):
                step(key(), value(), index == 0)

            def one_extra(slot, carry):
                @pl.when(valid_ref[slot] > 0)
                def _():
                    for key, value in pairs_of(key_extra, value_extra, (slot,), 512):
                        step(key(), value(), False)

                return carry

            lax.fori_loop(0, extras, one_extra, 0)
            acc = acc_slow[...]
            out_ref[block] = (acc[:, :HEAD] / acc[:, HEAD:]).astype(BF16)
            return carry

        lax.fori_loop(0, blocks, one_block, 0)


def whole(array):
    return pl.BlockSpec(
        array.shape, lambda i: (0,) * array.ndim, pipeline_mode=pl.Buffered(1)
    )


def frame_of(array, frame):
    blocks, _, rows, width = array.shape
    return pl.BlockSpec(
        (blocks, None, rows, width), lambda i: (0, frame, 0, 0), pipeline_mode=pl.Buffered(1)
    )


def attention_cost(queries, keys):
    return pl.CostEstimate(
        flops=4 * queries * keys * HEAD,
        bytes_accessed=4 * (queries + keys) * HEAD,
        transcendentals=queries * keys,
    )


def attend_own(frame, query, key, value, steps, tile):
    blocks, rows, _ = query.shape
    per_step = blocks // steps
    total = blocks * rows
    return pl.pallas_call(
        functools.partial(own_kernel, tile=tile),
        grid=(steps,),
        in_specs=[
            pl.BlockSpec((per_step, rows, HEAD), lambda i: (i, 0, 0)),
            frame_of(key, frame),
            frame_of(value, frame),
        ],
        out_specs=pl.BlockSpec((per_step * rows, 2 * HEAD), lambda i: (i, 0)),
        out_shape=jax.ShapeDtypeStruct((total, 2 * HEAD), F32),
        scratch_shapes=[pltpu.SMEM((1,), F32)],
        compiler_params=pltpu.CompilerParams(vmem_limit_bytes=24 << 20),
        cost_estimate=attention_cost(total, total),
        name="attend_own",
    )(query, key, value)


def attend_extra(frame, valid, query, key, value, key_extra, value_extra, acc, steps, tile):
    blocks, rows, _ = query.shape
    per_step = blocks // steps
    total = blocks * rows
    pieces = len(key_extra)
    extras = valid.shape[0]
    acc = [] if acc is None else [acc]
    return pl.pallas_call(
        functools.partial(extra_kernel, tile=tile, pieces=pieces, extras=extras),
        grid=(steps,),
        in_specs=[
            pl.BlockSpec(memory_space=pltpu.SMEM),
            pl.BlockSpec((per_step, rows, HEAD), lambda i: (i, 0, 0)),
            frame_of(key, frame),
            frame_of(value, frame),
            *[whole(a) for a in key_extra],
            *[whole(a) for a in value_extra],
            *[pl.BlockSpec((per_step * rows, 2 * HEAD), lambda i: (i, 0)) for _ in acc],
        ],
        out_specs=pl.BlockSpec((per_step, rows, HEAD), lambda i: (i, 0, 0)),
        out_shape=jax.ShapeDtypeStruct((blocks, rows, HEAD), BF16),
        scratch_shapes=[
            pltpu.SMEM((1,), F32),
            pltpu.VMEM((per_step * rows, 2 * HEAD), F32),
            pltpu.VMEM((rows, HEAD), F32),
        ],
        compiler_params=pltpu.CompilerParams(vmem_limit_bytes=24 << 20),
        cost_estimate=attention_cost(total, extras * total),
        name="attend_extra",
    )(valid, query, key, value, *key_extra, *value_extra, *acc)


def cut_kernel(place_ref, keyframes_ref, source_ref, *out_refs, xs):
    blocks, frames = source_ref.shape[:2]
    quarter = blocks // xs
    x = place_ref[0] // 2
    for step, out_ref in enumerate(out_refs, 1):
        start = lax.rem(x + step, xs) * quarter
        for j in range(out_ref.shape[0]):
            slot = lax.rem(keyframes_ref[j], frames)
            for block in range(quarter):
                out_ref[j, block] = source_ref[start + block, slot]


def pick_x_kernel(place_ref, keyframes_ref, source_ref, *refs):
    *got_refs, out_ref = refs
    xs = len(got_refs) + 1
    blocks, frames = source_ref.shape[:2]
    quarter = blocks // xs
    x = place_ref[0] // 2
    for j in range(out_ref.shape[0]):
        keyframe = keyframes_ref[j]
        step = lax.rem(x - keyframe // (2 * frames) + xs, xs)

        @pl.when(step == 0)
        def _():
            slot = lax.rem(keyframe, frames)
            for block in range(quarter):
                out_ref[j, block] = source_ref[x * quarter + block, slot]

        for which, got_ref in enumerate(got_refs, 1):

            @pl.when(step == which)
            def _():
                out_ref[j] = got_ref[j]


def pick_y_kernel(place_ref, keyframes_ref, mine_ref, other_ref, out_ref, *, frames):
    y = lax.rem(place_ref[0], 2)
    for j in range(out_ref.shape[0]):
        same = lax.rem(keyframes_ref[j] // frames, 2) == y

        @pl.when(same)
        def _():
            out_ref[j] = mine_ref[j]

        @pl.when(jnp.logical_not(same))
        def _():
            out_ref[j] = other_ref[j]


def move_call(kernel, out_shapes, place, keyframes, *arrays):
    smem = pl.BlockSpec(memory_space=pltpu.SMEM)
    vmem = pl.BlockSpec(memory_space=pltpu.VMEM)
    moved = sum(a.size for a in arrays) + sum(math.prod(o.shape) for o in out_shapes)
    return pl.pallas_call(
        kernel,
        in_specs=[smem, smem] + [vmem] * len(arrays),
        out_specs=[vmem] * len(out_shapes),
        out_shape=out_shapes,
        cost_estimate=pl.CostEstimate(flops=0, bytes_accessed=2 * moved, transcendentals=0),
    )(place, keyframes, *arrays)


def piece_shape(keyframes, by_frame, xs):
    blocks, _, rows, width = by_frame.shape
    return jax.ShapeDtypeStruct((keyframes.shape[0], blocks // xs, rows, width), BF16)


def cut_pieces(place, keyframes, by_frame, xs):
    return move_call(
        functools.partial(cut_kernel, xs=xs),
        [piece_shape(keyframes, by_frame, xs)] * (xs - 1), place, keyframes, by_frame,
    )


def pick_along_x(place, keyframes, by_frame, got):
    return move_call(
        pick_x_kernel,
        [piece_shape(keyframes, by_frame, len(got) + 1)], place, keyframes, by_frame, *got,
    )[0]


def pick_along_y(place, keyframes, mine, other, frames):
    return move_call(
        functools.partial(pick_y_kernel, frames=frames),
        [jax.ShapeDtypeStruct(mine.shape, BF16)], place, keyframes, mine, other,
    )[0]


def swap_branch(value):
    return lax.ppermute(value, "branch", [(0, 1), (1, 0)])


def to_heads(value):
    return lax.all_to_all(value, "seq", split_axis=0, concat_axis=0, tiled=True)


def shift_x(value, step):
    size = lax.axis_size("mp")
    return lax.ppermute(value, "mp", [(m, (m + 2 * step) % size) for m in range(size)])


def flip_y(value):
    size = lax.axis_size("mp")
    return lax.ppermute(value, "mp", [(m, m ^ 1) for m in range(size)])


def spread_keyframes(by_frame, keyframes):
    place = lax.axis_index("mp").astype(jnp.int32).reshape(1)
    xs = lax.axis_size("mp") // 2
    pieces = cut_pieces(place, keyframes, by_frame, xs)
    got = [shift_x(piece, step) for step, piece in enumerate(pieces, 1)]
    mine = pick_along_x(place, keyframes, by_frame, got)
    other = flip_y(mine)
    mine = pick_along_y(place, keyframes, mine, other, by_frame.shape[1])
    return [mine] + [shift_x(mine, step) for step in range(1, xs)]


def by_head(block):
    frames, rows, width = block.shape
    return block.reshape(frames, rows, width // HEAD, HEAD).transpose(2, 0, 1, 3)


def local(queries, keys, values, inject, keyframes, key_mask):
    queries, keys, values = queries[0], keys[0], values[0]
    frames = queries.shape[0]
    partner_keys = swap_branch(keys)
    partner_queries = swap_branch(queries)

    value_rows = by_head(values)
    value_heads = to_heads(value_rows)
    value_extra = spread_keyframes(value_heads, keyframes)

    (key_rows,) = blend_heads(inject, keys, partner_keys, False)
    key_heads = to_heads(key_rows)
    key_source, *value_extra = lax.optimization_barrier((key_heads, *value_extra))
    key_extra = spread_keyframes(key_source, keyframes)

    query_rows = blend_heads(inject, queries, partner_queries, True)
    query_frames = []
    for f in range(frames):
        query_frames.append(to_heads(query_rows[f]))

    first = lax.axis_index("mp") * frames
    outs = []
    for f in range(frames):
        acc = None
        if f == 0:
            acc = attend_own(f, query_frames[f], key_heads, value_heads, 2, 512)
        valid = lax.dynamic_index_in_dim(key_mask, first + f, 0, keepdims=False)
        out = attend_extra(
            f, valid, query_frames[f], key_heads, value_heads,
            key_extra, value_extra, acc, 2, 512,
        )
        back = to_heads(out)
        heads, rows, _ = back.shape
        outs.append(back.transpose(1, 0, 2).reshape(rows, heads * HEAD))
    return jnp.stack(outs)[None]


def solution(mesh):
    return jax.shard_map(
        local,
        mesh=mesh,
        in_specs=(
            P("branch", "mp", "seq", None),
            P("branch", "mp", "seq", None),
            P("branch", "mp", "seq", None),
            P("branch", None),
            P(),
            P(),
        ),
        out_specs=P("branch", "mp", "seq", None),
        check_vma=False,
    )
```

time: 388 us -> 293 us (0.76)
  the two profiles are of different devices: /device:TPU:1 before, /device:TPU:23 now
where the time goes in v1:
time: 293 us; the launch traced here: 292 us
  Pallas kernels  108 us (37%)
  waiting for transfers between devices  107 us (37%)
  starting transfers between devices  62.7 us (21%)
  local copies, waits for them, and re-layouts  14 us (5%)
    pallas_call x2, Pallas kernels, attend_extra(): pl.pallas_call(functools.partial(extra_kernel, tile=tile, pieces=pieces,...  84.5 us
    all_to_all x6, starting transfers between devices, to_heads(): return lax.all_to_all(value, 'seq', split_axis=0, concat_axis=0, tiled=True)  48 us
    ppermute x2, waiting for transfers between devices, swap_branch(): return lax.ppermute(value, 'branch', [(0, 1), (1, 0)])  43 us
    ppermute x12, waiting for transfers between devices, shift_x(): lax.ppermute(value, 'mp', [(m, (m + 2 * step) % size) for m in range(size)])  28.8 us
    ppermute x2, waiting for transfers between devices, flip_y(): return lax.ppermute(value, 'mp', [(m, m ^ 1) for m in range(size)])  18.3 us
    all_to_all x6, waiting for transfers between devices, to_heads(): return lax.all_to_all(value, 'seq', split_axis=0, concat_axis=0, tiled=True)  16.9 us
    ppermute x12, starting transfers between devices, shift_x(): lax.ppermute(value, 'mp', [(m, (m + 2 * step) % size) for m in range(size)])  12.5 us
    pallas_call x6, Pallas kernels, move_call(): pl.pallas_call(kernel, in_specs=[smem, smem] + [vmem] * len(arrays), out_...  12.4 us
  transfers between devices with their start and end apart: 22, of which 13 were waited for; matrix products, arithmetic and copies ran while one was open for 0% of the time, Pallas kernels for 37%

profile of v1, /device:TPU:23, one launch (start us, length us, event | category | flops | bytes accessed | tf_op | source)
XLA Modules:
  0.0 292.2 jit_solution(13098787040156184380)
XLA Ops:
  0.0 1.6 copy.7
  1.6 1.3 copy.8
  3.0 9.3 %all-to-all-start.2 = ((bf16[16,2,128,128]{3,2,1,0:T(8,128)(2,1)}), bf16[16,2,128,128]{3,2,1,0:T(8,128)(2,1)S(1)}, u32[]{:S(2)}, u32[]{:S(2)}) async-start(bf16[16,2,128,128]{3,2,1,0:T(8,128)(2,1)} %bitcast.3), calls=%async_computation.2 | async-start | bytes 2097152 | tf_op jit(solution)/shard_map/all_to_all | solution.py:368
  12.2 1.1 collective-permute-start.1
  13.3 23.7 %collective-permute-done.1.partner_ref = bf16[2,128,2048]{2,1,0:T(8,128)(2,1)} collective-permute-done((bf16[2,128,2048]{2,1,0:T(8,128)(2,1)S(1)}, bf16[2,128,2048]{2,1,0:T(8,128)(2,1)}, u32[]{:S(2)}, u32[]{:S(2)}) %collective-permute-start.1) | collective-permute-done | bytes 1048608 | tf_op jit(solution)/shard_map/ppermute | solution.py:364
  37.1 3.7 %blend.3 = bf16[16,2,128,128]{3,2,1,0:T(8,128)(2,1)} custom-call(f32[1,16]{1,0:T(1,128)} %strength_ref.3, bf16[2,128,2048]{2,1,0:T(8,128)(2,1)} %bitcast.18, bf16[2,128,2048]{2,1,0:T(8,128)(2,1)} %collective-permute-done.1.partner_ref), custom_call_target="tpu_custom_call" | custom-call | flops 1572864 | bytes 3145728 | tf_op jit(solution)/shard_map/blend/pallas_call | solution.py:46
  40.8 7.8 %all-to-all-start.1 = ((bf16[16,2,128,128]{3,2,1,0:T(8,128)(2,1)}), bf16[16,2,128,128]{3,2,1,0:T(8,128)(2,1)S(1)}, u32[]{:S(2)}, u32[]{:S(2)}) async-start(bf16[16,2,128,128]{3,2,1,0:T(8,128)(2,1)} %blend.3), calls=%async_computation.1 | async-start | bytes 2097152 | tf_op jit(solution)/shard_map/all_to_all | solution.py:368
  48.6 1.0 collective-permute-start
  49.6 2.2 shard_map.64
  52.0 2.1 collective-permute-start.3
  54.1 19.3 %collective-permute-done.partner_ref = bf16[2,128,2048]{2,1,0:T(8,128)(2,1)} collective-permute-done((bf16[2,128,2048]{2,1,0:T(8,128)(2,1)}, bf16[2,128,2048]{2,1,0:T(8,128)(2,1)}, u32[]{:S(2)}, u32[]{:S(2)}) %collective-permute-start) | collective-permute-done | bytes 1048608 | tf_op jit(solution)/shard_map/ppermute | solution.py:364
  73.4 3.7 %blend.2 = (bf16[16,128,128]{2,1,0:T(8,128)(2,1)}, bf16[16,128,128]{2,1,0:T(8,128)(2,1)}) custom-call(f32[1,16]{1,0:T(1,128)} %strength_ref.3, bf16[2,128,2048]{2,1,0:T(8,128)(2,1)} %bitcast.17, bf16[2,128,2048]{2,1,0:T(8,128)(2,1)} %collective-permute-done.partner_ref), custom_call_target="tpu_custom_call" | custom-call | flops 1572864 | bytes 3145728 | tf_op jit(solution)/shard_map/blend/pallas_call | solution.py:46
  77.2 7.9 %all-to-all-start.4 = ((bf16[16,128,128]{2,1,0:T(8,128)(2,1)}), bf16[16,128,128]{2,1,0:T(8,128)(2,1)S(1)}, u32[]{:S(2)}, u32[]{:S(2)}) async-start(bf16[16,128,128]{2,1,0:T(8,128)(2,1)} %get-tuple-element.30), calls=%async_computation.4 | async-start | bytes 1048576 | tf_op jit(solution)/shard_map/all_to_all | solution.py:368
  86.6 2.2 shard_map.65.mine_ref
  88.9 9.4 %collective-permute-done.5.other_ref = bf16[2,4,128,128]{3,2,1,0:T(8,128)(2,1)S(1)} collective-permute-done((bf16[2,4,128,128]{3,2,1,0:T(8,128)(2,1)}, bf16[2,4,128,128]{3,2,1,0:T(8,128)(2,1)S(1)}, u32[]{:S(2)}, u32[]{:S(2)}) %collective-permute-start.5) | collective-permute-done | bytes 262176 | tf_op jit(solution)/shard_map/ppermute | solution.py:378
  98.3 0.7 copy-done.18
  99.0 1.8 shard_map.66.refs_4_
  101.3 0.8 collective-permute-start.7
  102.2 1.8 collective-permute-start.6
  104.0 6.4 %collective-permute-done.8.refs_7_ = bf16[2,4,128,128]{3,2,1,0:T(8,128)(2,1)S(1)} collective-permute-done((bf16[2,4,128,128]{3,2,1,0:T(8,128)(2,1)}, bf16[2,4,128,128]{3,2,1,0:T(8,128)(2,1)S(1)}, u32[]{:S(2)}, u32[]{:S(2)}) %collective-permute-start.8) | collective-permute-done | bytes 262176 | tf_op jit(solution)/shard_map/ppermute | solution.py:373
  111.1 2.4 collective-permute-done.7.refs_6_
  114.2 1.5 collective-permute-done.6.refs_5_
  115.7 0.7 copy-done.14
  116.5 2.2 shard_map.67
  118.7 3.4 %collective-permute-start.9 = (bf16[2,4,128,128]{3,2,1,0:T(8,128)(2,1)}, bf16[2,4,128,128]{3,2,1,0:T(8,128)(2,1)}, u32[]{:S(2)}, u32[]{:S(2)}) collective-permute-start(bf16[2,4,128,128]{3,2,1,0:T(8,128)(2,1)} %get-tuple-element.23), channel_id=1, source_target_pairs={{0,2},{1,3},{2,4},{3,5},{4,6},{5,7},{6,0},{7,1},{8,10},{9,11},{10,... | collective-permute-start | bytes 786440 | tf_op jit(solution)/shard_map/ppermute | solution.py:373
  122.7 7.6 %all-to-all-start = ((bf16[16,128,128]{2,1,0:T(8,128)(2,1)}), bf16[16,128,128]{2,1,0:T(8,128)(2,1)S(1)}, u32[]{:S(2)}, u32[]{:S(2)}) async-start(bf16[16,128,128]{2,1,0:T(8,128)(2,1)} %get-tuple-element.18), calls=%async_computation | async-start | bytes 1048576 | tf_op jit(solution)/shard_map/all_to_all | solution.py:368
  130.3 2.8 collective-permute-done.9.refs_0_
  133.1 4.0 %collective-permute-done.11.refs_2_ = bf16[2,4,128,128]{3,2,1,0:T(8,128)(2,1)} collective-permute-done((bf16[2,4,128,128]{3,2,1,0:T(8,128)(2,1)}, bf16[2,4,128,128]{3,2,1,0:T(8,128)(2,1)}, u32[]{:S(2)}, u32[]{:S(2)}) %collective-permute-start.11) | collective-permute-done | bytes 262176 | tf_op jit(solution)/shard_map/ppermute | solution.py:373
  137.1 2.2 shard_map.68.mine_ref
  139.4 8.8 %collective-permute-done.12.other_ref = bf16[2,4,128,128]{3,2,1,0:T(8,128)(2,1)} collective-permute-done((bf16[2,4,128,128]{3,2,1,0:T(8,128)(2,1)}, bf16[2,4,128,128]{3,2,1,0:T(8,128)(2,1)}, u32[]{:S(2)}, u32[]{:S(2)}) %collective-permute-start.12) | collective-permute-done | bytes 262176 | tf_op jit(solution)/shard_map/ppermute | solution.py:378
  148.3 1.8 shard_map.69.refs_0_
  150.1 0.9 collective-permute-start.14
  150.9 2.1 collective-permute-start.13
  153.2 7.0 %collective-permute-done.15.refs_3_ = bf16[2,4,128,128]{3,2,1,0:T(8,128)(2,1)} collective-permute-done((bf16[2,4,128,128]{3,2,1,0:T(8,128)(2,1)}, bf16[2,4,128,128]{3,2,1,0:T(8,128)(2,1)}, u32[]{:S(2)}, u32[]{:S(2)}) %collective-permute-start.15) | collective-permute-done | bytes 262176 | tf_op jit(solution)/shard_map/ppermute | solution.py:373
  160.2 1.3 collective-permute-done.14.refs_2_
  161.5 3.4 %collective-permute-done.13.refs_1_ = bf16[2,4,128,128]{3,2,1,0:T(8,128)(2,1)} collective-permute-done((bf16[2,4,128,128]{3,2,1,0:T(8,128)(2,1)}, bf16[2,4,128,128]{3,2,1,0:T(8,128)(2,1)}, u32[]{:S(2)}, u32[]{:S(2)}) %collective-permute-start.13) | collective-permute-done | bytes 262176 | tf_op jit(solution)/shard_map/ppermute | solution.py:373
  164.9 0.9 copy-done.6
  165.9 0.9 copy-done.9
  166.8 0.9 copy-done.12
  167.8 0.9 copy-done.15
  168.7 51.0 %attend_extra.3 = bf16[16,128,128]{2,1,0:T(8,128)(2,1)S(1)} custom-call(s32[2]{0:T(128)S(1)} %get-tuple-element.32.valid_ref, bf16[16,128,128]{2,1,0:T(8,128)(2,1)S(1)} %all-to-all-done.4.query_ref, bf16[16,2,128,128]{3,2,1,0:T(8,128)(2,1)S(1)} %copy-done.1, bf16[16,2,128,128]{3,2,1,0:T(8,128)(2,1)S(1)} %copy-done.3, bf16[2,4,128,128]{3,2,1,0:T(8,128)(2,1)S(1)} %copy-done.6, ...), custom_call_target="tpu_custom_call" | custom-call | flops 4294967296 | bytes 3145728 | tf_op jit(solution)/shard_map/attend_extra/pallas_call | solution.py:250
  219.7 0.8 copy-done.4
  220.5 8.2 %all-to-all-start.5 = ((bf16[16,128,128]{2,1,0:T(8,128)(2,1)}), bf16[16,128,128]{2,1,0:T(8,128)(2,1)S(1)}, u32[]{:S(2)}, u32[]{:S(2)}) async-start(bf16[16,128,128]{2,1,0:T(8,128)(2,1)} %copy-done.4), calls=%async_computation.5 | async-start | bytes 1048576 | tf_op jit(solution)/shard_map/all_to_all | solution.py:368
  228.7 3.7 %attend_own.1.refs_8_ = f32[2048,256]{1,0:T(8,128)S(1)} custom-call(bf16[16,128,128]{2,1,0:T(8,128)(2,1)S(1)} %all-to-all-done.query_ref, bf16[16,2,128,128]{3,2,1,0:T(8,128)(2,1)S(1)} %copy-done.1, bf16[16,2,128,128]{3,2,1,0:T(8,128)(2,1)S(1)} %copy-done.3), custom_call_target="tpu_custom_call" | custom-call | flops 2147483648 | bytes 2097152 | tf_op jit(solution)/shard_map/attend_own/pallas_call | solution.py:226
  232.5 33.6 %attend_extra.2 = bf16[16,128,128]{2,1,0:T(8,128)(2,1)} custom-call(s32[2]{0:T(128)S(1)} %get-tuple-element.31.valid_ref, bf16[16,128,128]{2,1,0:T(8,128)(2,1)S(1)} %all-to-all-done.query_ref, bf16[16,2,128,128]{3,2,1,0:T(8,128)(2,1)S(1)} %copy-done.1, bf16[16,2,128,128]{3,2,1,0:T(8,128)(2,1)S(1)} %copy-done.3, bf16[2,4,128,128]{3,2,1,0:T(8,128)(2,1)S(1)} %copy-done.7, ...), custom_call_target="tpu_custom_call" | custom-call | flops 4294967296 | bytes 3145728 | tf_op jit(solution)/shard_map/attend_extra/pallas_call | solution.py:250
  266.1 7.2 %all-to-all-start.3 = ((bf16[16,128,128]{2,1,0:T(8,128)(2,1)}), bf16[16,128,128]{2,1,0:T(8,128)(2,1)S(1)}, u32[]{:S(2)}, u32[]{:S(2)}) async-start(bf16[16,128,128]{2,1,0:T(8,128)(2,1)} %attend_extra.2), calls=%async_computation.3 | async-start | bytes 1048576 | tf_op jit(solution)/shard_map/all_to_all | solution.py:368
  273.6 16.9 %all-to-all-done.3 = bf16[16,128,128]{2,1,0:T(8,128)(2,1)S(1)} async-done(((bf16[16,128,128]{2,1,0:T(8,128)(2,1)}), bf16[16,128,128]{2,1,0:T(8,128)(2,1)S(1)}, u32[]{:S(2)}, u32[]{:S(2)}) %all-to-all-start.3) | async-done | bytes 524320 | tf_op jit(solution)/shard_map/all_to_all | solution.py:368
  290.9 1.3 copy.11
  (60 shorter events, 5.4 us)
Async XLA Ops:
  3.0 9.3 %copy-start.17 = (bf16[1,2,128,2048]{3,2,1,0:T(8,128)(2,1)S(1)}, bf16[1,2,128,2048]{3,2,1,0:T(8,128)(2,1)}, u32[]{:S(2)}) copy-start(bf16[1,2,128,2048]{3,2,1,0:T(8,128)(2,1)} %param.7) | copy-start | bytes 3145732
  3.0 37.8 %all-to-all-start.2 = ((bf16[16,2,128,128]{3,2,1,0:T(8,128)(2,1)}), bf16[16,2,128,128]{3,2,1,0:T(8,128)(2,1)S(1)}, u32[]{:S(2)}, u32[]{:S(2)}) async-start(bf16[16,2,128,128]{3,2,1,0:T(8,128)(2,1)} %bitcast.3), calls=%async_computation.2 | async-start | bytes 2097152 | tf_op jit(solution)/shard_map/all_to_all | solution.py:368
  12.2 24.8 %collective-permute-start.1 = (bf16[2,128,2048]{2,1,0:T(8,128)(2,1)S(1)}, bf16[2,128,2048]{2,1,0:T(8,128)(2,1)}, u32[]{:S(2)}, u32[]{:S(2)}) collective-permute-start(bf16[2,128,2048]{2,1,0:T(8,128)(2,1)S(1)} %bitcast.19), channel_id=1, source_target_pairs={{0,128},{128,0},{1,129},{129,1},{2,130},{130,2},{3,131},{131,3},{4... | collective-permute-start | bytes 3145736 | tf_op jit(solution)/shard_map/ppermute | solution.py:364
  40.8 8.8 %copy-start.2 = (bf16[16,2,128,128]{3,2,1,0:T(8,128)(2,1)}, bf16[16,2,128,128]{3,2,1,0:T(8,128)(2,1)S(1)}, u32[]{:S(2)}) copy-start(bf16[16,2,128,128]{3,2,1,0:T(8,128)(2,1)S(1)} %all-to-all-done.2.source_ref.value_ref) | copy-start | bytes 3145732
  40.8 36.4 %all-to-all-start.1 = ((bf16[16,2,128,128]{3,2,1,0:T(8,128)(2,1)}), bf16[16,2,128,128]{3,2,1,0:T(8,128)(2,1)S(1)}, u32[]{:S(2)}, u32[]{:S(2)}) async-start(bf16[16,2,128,128]{3,2,1,0:T(8,128)(2,1)} %blend.3), calls=%async_computation.1 | async-start | bytes 2097152 | tf_op jit(solution)/shard_map/all_to_all | solution.py:368
  48.6 24.8 %collective-permute-start = (bf16[2,128,2048]{2,1,0:T(8,128)(2,1)}, bf16[2,128,2048]{2,1,0:T(8,128)(2,1)}, u32[]{:S(2)}, u32[]{:S(2)}) collective-permute-start(bf16[2,128,2048]{2,1,0:T(8,128)(2,1)} %bitcast.16), channel_id=1, source_target_pairs={{0,128},{128,0},{1,129},{129,1},{2,130},{130,2},{3,131},{131,3},{4... | collective-permute-start | bytes 3145736 | tf_op jit(solution)/shard_map/ppermute | solution.py:364
  51.8 33.3 %collective-permute-start.2 = (bf16[2,4,128,128]{3,2,1,0:T(8,128)(2,1)}, bf16[2,4,128,128]{3,2,1,0:T(8,128)(2,1)S(1)}, u32[]{:S(2)}, u32[]{:S(2)}) collective-permute-start(bf16[2,4,128,128]{3,2,1,0:T(8,128)(2,1)} %get-tuple-element.19), channel_id=1, source_target_pairs={{0,2},{1,3},{2,4},{3,5},{4,6},{5,7},{6,0},{7,1},{8,10},{9,11},{10,... | collective-permute-start | bytes 786440 | tf_op jit(solution)/shard_map/ppermute | solution.py:373
  52.0 33.1 %collective-permute-start.3 = (bf16[2,4,128,128]{3,2,1,0:T(8,128)(2,1)}, bf16[2,4,128,128]{3,2,1,0:T(8,128)(2,1)S(1)}, u32[]{:S(2)}, u32[]{:S(2)}) collective-permute-start(bf16[2,4,128,128]{3,2,1,0:T(8,128)(2,1)} %get-tuple-element.20), channel_id=1, source_target_pairs={{0,4},{1,5},{2,6},{3,7},{4,0},{5,1},{6,2},{7,3},{8,12},{9,13},{10,... | collective-permute-start | bytes 786440 | tf_op jit(solution)/shard_map/ppermute | solution.py:373
  54.1 31.0 %collective-permute-start.4 = (bf16[2,4,128,128]{3,2,1,0:T(8,128)(2,1)}, bf16[2,4,128,128]{3,2,1,0:T(8,128)(2,1)S(1)}, u32[]{:S(2)}, u32[]{:S(2)}) collective-permute-start(bf16[2,4,128,128]{3,2,1,0:T(8,128)(2,1)} %get-tuple-element.21), channel_id=1, source_target_pairs={{0,6},{1,7},{2,0},{3,1},{4,2},{5,3},{6,4},{7,5},{8,14},{9,15},{10,... | collective-permute-start | bytes 786440 | tf_op jit(solution)/shard_map/ppermute | solution.py:373
  77.2 38.6 %copy-start = (bf16[16,2,128,128]{3,2,1,0:T(8,128)(2,1)}, bf16[16,2,128,128]{3,2,1,0:T(8,128)(2,1)S(1)}, u32[]{:S(2)}) copy-start(bf16[16,2,128,128]{3,2,1,0:T(8,128)(2,1)S(1)} %all-to-all-done.1.source_ref.key_ref) | copy-start | bytes 3145732
  77.2 45.6 %all-to-all-start.4 = ((bf16[16,128,128]{2,1,0:T(8,128)(2,1)}), bf16[16,128,128]{2,1,0:T(8,128)(2,1)S(1)}, u32[]{:S(2)}, u32[]{:S(2)}) async-start(bf16[16,128,128]{2,1,0:T(8,128)(2,1)} %get-tuple-element.30), calls=%async_computation.4 | async-start | bytes 1048576 | tf_op jit(solution)/shard_map/all_to_all | solution.py:368
  85.1 0.7 copy-start.19
  85.1 0.8 copy-start.20
  85.9 0.7 copy-start.21
  88.8 9.5 %collective-permute-start.5 = (bf16[2,4,128,128]{3,2,1,0:T(8,128)(2,1)}, bf16[2,4,128,128]{3,2,1,0:T(8,128)(2,1)S(1)}, u32[]{:S(2)}, u32[]{:S(2)}) collective-permute-start(bf16[2,4,128,128]{3,2,1,0:T(8,128)(2,1)} %shard_map.65.mine_ref), channel_id=1, source_target_pairs={{0,1},{1,0},{2,3},{3,2},{4,5},{5,4},{6,7},{7,6},{8,9},{9,8},{10,11... | collective-permute-start | bytes 786440 | tf_op jit(solution)/shard_map/ppermute | solution.py:378
  98.3 0.7 copy-start.18
  100.8 9.6 %collective-permute-start.8 = (bf16[2,4,128,128]{3,2,1,0:T(8,128)(2,1)}, bf16[2,4,128,128]{3,2,1,0:T(8,128)(2,1)S(1)}, u32[]{:S(2)}, u32[]{:S(2)}) collective-permute-start(bf16[2,4,128,128]{3,2,1,0:T(8,128)(2,1)} %shard_map.66.refs_4_), channel_id=1, source_target_pairs={{0,6},{1,7},{2,0},{3,1},{4,2},{5,3},{6,4},{7,5},{8,14},{9,15},{10,... | collective-permute-start | bytes 786440 | tf_op jit(solution)/shard_map/ppermute | solution.py:373
  101.3 12.1 %collective-permute-start.7 = (bf16[2,4,128,128]{3,2,1,0:T(8,128)(2,1)}, bf16[2,4,128,128]{3,2,1,0:T(8,128)(2,1)S(1)}, u32[]{:S(2)}, u32[]{:S(2)}) collective-permute-start(bf16[2,4,128,128]{3,2,1,0:T(8,128)(2,1)} %shard_map.66.refs_4_), channel_id=1, source_target_pairs={{0,4},{1,5},{2,6},{3,7},{4,0},{5,1},{6,2},{7,3},{8,12},{9,13},{10,... | collective-permute-start | bytes 786440 | tf_op jit(solution)/shard_map/ppermute | solution.py:373
  102.2 13.6 %collective-permute-start.6 = (bf16[2,4,128,128]{3,2,1,0:T(8,128)(2,1)}, bf16[2,4,128,128]{3,2,1,0:T(8,128)(2,1)S(1)}, u32[]{:S(2)}, u32[]{:S(2)}) collective-permute-start(bf16[2,4,128,128]{3,2,1,0:T(8,128)(2,1)} %shard_map.66.refs_4_), channel_id=1, source_target_pairs={{0,2},{1,3},{2,4},{3,5},{4,6},{5,7},{6,0},{7,1},{8,10},{9,11},{10,... | collective-permute-start | bytes 786440 | tf_op jit(solution)/shard_map/ppermute | solution.py:373
  110.4 0.7 copy-start.8
  113.5 0.7 copy-start.11
  115.7 0.7 copy-start.14
  118.7 34.3 %copy-start.22 = (s32[16,2]{0,1:T(2,128)S(1)}, s32[16,2]{0,1:T(2,128)}, u32[]{:S(2)}) copy-start(s32[16,2]{0,1:T(2,128)} %param.11) | copy-start | bytes 388
  118.7 46.3 %copy-start.1 = (bf16[16,2,128,128]{3,2,1,0:T(8,128)(2,1)S(1)}, bf16[16,2,128,128]{3,2,1,0:T(8,128)(2,1)}, u32[]{:S(2)}) copy-start(bf16[16,2,128,128]{3,2,1,0:T(8,128)(2,1)} %copy-done) | copy-start | bytes 3145732
  118.7 46.3 %copy-start.3 = (bf16[16,2,128,128]{3,2,1,0:T(8,128)(2,1)S(1)}, bf16[16,2,128,128]{3,2,1,0:T(8,128)(2,1)}, u32[]{:S(2)}) copy-start(bf16[16,2,128,128]{3,2,1,0:T(8,128)(2,1)} %copy-done.2) | copy-start | bytes 3145732
  118.7 46.3 %copy-start.5 = (bf16[2,4,128,128]{3,2,1,0:T(8,128)(2,1)S(1)}, bf16[2,4,128,128]{3,2,1,0:T(8,128)(2,1)}, u32[]{:S(2)}) copy-start(bf16[2,4,128,128]{3,2,1,0:T(8,128)(2,1)} %shard_map.66.refs_4_) | copy-start | bytes 786436
  118.7 14.4 %collective-permute-start.9 = (bf16[2,4,128,128]{3,2,1,0:T(8,128)(2,1)}, bf16[2,4,128,128]{3,2,1,0:T(8,128)(2,1)}, u32[]{:S(2)}, u32[]{:S(2)}) collective-permute-start(bf16[2,4,128,128]{3,2,1,0:T(8,128)(2,1)} %get-tuple-element.23), channel_id=1, source_target_pairs={{0,2},{1,3},{2,4},{3,5},{4,6},{5,7},{6,0},{7,1},{8,10},{9,11},{10,... | collective-permute-start | bytes 786440 | tf_op jit(solution)/shard_map/ppermute | solution.py:373
  122.1 11.1 %collective-permute-start.10 = (bf16[2,4,128,128]{3,2,1,0:T(8,128)(2,1)}, bf16[2,4,128,128]{3,2,1,0:T(8,128)(2,1)}, u32[]{:S(2)}, u32[]{:S(2)}) collective-permute-start(bf16[2,4,128,128]{3,2,1,0:T(8,128)(2,1)} %get-tuple-element.24), channel_id=1, source_target_pairs={{0,4},{1,5},{2,6},{3,7},{4,0},{5,1},{6,2},{7,3},{8,12},{9,13},{10,... | collective-permute-start | bytes 786440 | tf_op jit(solution)/shard_map/ppermute | solution.py:373
  122.1 15.1 %collective-permute-start.11 = (bf16[2,4,128,128]{3,2,1,0:T(8,128)(2,1)}, bf16[2,4,128,128]{3,2,1,0:T(8,128)(2,1)}, u32[]{:S(2)}, u32[]{:S(2)}) collective-permute-start(bf16[2,4,128,128]{3,2,1,0:T(8,128)(2,1)} %get-tuple-element.25), channel_id=1, source_target_pairs={{0,6},{1,7},{2,0},{3,1},{4,2},{5,3},{6,4},{7,5},{8,14},{9,15},{10,... | collective-permute-start | bytes 786440 | tf_op jit(solution)/shard_map/ppermute | solution.py:373
  122.7 97.8 %all-to-all-start = ((bf16[16,128,128]{2,1,0:T(8,128)(2,1)}), bf16[16,128,128]{2,1,0:T(8,128)(2,1)S(1)}, u32[]{:S(2)}, u32[]{:S(2)}) async-start(bf16[16,128,128]{2,1,0:T(8,128)(2,1)} %get-tuple-element.18), calls=%async_computation | async-start | bytes 1048576 | tf_op jit(solution)/shard_map/all_to_all | solution.py:368
  139.4 8.9 %collective-permute-start.12 = (bf16[2,4,128,128]{3,2,1,0:T(8,128)(2,1)}, bf16[2,4,128,128]{3,2,1,0:T(8,128)(2,1)}, u32[]{:S(2)}, u32[]{:S(2)}) collective-permute-start(bf16[2,4,128,128]{3,2,1,0:T(8,128)(2,1)} %shard_map.68.mine_ref), channel_id=1, source_target_pairs={{0,1},{1,0},{2,3},{3,2},{4,5},{5,4},{6,7},{7,6},{8,9},{9,8},{10,11... | collective-permute-start | bytes 786440 | tf_op jit(solution)/shard_map/ppermute | solution.py:378
  150.0 10.2 %collective-permute-start.15 = (bf16[2,4,128,128]{3,2,1,0:T(8,128)(2,1)}, bf16[2,4,128,128]{3,2,1,0:T(8,128)(2,1)}, u32[]{:S(2)}, u32[]{:S(2)}) collective-permute-start(bf16[2,4,128,128]{3,2,1,0:T(8,128)(2,1)} %shard_map.69.refs_0_), channel_id=1, source_target_pairs={{0,6},{1,7},{2,0},{3,1},{4,2},{5,3},{6,4},{7,5},{8,14},{9,15},{10,... | collective-permute-start | bytes 786440 | tf_op jit(solution)/shard_map/ppermute | solution.py:373
  150.1 11.5 %collective-permute-start.14 = (bf16[2,4,128,128]{3,2,1,0:T(8,128)(2,1)}, bf16[2,4,128,128]{3,2,1,0:T(8,128)(2,1)}, u32[]{:S(2)}, u32[]{:S(2)}) collective-permute-start(bf16[2,4,128,128]{3,2,1,0:T(8,128)(2,1)} %shard_map.69.refs_0_), channel_id=1, source_target_pairs={{0,4},{1,5},{2,6},{3,7},{4,0},{5,1},{6,2},{7,3},{8,12},{9,13},{10,... | collective-permute-start | bytes 786440 | tf_op jit(solution)/shard_map/ppermute | solution.py:373
  150.9 14.0 %collective-permute-start.13 = (bf16[2,4,128,128]{3,2,1,0:T(8,128)(2,1)}, bf16[2,4,128,128]{3,2,1,0:T(8,128)(2,1)}, u32[]{:S(2)}, u32[]{:S(2)}) collective-permute-start(bf16[2,4,128,128]{3,2,1,0:T(8,128)(2,1)} %shard_map.69.refs_0_), channel_id=1, source_target_pairs={{0,2},{1,3},{2,4},{3,5},{4,6},{5,7},{6,0},{7,1},{8,10},{9,11},{10,... | collective-permute-start | bytes 786440 | tf_op jit(solution)/shard_map/ppermute | solution.py:373
  164.9 1.0 copy-start.6
  165.9 0.9 copy-start.9
  166.8 0.9 copy-start.12
  167.8 0.9 copy-start.15
  219.7 0.8 copy-start.4
  220.5 45.6 %all-to-all-start.5 = ((bf16[16,128,128]{2,1,0:T(8,128)(2,1)}), bf16[16,128,128]{2,1,0:T(8,128)(2,1)S(1)}, u32[]{:S(2)}, u32[]{:S(2)}) async-start(bf16[16,128,128]{2,1,0:T(8,128)(2,1)} %copy-done.4), calls=%async_computation.5 | async-start | bytes 1048576 | tf_op jit(solution)/shard_map/all_to_all | solution.py:368
  228.7 3.8 %copy-start.7 = (bf16[2,4,128,128]{3,2,1,0:T(8,128)(2,1)S(1)}, bf16[2,4,128,128]{3,2,1,0:T(8,128)(2,1)}, u32[]{:S(2)}) copy-start(bf16[2,4,128,128]{3,2,1,0:T(8,128)(2,1)} %shard_map.69.refs_0_) | copy-start | bytes 786436
  228.7 3.8 %copy-start.10 = (bf16[2,4,128,128]{3,2,1,0:T(8,128)(2,1)S(1)}, bf16[2,4,128,128]{3,2,1,0:T(8,128)(2,1)}, u32[]{:S(2)}) copy-start(bf16[2,4,128,128]{3,2,1,0:T(8,128)(2,1)} %copy-done.8) | copy-start | bytes 786436
  228.7 3.8 %copy-start.13 = (bf16[2,4,128,128]{3,2,1,0:T(8,128)(2,1)S(1)}, bf16[2,4,128,128]{3,2,1,0:T(8,128)(2,1)}, u32[]{:S(2)}) copy-start(bf16[2,4,128,128]{3,2,1,0:T(8,128)(2,1)} %copy-done.11) | copy-start | bytes 786436
  228.7 3.8 %copy-start.16 = (bf16[2,4,128,128]{3,2,1,0:T(8,128)(2,1)S(1)}, bf16[2,4,128,128]{3,2,1,0:T(8,128)(2,1)}, u32[]{:S(2)}) copy-start(bf16[2,4,128,128]{3,2,1,0:T(8,128)(2,1)} %copy-done.14) | copy-start | bytes 786436
  266.1 24.4 %all-to-all-start.3 = ((bf16[16,128,128]{2,1,0:T(8,128)(2,1)}), bf16[16,128,128]{2,1,0:T(8,128)(2,1)S(1)}, u32[]{:S(2)}, u32[]{:S(2)}) async-start(bf16[16,128,128]{2,1,0:T(8,128)(2,1)} %attend_extra.2), calls=%async_computation.3 | async-start | bytes 1048576 | tf_op jit(solution)/shard_map/all_to_all | solution.py:368

commit v2 on v1

v2 whole, which is shorter than its diff:
```python
import functools
import math

import jax
import jax.numpy as jnp
from jax import lax
from jax.experimental import pallas as pl
from jax.experimental.pallas import tpu as pltpu
from jax.sharding import PartitionSpec as P


HEAD = 128
SCALE = math.log2(math.e) / math.sqrt(HEAD)
SAFE = 100.0
LOWEST = -1e30
BF16 = jnp.bfloat16
F32 = jnp.float32


def blend_kernel(strength_ref, own_ref, partner_ref, *out_refs, heads):
    first = pl.program_id(0) * heads
    for head in range(heads):
        share = strength_ref[0, first + head]
        lanes = slice(head * HEAD, (head + 1) * HEAD)
        mixed = (
            (1.0 - share) * own_ref[:, :, lanes].astype(F32)
            + share * partner_ref[:, :, lanes].astype(F32)
        ).astype(BF16)
        if len(out_refs) == 1:
            out_refs[0][head] = mixed
        else:
            for frame, out_ref in enumerate(out_refs):
                out_ref[head] = mixed[frame]


def blend_heads(strength, own, partner, per_frame, steps=2):
    frames, rows, width = own.shape
    heads = width // HEAD
    group = heads // steps
    block = pl.BlockSpec((frames, rows, group * HEAD), lambda h: (0, 0, h))
    if per_frame:
        out_specs = [pl.BlockSpec((group, rows, HEAD), lambda h: (h, 0, 0))] * frames
        out_shape = [jax.ShapeDtypeStruct((heads, rows, HEAD), BF16)] * frames
    else:
        out_specs = [pl.BlockSpec((group, frames, rows, HEAD), lambda h: (h, 0, 0, 0))]
        out_shape = [jax.ShapeDtypeStruct((heads, frames, rows, HEAD), BF16)]
    return pl.pallas_call(
        functools.partial(blend_kernel, heads=group),
        grid=(steps,),
        in_specs=[pl.BlockSpec(memory_space=pltpu.SMEM), block, block],
        out_specs=out_specs,
        out_shape=out_shape,
        cost_estimate=pl.CostEstimate(
            flops=3 * own.size, bytes_accessed=6 * own.size, transcendentals=0
        ),
        name="blend",
    )(strength, own, partner)


def split_kernel(source_ref, out_ref, sem):
    heads = out_ref.shape[0]
    copies = [
        pltpu.make_async_copy(
            source_ref.at[:, :, pl.ds(head * HEAD, HEAD)], out_ref.at[head], sem.at[head]
        )
        for head in range(heads)
    ]
    for copy in copies:
        copy.start()
    for copy in copies:
        copy.wait()


def split_heads(rows):
    frames, count, width = rows.shape
    heads = width // HEAD
    out = jax.ShapeDtypeStruct((heads, frames, count, HEAD), BF16)
    return pl.pallas_call(
        split_kernel,
        grid=(1,),
        in_specs=[pl.BlockSpec(memory_space=pl.ANY)],
        out_specs=whole(out),
        out_shape=out,
        scratch_shapes=[pltpu.SemaphoreType.DMA((heads,))],
        cost_estimate=pl.CostEstimate(flops=0, bytes_accessed=4 * rows.size, transcendentals=0),
        name="split_heads",
    )(rows)


def dot_nt(a, b):
    return lax.dot_general(a, b, (((1,), (1,)), ((), ())), preferred_element_type=F32)


def scaled_split(query):
    scaled = query.astype(F32) * SCALE
    high = scaled.astype(BF16)
    low = (scaled - high.astype(F32)).astype(BF16)
    return jnp.concatenate([high, low], axis=1)


def score_tile(query_pair, key):
    return dot_nt(query_pair, jnp.concatenate([key, key], axis=1))


def with_ones(value):
    return jnp.concatenate([value, jnp.ones_like(value)], axis=1)


def weighted(weights, value):
    return jnp.dot(weights.astype(BF16), with_ones(value), preferred_element_type=F32)


def norm_max(rows):
    rows = rows.reshape(-1, HEAD)
    sums = jnp.dot(rows * rows, jnp.ones((HEAD, HEAD), BF16), preferred_element_type=F32)
    return jnp.max(sums)


def copy_all(sources, target, sem):
    copies = []
    start = 0
    for source in sources:
        blocks = source.shape[0]
        copies.append(
            pltpu.make_async_copy(source, target.at[pl.ds(start, blocks)], sem.at[len(copies)])
        )
        start += blocks
    for copy in copies:
        copy.start()
    return copies


def attend_kernel(valid_ref, query_ref, key_ref, value_ref, *refs, frame, tile, pieces, mode):
    key_extra, value_extra = refs[:pieces], refs[pieces : 2 * pieces]
    acc_in = refs[2 * pieces : 2 * pieces + 1] if mode == "more" else ()
    out_ref, keys, values, acc, top, key_sem, value_sem = refs[2 * pieces + len(acc_in) :]
    parts = keys.shape[0]
    blocks, rows = query_ref.shape[0], query_ref.shape[1]
    step = tile // rows

    key_copies, value_copies = [], []
    for part in range(parts):
        if part == 0:
            key_sources, value_sources = [key_ref.at[:, frame]], [value_ref.at[:, frame]]
        else:
            key_sources = [ref.at[part - 1] for ref in key_extra]
            value_sources = [ref.at[part - 1] for ref in value_extra]
        key_copies += copy_all(key_sources, keys.at[part], key_sem.at[part])
        value_copies += copy_all(value_sources, values.at[part], value_sem.at[part])

    query = query_ref[...].reshape(-1, HEAD)
    query_norm = norm_max(query)
    for copy in key_copies:
        copy.wait()
    key_norm = norm_max(keys[0])
    for part in range(1, parts):
        key_norm = jnp.maximum(key_norm, norm_max(keys[part]))
    safe = query_norm * key_norm * (SCALE * SCALE) <= SAFE * SAFE
    for copy in value_copies:
        copy.wait()

    def tiles(part, first=0, count=blocks):
        for start in range(0, count, step):
            span = pl.ds(first + start, step)
            yield keys[part, span].reshape(tile, HEAD), values[part, span].reshape(tile, HEAD)

    def finish(sums):
        return (sums[:, :HEAD] / sums[:, HEAD:]).astype(BF16)

    @pl.when(safe)
    def _():
        pair = scaled_split(query)
        sums = out_ref if mode == "own" else acc
        sums[...] = acc_in[0][...] if mode == "more" else jnp.zeros_like(sums)

        def half_part(index, carry):
            part = index // 2

            @pl.when(valid_ref[part] > 0)
            def _():
                half = blocks // 2
                for key, value in tiles(part, lax.rem(index, 2) * half, half):
                    sums[...] += weighted(jnp.exp2(score_tile(pair, key)), value)

            return carry

        lax.fori_loop(2 if mode == "more" else 0, 2 * parts, half_part, 0)
        if mode != "own":
            out_ref[...] = finish(sums[...]).reshape(out_ref.shape)

    if mode == "own":
        return

    @pl.when(jnp.logical_not(safe))
    def _():
        def one_block(block, carry):
            pair = scaled_split(query_ref[block])
            sums = acc.at[pl.ds(0, rows)]
            sums[...] = jnp.zeros_like(sums)
            top[...] = jnp.full_like(top, LOWEST)

            def one_part(part, carry):
                @pl.when(valid_ref[part] > 0)
                def _():
                    for key, value in tiles(part):
                        scores = score_tile(pair, key)
                        old_top = top[:, :1]
                        new_top = jnp.maximum(old_top, jnp.max(scores, axis=1, keepdims=True))
                        part_sums = weighted(jnp.exp2(scores - new_top), value)
                        sums[...] = sums[...] * jnp.exp2(old_top - new_top) + part_sums
                        top[...] = jnp.broadcast_to(new_top, top.shape)

                return carry

            lax.fori_loop(0, parts, one_part, 0)
            out_ref[block] = finish(sums[...])
            return carry

        lax.fori_loop(0, blocks, one_block, 0)


def whole(array):
    return pl.BlockSpec(
        array.shape, lambda i: (0,) * len(array.shape), pipeline_mode=pl.Buffered(1)
    )


ANY = pl.BlockSpec(memory_space=pl.ANY)
SMEM = pl.BlockSpec(memory_space=pltpu.SMEM)


def attend(mode, frame, valid, query, key, value, key_extra=(), value_extra=(), acc=None, tile=512):
    blocks, rows, _ = query.shape
    total = blocks * rows
    parts = valid.shape[0] if mode != "own" else 1
    pieces = len(key_extra)
    if mode == "own":
        out = jax.ShapeDtypeStruct((total, 2 * HEAD), F32)
    else:
        out = jax.ShapeDtypeStruct((blocks, rows, HEAD), BF16)
    accs = [acc] if mode == "more" else []
    return pl.pallas_call(
        functools.partial(attend_kernel, frame=frame, tile=tile, pieces=pieces, mode=mode),
        grid=(1,),
        in_specs=[SMEM, whole(query), ANY, ANY, *[ANY] * (2 * pieces), *[whole(a) for a in accs]],
        out_specs=whole(out),
        out_shape=out,
        scratch_shapes=[
            pltpu.VMEM((parts, blocks, rows, HEAD), BF16),
            pltpu.VMEM((parts, blocks, rows, HEAD), BF16),
            pltpu.VMEM((total, 2 * HEAD), F32),
            pltpu.VMEM((rows, HEAD), F32),
            pltpu.SemaphoreType.DMA((parts, max(1, pieces))),
            pltpu.SemaphoreType.DMA((parts, max(1, pieces))),
        ],
        compiler_params=pltpu.CompilerParams(vmem_limit_bytes=24 << 20),
        cost_estimate=pl.CostEstimate(
            flops=4 * total * total * HEAD * (parts - (mode == "more")),
            bytes_accessed=4 * total * HEAD * (1 + parts),
            transcendentals=total * total,
        ),
    )(valid, query, key, value, *key_extra, *value_extra, *accs)


def cut_kernel(place_ref, keyframes_ref, source_ref, *refs, xs):
    *out_refs, sem = refs
    blocks, frames = source_ref.shape[:2]
    quarter = blocks // xs
    x = place_ref[0] // 2
    copies = []
    for step, out_ref in enumerate(out_refs, 1):
        start = lax.rem(x + step, xs) * quarter
        for j in range(out_ref.shape[0]):
            slot = lax.rem(keyframes_ref[j], frames)
            copies.append(
                pltpu.make_async_copy(
                    source_ref.at[pl.ds(start, quarter), slot], out_ref.at[j], sem.at[len(copies)]
                )
            )
    for copy in copies:
        copy.start()
    for copy in copies:
        copy.wait()


def pick_x_kernel(place_ref, keyframes_ref, source_ref, *refs):
    *got_refs, out_ref, sem = refs
    xs = len(got_refs) + 1
    blocks, frames = source_ref.shape[:2]
    quarter = blocks // xs
    x = place_ref[0] // 2
    extras = out_ref.shape[0]
    for j in range(extras):
        keyframe = keyframes_ref[j]
        step = lax.rem(x - keyframe // (2 * frames) + xs, xs)

        @pl.when(step == 0)
        def _():
            slot = lax.rem(keyframe, frames)
            pltpu.make_async_copy(
                source_ref.at[pl.ds(x * quarter, quarter), slot], out_ref.at[j], sem.at[j]
            ).start()

        for which, got_ref in enumerate(got_refs, 1):

            @pl.when(step == which)
            def _():
                pltpu.make_async_copy(got_ref.at[j], out_ref.at[j], sem.at[j]).start()

    for j in range(extras):
        pltpu.make_async_copy(got_refs[0].at[j], out_ref.at[j], sem.at[j]).wait()


def pick_y_kernel(place_ref, keyframes_ref, mine_ref, other_ref, out_ref, sem, *, frames):
    y = lax.rem(place_ref[0], 2)
    extras = out_ref.shape[0]
    for j in range(extras):
        same = lax.rem(keyframes_ref[j] // frames, 2) == y

        @pl.when(same)
        def _():
            pltpu.make_async_copy(mine_ref.at[j], out_ref.at[j], sem.at[j]).start()

        @pl.when(jnp.logical_not(same))
        def _():
            pltpu.make_async_copy(other_ref.at[j], out_ref.at[j], sem.at[j]).start()

    for j in range(extras):
        pltpu.make_async_copy(mine_ref.at[j], out_ref.at[j], sem.at[j]).wait()


def move_call(kernel, out_shapes, place, keyframes, *arrays):
    moved = sum(math.prod(o.shape) for o in out_shapes)
    return pl.pallas_call(
        kernel,
        grid=(1,),
        in_specs=[SMEM, SMEM] + [ANY] * len(arrays),
        out_specs=[whole(o) for o in out_shapes],
        out_shape=out_shapes,
        scratch_shapes=[pltpu.SemaphoreType.DMA((len(out_shapes) * keyframes.shape[0],))],
        compiler_params=pltpu.CompilerParams(vmem_limit_bytes=8 << 20),
        cost_estimate=pl.CostEstimate(flops=0, bytes_accessed=4 * moved, transcendentals=0),
    )(place, keyframes, *arrays)


def piece_shape(keyframes, by_frame, xs):
    blocks, _, rows, width = by_frame.shape
    return jax.ShapeDtypeStruct((keyframes.shape[0], blocks // xs, rows, width), BF16)


def cut_pieces(place, keyframes, by_frame, xs):
    return move_call(
        functools.partial(cut_kernel, xs=xs),
        [piece_shape(keyframes, by_frame, xs)] * (xs - 1), place, keyframes, by_frame,
    )


def pick_along_x(place, keyframes, by_frame, got):
    return move_call(
        pick_x_kernel,
        [piece_shape(keyframes, by_frame, len(got) + 1)], place, keyframes, by_frame, *got,
    )[0]


def pick_along_y(place, keyframes, mine, other, frames):
    return move_call(
        functools.partial(pick_y_kernel, frames=frames),
        [jax.ShapeDtypeStruct(mine.shape, BF16)], place, keyframes, mine, other,
    )[0]


def swap_branch(value):
    return lax.ppermute(value, "branch", [(0, 1), (1, 0)])


def to_heads(value):
    return lax.all_to_all(value, "seq", split_axis=0, concat_axis=0, tiled=True)


def shift_x(value, step):
    size = lax.axis_size("mp")
    return lax.ppermute(value, "mp", [(m, (m + 2 * step) % size) for m in range(size)])


def flip_y(value):
    size = lax.axis_size("mp")
    return lax.ppermute(value, "mp", [(m, m ^ 1) for m in range(size)])


def spread_keyframes(by_frame, keyframes):
    place = lax.axis_index("mp").astype(jnp.int32).reshape(1)
    xs = lax.axis_size("mp") // 2
    pieces = cut_pieces(place, keyframes, by_frame, xs)
    got = [shift_x(piece, step) for step, piece in enumerate(pieces, 1)]
    mine = pick_along_x(place, keyframes, by_frame, got)
    other = flip_y(mine)
    mine = pick_along_y(place, keyframes, mine, other, by_frame.shape[1])
    return [mine] + [shift_x(mine, step) for step in range(1, xs)]


def local(queries, keys, values, inject, keyframes, key_mask):
    queries, keys, values = queries[0], keys[0], values[0]
    frames = queries.shape[0]
    partner_keys = swap_branch(keys)
    partner_queries = swap_branch(queries)

    value_rows = split_heads(values)
    value_heads = to_heads(value_rows)
    value_extra = spread_keyframes(value_heads, keyframes)

    (key_rows,) = blend_heads(inject, keys, partner_keys, False)
    key_heads = to_heads(key_rows)
    key_extra = spread_keyframes(key_heads, keyframes)

    query_rows = blend_heads(inject, queries, partner_queries, True)
    query_frames = []
    for f in range(frames):
        query_frames.append(to_heads(query_rows[f]))

    first = lax.axis_index("mp") * frames
    outs = []
    for f in range(frames):
        masks = lax.dynamic_index_in_dim(key_mask, first + f, 0, keepdims=False)
        valid = jnp.concatenate([jnp.ones((1,), jnp.int32), masks])
        extra = (key_extra, value_extra)
        if f == 0:
            acc = attend("own", f, valid, query_frames[f], key_heads, value_heads)
            out = attend("more", f, valid, query_frames[f], key_heads, value_heads, *extra, acc)
        else:
            out = attend("all", f, valid, query_frames[f], key_heads, value_heads, *extra)
        back = to_heads(out)
        heads, rows, _ = back.shape
        outs.append(back.transpose(1, 0, 2).reshape(rows, heads * HEAD))
    return jnp.stack(outs)[None]


def solution(mesh):
    return jax.shard_map(
        local,
        mesh=mesh,
        in_specs=(
            P("branch", "mp", "seq", None),
            P("branch", "mp", "seq", None),
            P("branch", "mp", "seq", None),
            P("branch", None),
            P(),
            P(),
        ),
        out_specs=P("branch", "mp", "seq", None),
        check_vma=False,
    )
```

time: 293 us -> 329 us (1.12)
  the two profiles are of different devices: /device:TPU:23 before, /device:TPU:31 now
where the time goes in v2:
time: 329 us; the launch traced here: 328 us
  Pallas kernels  159 us (48%)
  waiting for transfers between devices  101 us (31%)
  starting transfers between devices  63 us (19%)
  local copies, waits for them, and re-layouts  3.92 us (1%)
    pallas_call x3, Pallas kernels, attend(): pl.pallas_call(functools.partial(attend_kernel, frame=frame, tile=tile, p...  145 us
    ppermute x2, waiting for transfers between devices, swap_branch(): return lax.ppermute(value, 'branch', [(0, 1), (1, 0)])  48.7 us
    all_to_all x6, starting transfers between devices, to_heads(): return lax.all_to_all(value, 'seq', split_axis=0, concat_axis=0, tiled=True)  47.4 us
    ppermute x12, waiting for transfers between devices, shift_x(): lax.ppermute(value, 'mp', [(m, (m + 2 * step) % size) for m in range(size)])  35.8 us
    all_to_all x6, waiting for transfers between devices, to_heads(): return lax.all_to_all(value, 'seq', split_axis=0, concat_axis=0, tiled=True)  17 us
    ppermute x12, starting transfers between devices, shift_x(): lax.ppermute(value, 'mp', [(m, (m + 2 * step) % size) for m in range(size)])  12.4 us
    pallas_call x6, Pallas kernels, move_call(): pl.pallas_call(kernel, grid=(1,), in_specs=[SMEM, SMEM] + [ANY] * len(arr...  6.73 us
  transfers between devices with their start and end apart: 22, of which 16 were waited for; matrix products, arithmetic and copies ran while one was open for 1% of the time, Pallas kernels for 48%

profile of v2, /device:TPU:31, one launch (start us, length us, event | category | flops | bytes accessed | tf_op | source)
XLA Modules:
  0.0 328.0 jit_solution(11834819580771231280)
XLA Ops:
  0.0 2.5 split_heads.1
  2.5 9.2 %all-to-all-start.2 = ((bf16[16,2,128,128]{3,2,1,0:T(8,128)(2,1)}), bf16[16,2,128,128]{3,2,1,0:T(8,128)(2,1)S(1)}, u32[]{:S(2)}, u32[]{:S(2)}) async-start(bf16[16,2,128,128]{3,2,1,0:T(8,128)(2,1)} %split_heads.1), calls=%async_computation.2 | async-start | bytes 2097152 | tf_op jit(solution)/shard_map/all_to_all | solution.py:377
  11.7 0.6 collective-permute-start.1
  12.2 24.3 %collective-permute-done.1.partner_ref = bf16[2,128,2048]{2,1,0:T(8,128)(2,1)} collective-permute-done((bf16[2,128,2048]{2,1,0:T(8,128)(2,1)S(1)}, bf16[2,128,2048]{2,1,0:T(8,128)(2,1)}, u32[]{:S(2)}, u32[]{:S(2)}) %collective-permute-start.1) | collective-permute-done | bytes 1048608 | tf_op jit(solution)/shard_map/ppermute | solution.py:373
  36.5 2.5 blend.3
  39.0 0.6 all-to-all-done.2.source_ref.value_ref
  39.6 7.1 %all-to-all-start.1 = ((bf16[16,2,128,128]{3,2,1,0:T(8,128)(2,1)}), bf16[16,2,128,128]{3,2,1,0:T(8,128)(2,1)S(1)}, u32[]{:S(2)}, u32[]{:S(2)}) async-start(bf16[16,2,128,128]{3,2,1,0:T(8,128)(2,1)} %blend.3), calls=%async_computation.1 | async-start | bytes 2097152 | tf_op jit(solution)/shard_map/all_to_all | solution.py:377
  46.8 0.6 collective-permute-start
  47.3 24.5 %collective-permute-done.partner_ref = bf16[2,128,2048]{2,1,0:T(8,128)(2,1)} collective-permute-done((bf16[2,128,2048]{2,1,0:T(8,128)(2,1)}, bf16[2,128,2048]{2,1,0:T(8,128)(2,1)}, u32[]{:S(2)}, u32[]{:S(2)}) %collective-permute-start) | collective-permute-done | bytes 1048608 | tf_op jit(solution)/shard_map/ppermute | solution.py:373
  71.8 2.5 blend.2
  74.4 0.4 all-to-all-done.1.source_ref.key_ref
  74.8 7.4 %all-to-all-start.4 = ((bf16[16,128,128]{2,1,0:T(8,128)(2,1)}), bf16[16,128,128]{2,1,0:T(8,128)(2,1)S(1)}, u32[]{:S(2)}, u32[]{:S(2)}) async-start(bf16[16,128,128]{2,1,0:T(8,128)(2,1)} %get-tuple-element.20), calls=%async_computation.4 | async-start | bytes 1048576 | tf_op jit(solution)/shard_map/all_to_all | solution.py:377
  82.2 0.9 shard_map.67
  83.3 2.1 collective-permute-start.10
  85.5 0.9 shard_map.64
  86.3 2.8 collective-permute-start.2
  89.2 1.6 collective-permute-done.9.refs_0_
  90.9 0.6 collective-permute-start.4
  91.4 0.9 collective-permute-done.10.refs_1_
  92.3 7.0 %collective-permute-done.11.refs_2_ = bf16[2,4,128,128]{3,2,1,0:T(8,128)(2,1)S(1)} collective-permute-done((bf16[2,4,128,128]{3,2,1,0:T(8,128)(2,1)S(1)}, bf16[2,4,128,128]{3,2,1,0:T(8,128)(2,1)S(1)}, u32[]{:S(2)}, u32[]{:S(2)}) %collective-permute-start.11) | collective-permute-done | bytes 262176 | tf_op jit(solution)/shard_map/ppermute | solution.py:382
  99.4 0.8 shard_map.68.mine_ref
  100.2 1.0 collective-permute-start.12
  101.3 0.9 collective-permute-done.2.refs_0_
  102.2 1.5 collective-permute-done.3.refs_1_
  103.6 6.3 %collective-permute-done.4.refs_2_ = bf16[2,4,128,128]{3,2,1,0:T(8,128)(2,1)S(1)} collective-permute-done((bf16[2,4,128,128]{3,2,1,0:T(8,128)(2,1)S(1)}, bf16[2,4,128,128]{3,2,1,0:T(8,128)(2,1)S(1)}, u32[]{:S(2)}, u32[]{:S(2)}) %collective-permute-start.4) | collective-permute-done | bytes 262176 | tf_op jit(solution)/shard_map/ppermute | solution.py:382
  109.9 0.8 shard_map.65.mine_ref
  110.8 1.0 collective-permute-start.5
  111.8 1.7 shard_map.69.refs_4_
  113.6 8.6 %all-to-all-start = ((bf16[16,128,128]{2,1,0:T(8,128)(2,1)}), bf16[16,128,128]{2,1,0:T(8,128)(2,1)S(1)}, u32[]{:S(2)}, u32[]{:S(2)}) async-start(bf16[16,128,128]{2,1,0:T(8,128)(2,1)} %get-tuple-element.13), calls=%async_computation | async-start | bytes 1048576 | tf_op jit(solution)/shard_map/all_to_all | solution.py:377
  122.3 1.1 collective-permute-start.14
  123.3 1.7 collective-permute-start.13
  125.1 1.6 shard_map.66.refs_0_
  126.8 1.6 collective-permute-start.7
  128.4 1.8 collective-permute-start.6
  130.6 1.2 collective-permute-done.14.refs_6_
  131.8 5.1 %collective-permute-done.13.refs_5_ = bf16[2,4,128,128]{3,2,1,0:T(8,128)(2,1)} collective-permute-done((bf16[2,4,128,128]{3,2,1,0:T(8,128)(2,1)}, bf16[2,4,128,128]{3,2,1,0:T(8,128)(2,1)}, u32[]{:S(2)}, u32[]{:S(2)}) %collective-permute-start.13) | collective-permute-done | bytes 262176 | tf_op jit(solution)/shard_map/ppermute | solution.py:382
  136.9 1.2 collective-permute-done.8.refs_3_
  138.1 4.9 %collective-permute-done.7.refs_2_ = bf16[2,4,128,128]{3,2,1,0:T(8,128)(2,1)} collective-permute-done((bf16[2,4,128,128]{3,2,1,0:T(8,128)(2,1)}, bf16[2,4,128,128]{3,2,1,0:T(8,128)(2,1)}, u32[]{:S(2)}, u32[]{:S(2)}) %collective-permute-start.7) | collective-permute-done | bytes 262176 | tf_op jit(solution)/shard_map/ppermute | solution.py:382
  143.0 5.1 %collective-permute-done.6.refs_1_ = bf16[2,4,128,128]{3,2,1,0:T(8,128)(2,1)} collective-permute-done((bf16[2,4,128,128]{3,2,1,0:T(8,128)(2,1)}, bf16[2,4,128,128]{3,2,1,0:T(8,128)(2,1)}, u32[]{:S(2)}, u32[]{:S(2)}) %collective-permute-start.6) | collective-permute-done | bytes 262176 | tf_op jit(solution)/shard_map/ppermute | solution.py:382
  148.2 84.4 %shard_map.72 = bf16[16,128,128]{2,1,0:T(8,128)(2,1)S(1)} custom-call(s32[3]{0:T(128)S(1)} %pad_add_fusion.valid_ref, bf16[16,128,128]{2,1,0:T(8,128)(2,1)S(1)} %all-to-all-done.4.query_ref, bf16[16,2,128,128]{3,2,1,0:T(8,128)(2,1)S(1)} %all-to-all-done.1.source_ref.key_ref, bf16[16,2,128,128]{3,2,1,0:T(8,128)(2,1)S(1)} %all-to-all-done.2.source_ref.value_ref, ...), custom_call_target="tpu_custom_call" | custom-call | flops 6442450944 | bytes 4194304 | tf_op jit(solution)/shard_map/pallas_call | solution.py:242
  232.6 0.8 copy-done
  233.4 7.9 %all-to-all-start.5 = ((bf16[16,128,128]{2,1,0:T(8,128)(2,1)}), bf16[16,128,128]{2,1,0:T(8,128)(2,1)}, u32[]{:S(2)}, u32[]{:S(2)}) async-start(bf16[16,128,128]{2,1,0:T(8,128)(2,1)} %copy-done), calls=%async_computation.5 | async-start | bytes 1048576 | tf_op jit(solution)/shard_map/all_to_all | solution.py:377
  241.4 1.7 shard_map.70.refs_8_
  243.0 58.8 %shard_map.71 = bf16[16,128,128]{2,1,0:T(8,128)(2,1)} custom-call(s32[3]{0:T(128)S(1)} %pad_add_fusion.1.valid_ref, bf16[16,128,128]{2,1,0:T(8,128)(2,1)S(1)} %all-to-all-done.query_ref, bf16[16,2,128,128]{3,2,1,0:T(8,128)(2,1)S(1)} %all-to-all-done.1.source_ref.key_ref, bf16[16,2,128,128]{3,2,1,0:T(8,128)(2,1)S(1)} %all-to-all-done.2.source_ref.value_ref, ...), custom_call_target="tpu_custom_call" | custom-call | flops 4294967296 | bytes 4194304 | tf_op jit(solution)/shard_map/pallas_call | solution.py:242
  301.8 7.2 %all-to-all-start.3 = ((bf16[16,128,128]{2,1,0:T(8,128)(2,1)}), bf16[16,128,128]{2,1,0:T(8,128)(2,1)S(1)}, u32[]{:S(2)}, u32[]{:S(2)}) async-start(bf16[16,128,128]{2,1,0:T(8,128)(2,1)} %shard_map.71), calls=%async_computation.3 | async-start | bytes 1048576 | tf_op jit(solution)/shard_map/all_to_all | solution.py:377
  309.1 1.3 copy.8
  310.4 15.9 %all-to-all-done.3 = bf16[16,128,128]{2,1,0:T(8,128)(2,1)S(1)} async-done(((bf16[16,128,128]{2,1,0:T(8,128)(2,1)}), bf16[16,128,128]{2,1,0:T(8,128)(2,1)S(1)}, u32[]{:S(2)}, u32[]{:S(2)}) %all-to-all-start.3) | async-done | bytes 524320 | tf_op jit(solution)/shard_map/all_to_all | solution.py:377
  326.7 1.3 copy.9
  (23 shorter events, 1.4 us)
Async XLA Ops:
  0.0 11.6 %copy-start.2 = (bf16[1,2,128,2048]{3,2,1,0:T(8,128)(2,1)S(1)}, bf16[1,2,128,2048]{3,2,1,0:T(8,128)(2,1)}, u32[]{:S(2)}) copy-start(bf16[1,2,128,2048]{3,2,1,0:T(8,128)(2,1)} %param.7) | copy-start | bytes 3145732
  2.5 37.2 %all-to-all-start.2 = ((bf16[16,2,128,128]{3,2,1,0:T(8,128)(2,1)}), bf16[16,2,128,128]{3,2,1,0:T(8,128)(2,1)S(1)}, u32[]{:S(2)}, u32[]{:S(2)}) async-start(bf16[16,2,128,128]{3,2,1,0:T(8,128)(2,1)} %split_heads.1), calls=%async_computation.2 | async-start | bytes 2097152 | tf_op jit(solution)/shard_map/all_to_all | solution.py:377
  11.7 24.8 %collective-permute-start.1 = (bf16[2,128,2048]{2,1,0:T(8,128)(2,1)S(1)}, bf16[2,128,2048]{2,1,0:T(8,128)(2,1)}, u32[]{:S(2)}, u32[]{:S(2)}) collective-permute-start(bf16[2,128,2048]{2,1,0:T(8,128)(2,1)S(1)} %bitcast.17), channel_id=1, source_target_pairs={{0,128},{128,0},{1,129},{129,1},{2,130},{130,2},{3,131},{131,3},{4... | collective-permute-start | bytes 3145736 | tf_op jit(solution)/shard_map/ppermute | solution.py:373
  39.6 35.1 %all-to-all-start.1 = ((bf16[16,2,128,128]{3,2,1,0:T(8,128)(2,1)}), bf16[16,2,128,128]{3,2,1,0:T(8,128)(2,1)S(1)}, u32[]{:S(2)}, u32[]{:S(2)}) async-start(bf16[16,2,128,128]{3,2,1,0:T(8,128)(2,1)} %blend.3), calls=%async_computation.1 | async-start | bytes 2097152 | tf_op jit(solution)/shard_map/all_to_all | solution.py:377
  46.8 35.4 %copy-start.1 = (s32[2]{0:T(128)S(1)}, s32[2]{0:T(128)}, u32[]{:S(2)}) copy-start(s32[2]{0:T(128)} %keyframes_ref.11) | copy-start | bytes 28
  46.8 25.0 %collective-permute-start = (bf16[2,128,2048]{2,1,0:T(8,128)(2,1)}, bf16[2,128,2048]{2,1,0:T(8,128)(2,1)}, u32[]{:S(2)}, u32[]{:S(2)}) collective-permute-start(bf16[2,128,2048]{2,1,0:T(8,128)(2,1)} %bitcast.13), channel_id=1, source_target_pairs={{0,128},{128,0},{1,129},{129,1},{2,130},{130,2},{3,131},{131,3},{4... | collective-permute-start | bytes 3145736 | tf_op jit(solution)/shard_map/ppermute | solution.py:373
  74.8 38.9 %all-to-all-start.4 = ((bf16[16,128,128]{2,1,0:T(8,128)(2,1)}), bf16[16,128,128]{2,1,0:T(8,128)(2,1)S(1)}, u32[]{:S(2)}, u32[]{:S(2)}) async-start(bf16[16,128,128]{2,1,0:T(8,128)(2,1)} %get-tuple-element.20), calls=%async_computation.4 | async-start | bytes 1048576 | tf_op jit(solution)/shard_map/all_to_all | solution.py:377
  83.0 7.8 %collective-permute-start.9 = (bf16[2,4,128,128]{3,2,1,0:T(8,128)(2,1)S(1)}, bf16[2,4,128,128]{3,2,1,0:T(8,128)(2,1)S(1)}, u32[]{:S(2)}, u32[]{:S(2)}) collective-permute-start(bf16[2,4,128,128]{3,2,1,0:T(8,128)(2,1)S(1)} %get-tuple-element.17), channel_id=1, source_target_pairs={{0,2},{1,3},{2,4},{3,5},{4,6},{5,7},{6,0},{7,1},{8,10},{9,11},{10,... | collective-permute-start | bytes 786440 | tf_op jit(solution)/shard_map/ppermute | solution.py:382
  83.3 9.0 %collective-permute-start.10 = (bf16[2,4,128,128]{3,2,1,0:T(8,128)(2,1)S(1)}, bf16[2,4,128,128]{3,2,1,0:T(8,128)(2,1)S(1)}, u32[]{:S(2)}, u32[]{:S(2)}) collective-permute-start(bf16[2,4,128,128]{3,2,1,0:T(8,128)(2,1)S(1)} %get-tuple-element.18), channel_id=1, source_target_pairs={{0,4},{1,5},{2,6},{3,7},{4,0},{5,1},{6,2},{7,3},{8,12},{9,13},{10,... | collective-permute-start | bytes 786440 | tf_op jit(solution)/shard_map/ppermute | solution.py:382
  85.5 13.9 %collective-permute-start.11 = (bf16[2,4,128,128]{3,2,1,0:T(8,128)(2,1)S(1)}, bf16[2,4,128,128]{3,2,1,0:T(8,128)(2,1)S(1)}, u32[]{:S(2)}, u32[]{:S(2)}) collective-permute-start(bf16[2,4,128,128]{3,2,1,0:T(8,128)(2,1)S(1)} %get-tuple-element.19), channel_id=1, source_target_pairs={{0,6},{1,7},{2,0},{3,1},{4,2},{5,3},{6,4},{7,5},{8,14},{9,15},{10,... | collective-permute-start | bytes 786440 | tf_op jit(solution)/shard_map/ppermute | solution.py:382
  86.3 15.8 %collective-permute-start.2 = (bf16[2,4,128,128]{3,2,1,0:T(8,128)(2,1)S(1)}, bf16[2,4,128,128]{3,2,1,0:T(8,128)(2,1)S(1)}, u32[]{:S(2)}, u32[]{:S(2)}) collective-permute-start(bf16[2,4,128,128]{3,2,1,0:T(8,128)(2,1)S(1)} %get-tuple-element.14), channel_id=1, source_target_pairs={{0,2},{1,3},{2,4},{3,5},{4,6},{5,7},{6,0},{7,1},{8,10},{9,11},{10,... | collective-permute-start | bytes 786440 | tf_op jit(solution)/shard_map/ppermute | solution.py:382
  89.1 14.5 %collective-permute-start.3 = (bf16[2,4,128,128]{3,2,1,0:T(8,128)(2,1)S(1)}, bf16[2,4,128,128]{3,2,1,0:T(8,128)(2,1)S(1)}, u32[]{:S(2)}, u32[]{:S(2)}) collective-permute-start(bf16[2,4,128,128]{3,2,1,0:T(8,128)(2,1)S(1)} %get-tuple-element.15), channel_id=1, source_target_pairs={{0,4},{1,5},{2,6},{3,7},{4,0},{5,1},{6,2},{7,3},{8,12},{9,13},{10,... | collective-permute-start | bytes 786440 | tf_op jit(solution)/shard_map/ppermute | solution.py:382
  90.9 19.0 %collective-permute-start.4 = (bf16[2,4,128,128]{3,2,1,0:T(8,128)(2,1)S(1)}, bf16[2,4,128,128]{3,2,1,0:T(8,128)(2,1)S(1)}, u32[]{:S(2)}, u32[]{:S(2)}) collective-permute-start(bf16[2,4,128,128]{3,2,1,0:T(8,128)(2,1)S(1)} %get-tuple-element.16), channel_id=1, source_target_pairs={{0,6},{1,7},{2,0},{3,1},{4,2},{5,3},{6,4},{7,5},{8,14},{9,15},{10,... | collective-permute-start | bytes 786440 | tf_op jit(solution)/shard_map/ppermute | solution.py:382
  100.2 30.1 %copy-start.3 = (s32[16,2]{0,1:T(2,128)S(1)}, s32[16,2]{0,1:T(2,128)}, u32[]{:S(2)}) copy-start(s32[16,2]{0,1:T(2,128)} %param.11) | copy-start | bytes 388
  100.2 11.6 %collective-permute-start.12 = (bf16[2,4,128,128]{3,2,1,0:T(8,128)(2,1)S(1)}, bf16[2,4,128,128]{3,2,1,0:T(8,128)(2,1)S(1)}, u32[]{:S(2)}, u32[]{:S(2)}) collective-permute-start(bf16[2,4,128,128]{3,2,1,0:T(8,128)(2,1)S(1)} %shard_map.68.mine_ref), channel_id=1, source_target_pairs={{0,1},{1,0},{2,3},{3,2},{4,5},{5,4},{6,7},{7,6},{8,9},{9,8},{10,11... | collective-permute-start | bytes 786440 | tf_op jit(solution)/shard_map/ppermute | solution.py:387
  110.8 14.3 %collective-permute-start.5 = (bf16[2,4,128,128]{3,2,1,0:T(8,128)(2,1)S(1)}, bf16[2,4,128,128]{3,2,1,0:T(8,128)(2,1)}, u32[]{:S(2)}, u32[]{:S(2)}) collective-permute-start(bf16[2,4,128,128]{3,2,1,0:T(8,128)(2,1)S(1)} %shard_map.65.mine_ref), channel_id=1, source_target_pairs={{0,1},{1,0},{2,3},{3,2},{4,5},{5,4},{6,7},{7,6},{8,9},{9,8},{10,11... | collective-permute-start | bytes 786440 | tf_op jit(solution)/shard_map/ppermute | solution.py:387
  113.5 15.0 %collective-permute-start.15 = (bf16[2,4,128,128]{3,2,1,0:T(8,128)(2,1)}, bf16[2,4,128,128]{3,2,1,0:T(8,128)(2,1)}, u32[]{:S(2)}, u32[]{:S(2)}) collective-permute-start(bf16[2,4,128,128]{3,2,1,0:T(8,128)(2,1)} %shard_map.69.refs_4_), channel_id=1, source_target_pairs={{0,6},{1,7},{2,0},{3,1},{4,2},{5,3},{6,4},{7,5},{8,14},{9,15},{10,... | collective-permute-start | bytes 786440 | tf_op jit(solution)/shard_map/ppermute | solution.py:382
  113.6 119.8 %all-to-all-start = ((bf16[16,128,128]{2,1,0:T(8,128)(2,1)}), bf16[16,128,128]{2,1,0:T(8,128)(2,1)S(1)}, u32[]{:S(2)}, u32[]{:S(2)}) async-start(bf16[16,128,128]{2,1,0:T(8,128)(2,1)} %get-tuple-element.13), calls=%async_computation | async-start | bytes 1048576 | tf_op jit(solution)/shard_map/all_to_all | solution.py:377
  122.3 9.5 %collective-permute-start.14 = (bf16[2,4,128,128]{3,2,1,0:T(8,128)(2,1)}, bf16[2,4,128,128]{3,2,1,0:T(8,128)(2,1)}, u32[]{:S(2)}, u32[]{:S(2)}) collective-permute-start(bf16[2,4,128,128]{3,2,1,0:T(8,128)(2,1)} %shard_map.69.refs_4_), channel_id=1, source_target_pairs={{0,4},{1,5},{2,6},{3,7},{4,0},{5,1},{6,2},{7,3},{8,12},{9,13},{10,... | collective-permute-start | bytes 786440 | tf_op jit(solution)/shard_map/ppermute | solution.py:382
  123.3 13.5 %collective-permute-start.13 = (bf16[2,4,128,128]{3,2,1,0:T(8,128)(2,1)}, bf16[2,4,128,128]{3,2,1,0:T(8,128)(2,1)}, u32[]{:S(2)}, u32[]{:S(2)}) collective-permute-start(bf16[2,4,128,128]{3,2,1,0:T(8,128)(2,1)} %shard_map.69.refs_4_), channel_id=1, source_target_pairs={{0,2},{1,3},{2,4},{3,5},{4,6},{5,7},{6,0},{7,1},{8,10},{9,11},{10,... | collective-permute-start | bytes 786440 | tf_op jit(solution)/shard_map/ppermute | solution.py:382
  126.7 11.4 %collective-permute-start.8 = (bf16[2,4,128,128]{3,2,1,0:T(8,128)(2,1)}, bf16[2,4,128,128]{3,2,1,0:T(8,128)(2,1)S(1)}, u32[]{:S(2)}, u32[]{:S(2)}) collective-permute-start(bf16[2,4,128,128]{3,2,1,0:T(8,128)(2,1)} %shard_map.66.refs_0_), channel_id=1, source_target_pairs={{0,6},{1,7},{2,0},{3,1},{4,2},{5,3},{6,4},{7,5},{8,14},{9,15},{10,... | collective-permute-start | bytes 786440 | tf_op jit(solution)/shard_map/ppermute | solution.py:382
  126.8 16.2 %collective-permute-start.7 = (bf16[2,4,128,128]{3,2,1,0:T(8,128)(2,1)}, bf16[2,4,128,128]{3,2,1,0:T(8,128)(2,1)}, u32[]{:S(2)}, u32[]{:S(2)}) collective-permute-start(bf16[2,4,128,128]{3,2,1,0:T(8,128)(2,1)} %shard_map.66.refs_0_), channel_id=1, source_target_pairs={{0,4},{1,5},{2,6},{3,7},{4,0},{5,1},{6,2},{7,3},{8,12},{9,13},{10,... | collective-permute-start | bytes 786440 | tf_op jit(solution)/shard_map/ppermute | solution.py:382
  128.4 19.7 %collective-permute-start.6 = (bf16[2,4,128,128]{3,2,1,0:T(8,128)(2,1)}, bf16[2,4,128,128]{3,2,1,0:T(8,128)(2,1)}, u32[]{:S(2)}, u32[]{:S(2)}) collective-permute-start(bf16[2,4,128,128]{3,2,1,0:T(8,128)(2,1)} %shard_map.66.refs_0_), channel_id=1, source_target_pairs={{0,2},{1,3},{2,4},{3,5},{4,6},{5,7},{6,0},{7,1},{8,10},{9,11},{10,... | collective-permute-start | bytes 786440 | tf_op jit(solution)/shard_map/ppermute | solution.py:382
  232.6 0.8 copy-start
  233.4 68.4 %all-to-all-start.5 = ((bf16[16,128,128]{2,1,0:T(8,128)(2,1)}), bf16[16,128,128]{2,1,0:T(8,128)(2,1)}, u32[]{:S(2)}, u32[]{:S(2)}) async-start(bf16[16,128,128]{2,1,0:T(8,128)(2,1)} %copy-done), calls=%async_computation.5 | async-start | bytes 1048576 | tf_op jit(solution)/shard_map/all_to_all | solution.py:377
  301.8 24.4 %all-to-all-start.3 = ((bf16[16,128,128]{2,1,0:T(8,128)(2,1)}), bf16[16,128,128]{2,1,0:T(8,128)(2,1)S(1)}, u32[]{:S(2)}, u32[]{:S(2)}) async-start(bf16[16,128,128]{2,1,0:T(8,128)(2,1)} %shard_map.71), calls=%async_computation.3 | async-start | bytes 1048576 | tf_op jit(solution)/shard_map/all_to_all | solution.py:377

commit v3 on v2

--- a/solution.py
+++ b/solution.py
@@ -17,39 +17,32 @@
 F32 = jnp.float32
 
 
-def blend_kernel(strength_ref, own_ref, partner_ref, *out_refs, heads):
+ANY = pl.BlockSpec(memory_space=pl.ANY)
+SMEM = pl.BlockSpec(memory_space=pltpu.SMEM)
+
+
+def blend_kernel(strength_ref, own_ref, partner_ref, out_ref, *, heads):
     first = pl.program_id(0) * heads
     for head in range(heads):
         share = strength_ref[0, first + head]
         lanes = slice(head * HEAD, (head + 1) * HEAD)
-        mixed = (
+        out_ref[head] = (
             (1.0 - share) * own_ref[:, :, lanes].astype(F32)
             + share * partner_ref[:, :, lanes].astype(F32)
         ).astype(BF16)
-        if len(out_refs) == 1:
-            out_refs[0][head] = mixed
-        else:
-            for frame, out_ref in enumerate(out_refs):
-                out_ref[head] = mixed[frame]
-
-
-def blend_heads(strength, own, partner, per_frame, steps=2):
+
+
+def blend_heads(strength, own, partner, steps=2):
     frames, rows, width = own.shape
     heads = width // HEAD
     group = heads // steps
     block = pl.BlockSpec((frames, rows, group * HEAD), lambda h: (0, 0, h))
-    if per_frame:
-        out_specs = [pl.BlockSpec((group, rows, HEAD), lambda h: (h, 0, 0))] * frames
-        out_shape = [jax.ShapeDtypeStruct((heads, rows, HEAD), BF16)] * frames
-    else:
-        out_specs = [pl.BlockSpec((group, frames, rows, HEAD), lambda h: (h, 0, 0, 0))]
-        out_shape = [jax.ShapeDtypeStruct((heads, frames, rows, HEAD), BF16)]
     return pl.pallas_call(
         functools.partial(blend_kernel, heads=group),
         grid=(steps,),
-        in_specs=[pl.BlockSpec(memory_space=pltpu.SMEM), block, block],
-        out_specs=out_specs,
-        out_shape=out_shape,
+        in_specs=[SMEM, block, block],
+        out_specs=pl.BlockSpec((group, frames, rows, HEAD), lambda h: (h, 0, 0, 0)),
+        out_shape=jax.ShapeDtypeStruct((heads, frames, rows, HEAD), BF16),
         cost_estimate=pl.CostEstimate(
             flops=3 * own.size, bytes_accessed=6 * own.size, transcendentals=0
         ),
@@ -78,7 +71,7 @@
     return pl.pallas_call(
         split_kernel,
         grid=(1,),
-        in_specs=[pl.BlockSpec(memory_space=pl.ANY)],
+        in_specs=[ANY],
         out_specs=whole(out),
         out_shape=out,
         scratch_shapes=[pltpu.SemaphoreType.DMA((heads,))],
@@ -116,103 +109,135 @@
     return jnp.max(sums)
 
 
-def copy_all(sources, target, sem):
-    copies = []
-    start = 0
-    for source in sources:
-        blocks = source.shape[0]
-        copies.append(
-            pltpu.make_async_copy(source, target.at[pl.ds(start, blocks)], sem.at[len(copies)])
-        )
-        start += blocks
-    for copy in copies:
-        copy.start()
-    return copies
-
-
-def attend_kernel(valid_ref, query_ref, key_ref, value_ref, *refs, frame, tile, pieces, mode):
-    key_extra, value_extra = refs[:pieces], refs[pieces : 2 * pieces]
-    acc_in = refs[2 * pieces : 2 * pieces + 1] if mode == "more" else ()
-    out_ref, keys, values, acc, top, key_sem, value_sem = refs[2 * pieces + len(acc_in) :]
-    parts = keys.shape[0]
-    blocks, rows = query_ref.shape[0], query_ref.shape[1]
-    step = tile // rows
-
-    key_copies, value_copies = [], []
-    for part in range(parts):
-        if part == 0:
-            key_sources, value_sources = [key_ref.at[:, frame]], [value_ref.at[:, frame]]
-        else:
-            key_sources = [ref.at[part - 1] for ref in key_extra]
-            value_sources = [ref.at[part - 1] for ref in value_extra]
-        key_copies += copy_all(key_sources, keys.at[part], key_sem.at[part])
-        value_copies += copy_all(value_sources, values.at[part], value_sem.at[part])
+def attend_kernel(valid_ref, *refs, frame, pieces, mode):
+    refs = list(refs)
+    frame = pl.program_id(0) if mode == "own" else frame
+    unsafe_in, acc_in = (refs.pop(0), refs.pop(0)) if mode == "more" else (None, None)
+    query_ref, key_ref, value_ref = refs[:3]
+    key_extra, value_extra = refs[3 : 3 + pieces], refs[3 + pieces : 3 + 2 * pieces]
+    refs = refs[3 + 2 * pieces :]
+    flag = 0
+    if mode == "own":
+        acc, unsafe = refs[:2]
+        flag = frame
+        refs = refs[2:]
+    else:
+        out_ref, acc, unsafe = refs[:3]
+        refs = refs[3:]
+    keys, values, top, key_sem, value_sem = refs
+    parts, cuts = keys.shape[:2]
+    blocks, rows = query_ref.shape[-3], query_ref.shape[-2]
+    quarter = blocks // cuts
+    tile = quarter * rows
+
+    def fetch(part):
+        for cut in range(cuts):
+            if part == 0:
+                span = pl.ds(cut * quarter, quarter)
+                key, value = key_ref.at[span, frame], value_ref.at[span, frame]
+            else:
+                key, value = key_extra[cut].at[part - 1], value_extra[cut].at[part - 1]
+            yield (
+                pltpu.make_async_copy(key, keys.at[part, cut], key_sem.at[part, cut]),
+                pltpu.make_async_copy(value, values.at[part, cut], value_sem.at[part, cut]),
+            )
+
+    def start(part):
+        for key_copy, value_copy in fetch(part):
+            key_copy.start()
+            value_copy.start()
+
+    def wait(target, sem, part):
+        for cut in range(cuts):
+            there = target.at[part, cut]
+            pltpu.make_async_copy(there, there, sem.at[part, cut]).wait()
+
+    def rows_of(target, part, cut):
+        return target[part, cut].reshape(tile, HEAD)
+
+    def add_part(part, pair, query_norm, assign):
+        wait(keys, key_sem, part)
+        safe = query_norm * norm_max(keys[part]) * (SCALE * SCALE) <= SAFE * SAFE
+        wait(values, value_sem, part)
+
+        @pl.when(safe)
+        def _():
+            for cut in range(cuts):
+                weights = jnp.exp2(score_tile(pair, rows_of(keys, part, cut)))
+                sums = weighted(weights, rows_of(values, part, cut))
+                acc[...] = sums if assign and cut == 0 else acc[...] + sums
+
+        @pl.when(jnp.logical_not(safe))
+        def _():
+            unsafe[flag] = 1
+
+    first = 1 if mode == "more" else 0
+    if first == 0:
+        start(0)
+    for part in range(1, parts):
+
+        @pl.when(valid_ref[part] > 0)
+        def _():
+            start(part)
 
     query = query_ref[...].reshape(-1, HEAD)
     query_norm = norm_max(query)
-    for copy in key_copies:
-        copy.wait()
-    key_norm = norm_max(keys[0])
-    for part in range(1, parts):
-        key_norm = jnp.maximum(key_norm, norm_max(keys[part]))
-    safe = query_norm * key_norm * (SCALE * SCALE) <= SAFE * SAFE
-    for copy in value_copies:
-        copy.wait()
-
-    def tiles(part, first=0, count=blocks):
-        for start in range(0, count, step):
-            span = pl.ds(first + start, step)
-            yield keys[part, span].reshape(tile, HEAD), values[part, span].reshape(tile, HEAD)
+    pair = scaled_split(query)
+    if mode == "more":
+        unsafe[0] = unsafe_in[frame]
+        acc[...] = acc_in[...]
+    else:
+        unsafe[flag] = 0
+        add_part(0, pair, query_norm, True)
+
+    if mode == "own":
+        return
+
+    def one_part(part, carry):
+        @pl.when(valid_ref[part] > 0)
+        def _():
+            add_part(part, pair, query_norm, False)
+
+        return carry
+
+    lax.fori_loop(1, parts, one_part, 0)
 
     def finish(sums):
         return (sums[:, :HEAD] / sums[:, HEAD:]).astype(BF16)
 
-    @pl.when(safe)
+    @pl.when(unsafe[0] == 0)
     def _():
-        pair = scaled_split(query)
-        sums = out_ref if mode == "own" else acc
-        sums[...] = acc_in[0][...] if mode == "more" else jnp.zeros_like(sums)
-
-        def half_part(index, carry):
-            part = index // 2
-
-            @pl.when(valid_ref[part] > 0)
-            def _():
-                half = blocks // 2
-                for key, value in tiles(part, lax.rem(index, 2) * half, half):
-                    sums[...] += weighted(jnp.exp2(score_tile(pair, key)), value)
-
-            return carry
-
-        lax.fori_loop(2 if mode == "more" else 0, 2 * parts, half_part, 0)
-        if mode != "own":
-            out_ref[...] = finish(sums[...]).reshape(out_ref.shape)
-
-    if mode == "own":
-        return
-
-    @pl.when(jnp.logical_not(safe))
+        out_ref[...] = finish(acc[...]).reshape(out_ref.shape)
+
+    @pl.when(unsafe[0] > 0)
     def _():
+        if mode == "more":
+            start(0)
+            wait(keys, key_sem, 0)
+            wait(values, value_sem, 0)
+
         def one_block(block, carry):
             pair = scaled_split(query_ref[block])
             sums = acc.at[pl.ds(0, rows)]
             sums[...] = jnp.zeros_like(sums)
             top[...] = jnp.full_like(top, LOWEST)
 
-            def one_part(part, carry):
+            def slow_part(part, carry):
                 @pl.when(valid_ref[part] > 0)
                 def _():
-                    for key, value in tiles(part):
-                        scores = score_tile(pair, key)
+                    for cut in range(cuts):
+                        scores = score_tile(pair, rows_of(keys, part, cut))
                         old_top = top[:, :1]
                         new_top = jnp.maximum(old_top, jnp.max(scores, axis=1, keepdims=True))
-                        part_sums = weighted(jnp.exp2(scores - new_top), value)
+                        part_sums = weighted(
+                            jnp.exp2(scores - new_top), rows_of(values, part, cut)
+                        )
                         sums[...] = sums[...] * jnp.exp2(old_top - new_top) + part_sums
                         top[...] = jnp.broadcast_to(new_top, top.shape)
 
                 return carry
 
-            lax.fori_loop(0, parts, one_part, 0)
+            lax.fori_loop(0, parts, slow_part, 0)
             out_ref[block] = finish(sums[...])
             return carry
 
@@ -225,41 +250,52 @@
     )
 
 
-ANY = pl.BlockSpec(memory_space=pl.ANY)
-SMEM = pl.BlockSpec(memory_space=pltpu.SMEM)
-
-
-def attend(mode, frame, valid, query, key, value, key_extra=(), value_extra=(), acc=None, tile=512):
-    blocks, rows, _ = query.shape
+def attend(mode, frame, valid, query, key, value, key_extra=(), value_extra=(), own=(), cuts=4):
+    blocks, frames, rows, _ = query.shape
     total = blocks * rows
     parts = valid.shape[0] if mode != "own" else 1
     pieces = len(key_extra)
+    acc = jax.ShapeDtypeStruct((frames, total, 2 * HEAD), F32)
+    flag = jax.ShapeDtypeStruct((frames,), jnp.int32)
+    out = jax.ShapeDtypeStruct((blocks, rows, HEAD), BF16)
+    kept = pltpu.VMEM((parts, cuts, blocks // cuts, rows, HEAD), BF16)
+    sems = pltpu.SemaphoreType.DMA((parts, cuts))
+    scratch = [kept, kept, pltpu.VMEM((rows, HEAD), F32), sems, sems]
     if mode == "own":
-        out = jax.ShapeDtypeStruct((total, 2 * HEAD), F32)
+        out_shape = [acc, flag]
+        out_specs = [pl.BlockSpec((None, total, 2 * HEAD), lambda i: (i, 0, 0)), SMEM]
     else:
-        out = jax.ShapeDtypeStruct((blocks, rows, HEAD), BF16)
-    accs = [acc] if mode == "more" else []
-    return pl.pallas_call(
-        functools.partial(attend_kernel, frame=frame, tile=tile, pieces=pieces, mode=mode),
-        grid=(1,),
-        in_specs=[SMEM, whole(query), ANY, ANY, *[ANY] * (2 * pieces), *[whole(a) for a in accs]],
-        out_specs=whole(out),
-        out_shape=out,
-        scratch_shapes=[
-            pltpu.VMEM((parts, blocks, rows, HEAD), BF16),
-            pltpu.VMEM((parts, blocks, rows, HEAD), BF16),
-            pltpu.VMEM((total, 2 * HEAD), F32),
-            pltpu.VMEM((rows, HEAD), F32),
-            pltpu.SemaphoreType.DMA((parts, max(1, pieces))),
-            pltpu.SemaphoreType.DMA((parts, max(1, pieces))),
+        out_shape, out_specs = [out], [whole(out)]
+        scratch = [pltpu.VMEM(acc.shape[1:], F32), pltpu.SMEM((1,), jnp.int32)] + scratch
+    if mode == "own":
+        query_spec = pl.BlockSpec((blocks, None, rows, HEAD), lambda i: (0, i, 0, 0))
+    else:
+        query_spec = pl.BlockSpec(
+            (blocks, None, rows, HEAD), lambda i: (0, frame, 0, 0), pipeline_mode=pl.Buffered(1)
+        )
+    acc_spec = pl.BlockSpec(
+        (None, total, 2 * HEAD), lambda i: (frame, 0, 0), pipeline_mode=pl.Buffered(1)
+    )
+    result = pl.pallas_call(
+        functools.partial(attend_kernel, frame=frame, pieces=pieces, mode=mode),
+        grid=(frames if mode == "own" else 1,),
+        in_specs=[
+            SMEM,
+            *([SMEM, acc_spec] if own else []),
+            query_spec,
+            *[ANY] * (2 + 2 * pieces),
         ],
+        out_specs=out_specs,
+        out_shape=out_shape,
+        scratch_shapes=scratch,
         compiler_params=pltpu.CompilerParams(vmem_limit_bytes=24 << 20),
         cost_estimate=pl.CostEstimate(
-            flops=4 * total * total * HEAD * (parts - (mode == "more")),
+            flops=8 * total * total * HEAD,
             bytes_accessed=4 * total * HEAD * (1 + parts),
-            transcendentals=total * total,
+            transcendentals=2 * total * total,
         ),
-    )(valid, query, key, value, *key_extra, *value_extra, *accs)
+    )(valid, *own[::-1], query, key, value, *key_extra, *value_extra)
+    return result if mode == "own" else result[0]
 
 
 def cut_kernel(place_ref, keyframes_ref, source_ref, *refs, xs):
@@ -408,26 +444,24 @@
     value_heads = to_heads(value_rows)
     value_extra = spread_keyframes(value_heads, keyframes)
 
-    (key_rows,) = blend_heads(inject, keys, partner_keys, False)
+    key_rows = blend_heads(inject, keys, partner_keys)
     key_heads = to_heads(key_rows)
     key_extra = spread_keyframes(key_heads, keyframes)
 
-    query_rows = blend_heads(inject, queries, partner_queries, True)
-    query_frames = []
-    for f in range(frames):
-        query_frames.append(to_heads(query_rows[f]))
+    query_rows = blend_heads(inject, queries, partner_queries)
+    query_heads = to_heads(query_rows)
 
     first = lax.axis_index("mp") * frames
+    always = jnp.ones((1,), jnp.int32)
+    own = attend("own", None, always, query_heads, key_heads, value_heads)
     outs = []
     for f in range(frames):
         masks = lax.dynamic_index_in_dim(key_mask, first + f, 0, keepdims=False)
-        valid = jnp.concatenate([jnp.ones((1,), jnp.int32), masks])
-        extra = (key_extra, value_extra)
-        if f == 0:
-            acc = attend("own", f, valid, query_frames[f], key_heads, value_heads)
-            out = attend("more", f, valid, query_frames[f], key_heads, value_heads, *extra, acc)
-        else:
-            out = attend("all", f, valid, query_frames[f], key_heads, value_heads, *extra)
+        valid = jnp.concatenate([always, masks])
+        out = attend(
+            "more", f, valid, query_heads, key_heads, value_heads,
+            key_extra, value_extra, own,
+        )
         back = to_heads(out)
         heads, rows, _ = back.shape
         outs.append(back.transpose(1, 0, 2).reshape(rows, heads * HEAD))

time: 329 us -> 323 us (0.982)
  starting transfers between devices: 63 us -> 52.9 us
  local copies, waits for them, and re-layouts: 3.92 us -> 8.88 us
    all_to_all x6 -> x5, starting transfers between devices: 47.4 us -> 39.4 us  [to_heads(): return lax.all_to_all(value, 'seq', split_axis=0, concat_axis=0, tiled=True)]
    unnamed x8 -> x16, local copies, waits for them, and re-layouts: 0.8 us -> 5.76 us
    ppermute x12, waiting for transfers between devices: 35.8 us -> 31.7 us  [shift_x(): lax.ppermute(value, 'mp', [(m, (m + 2 * step) % size) for m in range(size)])]
    all_to_all x6 -> x5, waiting for transfers between devices: 17 us -> 17.2 us  [to_heads(): return lax.all_to_all(value, 'seq', split_axis=0, concat_axis=0, tiled=True)]
  transfers between devices with their start and end apart: 22 -> 21, of which waited for: 16 -> 17; matrix products, arithmetic and copies ran while one was open for 1% -> 1% of each run, Pallas kernels for 48% -> 31%
where the time goes in v3:
time: 323 us
  Pallas kernels  160 us (50%)
  waiting for transfers between devices  100 us (31%)
  starting transfers between devices  52.9 us (16%)
  local copies, waits for them, and re-layouts  8.88 us (3%)
    pallas_call x3, Pallas kernels, attend(): pl.pallas_call(functools.partial(attend_kernel, frame=frame, pieces=piece...  146 us
    ppermute x2, waiting for transfers between devices, swap_branch(): return lax.ppermute(value, 'branch', [(0, 1), (1, 0)])  48.5 us
    all_to_all x5, starting transfers between devices, to_heads(): return lax.all_to_all(value, 'seq', split_axis=0, concat_axis=0, tiled=True)  39.4 us
    ppermute x12, waiting for transfers between devices, shift_x(): lax.ppermute(value, 'mp', [(m, (m + 2 * step) % size) for m in range(size)])  31.7 us
    all_to_all x5, waiting for transfers between devices, to_heads(): return lax.all_to_all(value, 'seq', split_axis=0, concat_axis=0, tiled=True)  17.2 us
    ppermute x12, starting transfers between devices, shift_x(): lax.ppermute(value, 'mp', [(m, (m + 2 * step) % size) for m in range(size)])  10.4 us
    pallas_call x6, Pallas kernels, move_call(): pl.pallas_call(kernel, grid=(1,), in_specs=[SMEM, SMEM] + [ANY] * len(arr...  6.75 us
  transfers between devices with their start and end apart: 21, of which 17 were waited for; matrix products, arithmetic and copies ran while one was open for 1% of the time, Pallas kernels for 31%

profile of v3, /device:TPU:31, one launch (start us, length us, event | category | flops | bytes accessed | tf_op | source)
XLA Modules:
  0.0 322.6 jit_solution(11513708202862008420)
XLA Ops:
  0.0 2.5 split_heads.1
  2.5 9.3 %all-to-all-start.2 = ((bf16[16,2,128,128]{3,2,1,0:T(8,128)(2,1)}), bf16[16,2,128,128]{3,2,1,0:T(8,128)(2,1)S(1)}, u32[]{:S(2)}, u32[]{:S(2)}) async-start(bf16[16,2,128,128]{3,2,1,0:T(8,128)(2,1)} %split_heads.1), calls=%async_computation.2 | async-start | bytes 2097152 | tf_op jit(solution)/shard_map/all_to_all | solution.py:413
  12.3 24.3 %collective-permute-done.1.partner_ref = bf16[2,128,2048]{2,1,0:T(8,128)(2,1)} collective-permute-done((bf16[2,128,2048]{2,1,0:T(8,128)(2,1)S(1)}, bf16[2,128,2048]{2,1,0:T(8,128)(2,1)}, u32[]{:S(2)}, u32[]{:S(2)}) %collective-permute-start.1) | collective-permute-done | bytes 1048608 | tf_op jit(solution)/shard_map/ppermute | solution.py:409
  36.6 2.6 blend.3
  39.1 0.6 all-to-all-done.2.refs_2_.source_ref.refs_4_
  39.8 7.2 %all-to-all-start.1 = ((bf16[16,2,128,128]{3,2,1,0:T(8,128)(2,1)}), bf16[16,2,128,128]{3,2,1,0:T(8,128)(2,1)S(1)}, u32[]{:S(2)}, u32[]{:S(2)}) async-start(bf16[16,2,128,128]{3,2,1,0:T(8,128)(2,1)} %blend.3), calls=%async_computation.1 | async-start | bytes 2097152 | tf_op jit(solution)/shard_map/all_to_all | solution.py:413
  47.5 24.3 %collective-permute-done.partner_ref = bf16[2,128,2048]{2,1,0:T(8,128)(2,1)} collective-permute-done((bf16[2,128,2048]{2,1,0:T(8,128)(2,1)S(1)}, bf16[2,128,2048]{2,1,0:T(8,128)(2,1)}, u32[]{:S(2)}, u32[]{:S(2)}) %collective-permute-start) | collective-permute-done | bytes 1048608 | tf_op jit(solution)/shard_map/ppermute | solution.py:409
  71.8 2.5 blend.2
  74.3 0.6 all-to-all-done.1.refs_1_.source_ref.refs_3_
  74.9 7.2 %all-to-all-start = ((bf16[16,2,128,128]{3,2,1,0:T(8,128)(2,1)}), bf16[16,2,128,128]{3,2,1,0:T(8,128)(2,1)S(1)}, u32[]{:S(2)}, u32[]{:S(2)}) async-start(bf16[16,2,128,128]{3,2,1,0:T(8,128)(2,1)} %blend.2), calls=%async_computation | async-start | bytes 2097152 | tf_op jit(solution)/shard_map/all_to_all | solution.py:413
  82.1 0.9 shard_map.68
  83.3 2.1 collective-permute-start.10
  85.4 0.9 shard_map.65
  86.3 2.8 collective-permute-start.2
  89.2 1.6 collective-permute-done.9.refs_0_
  90.8 0.6 collective-permute-start.4
  91.4 0.9 collective-permute-done.10.refs_1_
  92.3 7.0 %collective-permute-done.11.refs_2_ = bf16[2,4,128,128]{3,2,1,0:T(8,128)(2,1)S(1)} collective-permute-done((bf16[2,4,128,128]{3,2,1,0:T(8,128)(2,1)S(1)}, bf16[2,4,128,128]{3,2,1,0:T(8,128)(2,1)S(1)}, u32[]{:S(2)}, u32[]{:S(2)}) %collective-permute-start.11) | collective-permute-done | bytes 262176 | tf_op jit(solution)/shard_map/ppermute | solution.py:418
  99.3 0.8 shard_map.69.mine_ref
  100.2 1.0 collective-permute-start.12
  101.2 0.9 collective-permute-done.2.refs_0_
  102.1 1.5 collective-permute-done.3.refs_1_
  103.6 6.3 %collective-permute-done.4.refs_2_ = bf16[2,4,128,128]{3,2,1,0:T(8,128)(2,1)S(1)} collective-permute-done((bf16[2,4,128,128]{3,2,1,0:T(8,128)(2,1)S(1)}, bf16[2,4,128,128]{3,2,1,0:T(8,128)(2,1)S(1)}, u32[]{:S(2)}, u32[]{:S(2)}) %collective-permute-start.4) | collective-permute-done | bytes 262176 | tf_op jit(solution)/shard_map/ppermute | solution.py:418
  109.9 0.8 shard_map.66.mine_ref
  110.7 1.0 collective-permute-start.5
  111.7 1.7 shard_map.70.refs_9_
  113.9 1.4 collective-permute-start.14
  115.3 1.5 collective-permute-start.13
  116.8 3.0 collective-permute-done.5.other_ref
  119.8 1.7 shard_map.67.refs_5_
  121.5 1.0 collective-permute-start.7
  122.5 1.3 collective-permute-done.15.refs_12_
  124.2 3.6 %shard_map.64 = (f32[2,2048,256]{2,1,0:T(8,128)S(1)}, s32[2]{0:T(128)S(1)}) custom-call(s32[1]{0:T(128)} %constant.6.clone.1.valid_ref, bf16[16,2,128,128]{3,2,1,0:T(8,128)(2,1)S(1)} %all-to-all-done.refs_0_.refs_2_, bf16[16,2,128,128]{3,2,1,0:T(8,128)(2,1)S(1)} %all-to-all-done.1.refs_1_.source_ref.refs_3_, ...), custom_call_target="tpu_custom_call" | custom-call | flops 4294967296 | bytes 2097152 | tf_op jit(solution)/shard_map/pallas_call | solution.py:279
  127.8 1.8 collective-permute-done.13.refs_10_
  129.6 5.5 %collective-permute-done.8.refs_8_ = bf16[2,4,128,128]{3,2,1,0:T(8,128)(2,1)S(1)} collective-permute-done((bf16[2,4,128,128]{3,2,1,0:T(8,128)(2,1)}, bf16[2,4,128,128]{3,2,1,0:T(8,128)(2,1)S(1)}, u32[]{:S(2)}, u32[]{:S(2)}) %collective-permute-start.8) | collective-permute-done | bytes 262176 | tf_op jit(solution)/shard_map/ppermute | solution.py:418
  135.2 2.2 collective-permute-done.7.refs_7_
  137.4 2.6 collective-permute-done.6.refs_6_
  139.9 57.7 %shard_map.71 = bf16[16,128,128]{2,1,0:T(8,128)(2,1)S(1)} custom-call(s32[3]{0:T(128)S(1)} %pad_add_fusion.1.valid_ref, s32[2]{0:T(128)S(1)} %get-tuple-element.13.refs_0_, f32[2,2048,256]{2,1,0:T(8,128)S(1)} %get-tuple-element.14.refs_1_, bf16[16,2,128,128]{3,2,1,0:T(8,128)(2,1)S(1)} %all-to-all-done.refs_0_.refs_2_, ...), custom_call_target="tpu_custom_call" | custom-call | flops 4294967296 | bytes 4194304 | tf_op jit(solution)/shard_map/pallas_call | solution.py:279
  197.6 0.8 copy-done.1
  198.4 2.0 copy-done.3
  200.4 8.5 %all-to-all-start.3 = ((bf16[16,128,128]{2,1,0:T(8,128)(2,1)}), bf16[16,128,128]{2,1,0:T(8,128)(2,1)}, u32[]{:S(2)}, u32[]{:S(2)}) async-start(bf16[16,128,128]{2,1,0:T(8,128)(2,1)} %copy-done.1), calls=%async_computation.3 | async-start | bytes 1048576 | tf_op jit(solution)/shard_map/all_to_all | solution.py:413
  208.9 2.2 copy-done.4
  211.1 84.6 %shard_map.72 = bf16[16,128,128]{2,1,0:T(8,128)(2,1)S(1)} custom-call(s32[3]{0:T(128)S(1)} %pad_add_fusion.valid_ref, s32[2]{0:T(128)S(1)} %get-tuple-element.13.refs_0_, f32[2,2048,256]{2,1,0:T(8,128)S(1)} %copy-done.4, bf16[16,2,128,128]{3,2,1,0:T(8,128)(2,1)S(1)} %all-to-all-done.refs_0_.refs_2_, ...), custom_call_target="tpu_custom_call" | custom-call | flops 4294967296 | bytes 4194304 | tf_op jit(solution)/shard_map/pallas_call | solution.py:279
  295.7 0.8 copy-done
  296.5 7.2 %all-to-all-start.4 = ((bf16[16,128,128]{2,1,0:T(8,128)(2,1)}), bf16[16,128,128]{2,1,0:T(8,128)(2,1)S(1)}, u32[]{:S(2)}, u32[]{:S(2)}) async-start(bf16[16,128,128]{2,1,0:T(8,128)(2,1)} %copy-done), calls=%async_computation.4 | async-start | bytes 1048576 | tf_op jit(solution)/shard_map/all_to_all | solution.py:413
  303.7 1.3 copy.7
  305.1 15.9 %all-to-all-done.4 = bf16[16,128,128]{2,1,0:T(8,128)(2,1)S(1)} async-done(((bf16[16,128,128]{2,1,0:T(8,128)(2,1)}), bf16[16,128,128]{2,1,0:T(8,128)(2,1)S(1)}, u32[]{:S(2)}, u32[]{:S(2)}) %all-to-all-start.4) | async-done | bytes 524320 | tf_op jit(solution)/shard_map/all_to_all | solution.py:413
  321.3 1.3 copy.9
  (29 shorter events, 2.9 us)
Async XLA Ops:
  0.0 11.8 %copy-start.5 = (bf16[1,2,128,2048]{3,2,1,0:T(8,128)(2,1)S(1)}, bf16[1,2,128,2048]{3,2,1,0:T(8,128)(2,1)}, u32[]{:S(2)}) copy-start(bf16[1,2,128,2048]{3,2,1,0:T(8,128)(2,1)} %param.7) | copy-start | bytes 3145732
  2.5 44.5 %copy-start.6 = (bf16[1,2,128,2048]{3,2,1,0:T(8,128)(2,1)S(1)}, bf16[1,2,128,2048]{3,2,1,0:T(8,128)(2,1)}, u32[]{:S(2)}) copy-start(bf16[1,2,128,2048]{3,2,1,0:T(8,128)(2,1)} %param.6) | copy-start | bytes 3145732
  2.5 37.3 %all-to-all-start.2 = ((bf16[16,2,128,128]{3,2,1,0:T(8,128)(2,1)}), bf16[16,2,128,128]{3,2,1,0:T(8,128)(2,1)S(1)}, u32[]{:S(2)}, u32[]{:S(2)}) async-start(bf16[16,2,128,128]{3,2,1,0:T(8,128)(2,1)} %split_heads.1), calls=%async_computation.2 | async-start | bytes 2097152 | tf_op jit(solution)/shard_map/all_to_all | solution.py:413
  11.8 24.8 %collective-permute-start.1 = (bf16[2,128,2048]{2,1,0:T(8,128)(2,1)S(1)}, bf16[2,128,2048]{2,1,0:T(8,128)(2,1)}, u32[]{:S(2)}, u32[]{:S(2)}) collective-permute-start(bf16[2,128,2048]{2,1,0:T(8,128)(2,1)S(1)} %bitcast.15), channel_id=1, source_target_pairs={{0,128},{128,0},{1,129},{129,1},{2,130},{130,2},{3,131},{131,3},{4... | collective-permute-start | bytes 3145736 | tf_op jit(solution)/shard_map/ppermute | solution.py:409
  39.1 43.0 %copy-start.2 = (s32[2]{0:T(128)S(1)}, s32[2]{0:T(128)}, u32[]{:S(2)}) copy-start(s32[2]{0:T(128)} %keyframes_ref.11) | copy-start | bytes 28
  39.8 35.2 %all-to-all-start.1 = ((bf16[16,2,128,128]{3,2,1,0:T(8,128)(2,1)}), bf16[16,2,128,128]{3,2,1,0:T(8,128)(2,1)S(1)}, u32[]{:S(2)}, u32[]{:S(2)}) async-start(bf16[16,2,128,128]{3,2,1,0:T(8,128)(2,1)} %blend.3), calls=%async_computation.1 | async-start | bytes 2097152 | tf_op jit(solution)/shard_map/all_to_all | solution.py:413
  47.0 24.8 %collective-permute-start = (bf16[2,128,2048]{2,1,0:T(8,128)(2,1)S(1)}, bf16[2,128,2048]{2,1,0:T(8,128)(2,1)}, u32[]{:S(2)}, u32[]{:S(2)}) collective-permute-start(bf16[2,128,2048]{2,1,0:T(8,128)(2,1)S(1)} %bitcast.17), channel_id=1, source_target_pairs={{0,128},{128,0},{1,129},{129,1},{2,130},{130,2},{3,131},{131,3},{4... | collective-permute-start | bytes 3145736 | tf_op jit(solution)/shard_map/ppermute | solution.py:409
  74.3 39.3 %copy-start.7 = (s32[16,2]{0,1:T(2,128)S(1)}, s32[16,2]{0,1:T(2,128)}, u32[]{:S(2)}) copy-start(s32[16,2]{0,1:T(2,128)} %param.11) | copy-start | bytes 388
  74.9 49.3 %all-to-all-start = ((bf16[16,2,128,128]{3,2,1,0:T(8,128)(2,1)}), bf16[16,2,128,128]{3,2,1,0:T(8,128)(2,1)S(1)}, u32[]{:S(2)}, u32[]{:S(2)}) async-start(bf16[16,2,128,128]{3,2,1,0:T(8,128)(2,1)} %blend.2), calls=%async_computation | async-start | bytes 2097152 | tf_op jit(solution)/shard_map/all_to_all | solution.py:413
  83.0 7.8 %collective-permute-start.9 = (bf16[2,4,128,128]{3,2,1,0:T(8,128)(2,1)S(1)}, bf16[2,4,128,128]{3,2,1,0:T(8,128)(2,1)S(1)}, u32[]{:S(2)}, u32[]{:S(2)}) collective-permute-start(bf16[2,4,128,128]{3,2,1,0:T(8,128)(2,1)S(1)} %get-tuple-element.18), channel_id=1, source_target_pairs={{0,2},{1,3},{2,4},{3,5},{4,6},{5,7},{6,0},{7,1},{8,10},{9,11},{10,... | collective-permute-start | bytes 786440 | tf_op jit(solution)/shard_map/ppermute | solution.py:418
  83.3 9.0 %collective-permute-start.10 = (bf16[2,4,128,128]{3,2,1,0:T(8,128)(2,1)S(1)}, bf16[2,4,128,128]{3,2,1,0:T(8,128)(2,1)S(1)}, u32[]{:S(2)}, u32[]{:S(2)}) collective-permute-start(bf16[2,4,128,128]{3,2,1,0:T(8,128)(2,1)S(1)} %get-tuple-element.19), channel_id=1, source_target_pairs={{0,4},{1,5},{2,6},{3,7},{4,0},{5,1},{6,2},{7,3},{8,12},{9,13},{10,... | collective-permute-start | bytes 786440 | tf_op jit(solution)/shard_map/ppermute | solution.py:418
  85.4 13.9 %collective-permute-start.11 = (bf16[2,4,128,128]{3,2,1,0:T(8,128)(2,1)S(1)}, bf16[2,4,128,128]{3,2,1,0:T(8,128)(2,1)S(1)}, u32[]{:S(2)}, u32[]{:S(2)}) collective-permute-start(bf16[2,4,128,128]{3,2,1,0:T(8,128)(2,1)S(1)} %get-tuple-element.20), channel_id=1, source_target_pairs={{0,6},{1,7},{2,0},{3,1},{4,2},{5,3},{6,4},{7,5},{8,14},{9,15},{10,... | collective-permute-start | bytes 786440 | tf_op jit(solution)/shard_map/ppermute | solution.py:418
  86.3 15.8 %collective-permute-start.2 = (bf16[2,4,128,128]{3,2,1,0:T(8,128)(2,1)S(1)}, bf16[2,4,128,128]{3,2,1,0:T(8,128)(2,1)S(1)}, u32[]{:S(2)}, u32[]{:S(2)}) collective-permute-start(bf16[2,4,128,128]{3,2,1,0:T(8,128)(2,1)S(1)} %get-tuple-element.15), channel_id=1, source_target_pairs={{0,2},{1,3},{2,4},{3,5},{4,6},{5,7},{6,0},{7,1},{8,10},{9,11},{10,... | collective-permute-start | bytes 786440 | tf_op jit(solution)/shard_map/ppermute | solution.py:418
  89.0 14.5 %collective-permute-start.3 = (bf16[2,4,128,128]{3,2,1,0:T(8,128)(2,1)S(1)}, bf16[2,4,128,128]{3,2,1,0:T(8,128)(2,1)S(1)}, u32[]{:S(2)}, u32[]{:S(2)}) collective-permute-start(bf16[2,4,128,128]{3,2,1,0:T(8,128)(2,1)S(1)} %get-tuple-element.16), channel_id=1, source_target_pairs={{0,4},{1,5},{2,6},{3,7},{4,0},{5,1},{6,2},{7,3},{8,12},{9,13},{10,... | collective-permute-start | bytes 786440 | tf_op jit(solution)/shard_map/ppermute | solution.py:418
  90.8 19.0 %collective-permute-start.4 = (bf16[2,4,128,128]{3,2,1,0:T(8,128)(2,1)S(1)}, bf16[2,4,128,128]{3,2,1,0:T(8,128)(2,1)S(1)}, u32[]{:S(2)}, u32[]{:S(2)}) collective-permute-start(bf16[2,4,128,128]{3,2,1,0:T(8,128)(2,1)S(1)} %get-tuple-element.17), channel_id=1, source_target_pairs={{0,6},{1,7},{2,0},{3,1},{4,2},{5,3},{6,4},{7,5},{8,14},{9,15},{10,... | collective-permute-start | bytes 786440 | tf_op jit(solution)/shard_map/ppermute | solution.py:418
  100.2 11.6 %collective-permute-start.12 = (bf16[2,4,128,128]{3,2,1,0:T(8,128)(2,1)S(1)}, bf16[2,4,128,128]{3,2,1,0:T(8,128)(2,1)S(1)}, u32[]{:S(2)}, u32[]{:S(2)}) collective-permute-start(bf16[2,4,128,128]{3,2,1,0:T(8,128)(2,1)S(1)} %shard_map.69.mine_ref), channel_id=1, source_target_pairs={{0,1},{1,0},{2,3},{3,2},{4,5},{5,4},{6,7},{7,6},{8,9},{9,8},{10,11... | collective-permute-start | bytes 786440 | tf_op jit(solution)/shard_map/ppermute | solution.py:423
  110.7 9.1 %collective-permute-start.5 = (bf16[2,4,128,128]{3,2,1,0:T(8,128)(2,1)S(1)}, bf16[2,4,128,128]{3,2,1,0:T(8,128)(2,1)}, u32[]{:S(2)}, u32[]{:S(2)}) collective-permute-start(bf16[2,4,128,128]{3,2,1,0:T(8,128)(2,1)S(1)} %shard_map.66.mine_ref), channel_id=1, source_target_pairs={{0,1},{1,0},{2,3},{3,2},{4,5},{5,4},{6,7},{7,6},{8,9},{9,8},{10,11... | collective-permute-start | bytes 786440 | tf_op jit(solution)/shard_map/ppermute | solution.py:423
  113.4 10.4 %collective-permute-start.15 = (bf16[2,4,128,128]{3,2,1,0:T(8,128)(2,1)}, bf16[2,4,128,128]{3,2,1,0:T(8,128)(2,1)}, u32[]{:S(2)}, u32[]{:S(2)}) collective-permute-start(bf16[2,4,128,128]{3,2,1,0:T(8,128)(2,1)} %shard_map.70.refs_9_), channel_id=1, source_target_pairs={{0,6},{1,7},{2,0},{3,1},{4,2},{5,3},{6,4},{7,5},{8,14},{9,15},{10,... | collective-permute-start | bytes 786440 | tf_op jit(solution)/shard_map/ppermute | solution.py:418
  113.9 13.9 %collective-permute-start.14 = (bf16[2,4,128,128]{3,2,1,0:T(8,128)(2,1)}, bf16[2,4,128,128]{3,2,1,0:T(8,128)(2,1)}, u32[]{:S(2)}, u32[]{:S(2)}) collective-permute-start(bf16[2,4,128,128]{3,2,1,0:T(8,128)(2,1)} %shard_map.70.refs_9_), channel_id=1, source_target_pairs={{0,4},{1,5},{2,6},{3,7},{4,0},{5,1},{6,2},{7,3},{8,12},{9,13},{10,... | collective-permute-start | bytes 786440 | tf_op jit(solution)/shard_map/ppermute | solution.py:418
  115.3 14.3 %collective-permute-start.13 = (bf16[2,4,128,128]{3,2,1,0:T(8,128)(2,1)}, bf16[2,4,128,128]{3,2,1,0:T(8,128)(2,1)}, u32[]{:S(2)}, u32[]{:S(2)}) collective-permute-start(bf16[2,4,128,128]{3,2,1,0:T(8,128)(2,1)} %shard_map.70.refs_9_), channel_id=1, source_target_pairs={{0,2},{1,3},{2,4},{3,5},{4,6},{5,7},{6,0},{7,1},{8,10},{9,11},{10,... | collective-permute-start | bytes 786440 | tf_op jit(solution)/shard_map/ppermute | solution.py:418
  121.4 13.7 %collective-permute-start.8 = (bf16[2,4,128,128]{3,2,1,0:T(8,128)(2,1)}, bf16[2,4,128,128]{3,2,1,0:T(8,128)(2,1)S(1)}, u32[]{:S(2)}, u32[]{:S(2)}) collective-permute-start(bf16[2,4,128,128]{3,2,1,0:T(8,128)(2,1)} %shard_map.67.refs_5_), channel_id=1, source_target_pairs={{0,6},{1,7},{2,0},{3,1},{4,2},{5,3},{6,4},{7,5},{8,14},{9,15},{10,... | collective-permute-start | bytes 786440 | tf_op jit(solution)/shard_map/ppermute | solution.py:418
  121.5 15.8 %collective-permute-start.7 = (bf16[2,4,128,128]{3,2,1,0:T(8,128)(2,1)}, bf16[2,4,128,128]{3,2,1,0:T(8,128)(2,1)}, u32[]{:S(2)}, u32[]{:S(2)}) collective-permute-start(bf16[2,4,128,128]{3,2,1,0:T(8,128)(2,1)} %shard_map.67.refs_5_), channel_id=1, source_target_pairs={{0,4},{1,5},{2,6},{3,7},{4,0},{5,1},{6,2},{7,3},{8,12},{9,13},{10,... | collective-permute-start | bytes 786440 | tf_op jit(solution)/shard_map/ppermute | solution.py:418
  123.8 16.1 %collective-permute-start.6 = (bf16[2,4,128,128]{3,2,1,0:T(8,128)(2,1)}, bf16[2,4,128,128]{3,2,1,0:T(8,128)(2,1)}, u32[]{:S(2)}, u32[]{:S(2)}) collective-permute-start(bf16[2,4,128,128]{3,2,1,0:T(8,128)(2,1)} %shard_map.67.refs_5_), channel_id=1, source_target_pairs={{0,2},{1,3},{2,4},{3,5},{4,6},{5,7},{6,0},{7,1},{8,10},{9,11},{10,... | collective-permute-start | bytes 786440 | tf_op jit(solution)/shard_map/ppermute | solution.py:418
  197.6 0.8 copy-start.1
  198.4 2.0 copy-start.3
  200.4 96.1 %all-to-all-start.3 = ((bf16[16,128,128]{2,1,0:T(8,128)(2,1)}), bf16[16,128,128]{2,1,0:T(8,128)(2,1)}, u32[]{:S(2)}, u32[]{:S(2)}) async-start(bf16[16,128,128]{2,1,0:T(8,128)(2,1)} %copy-done.1), calls=%async_computation.3 | async-start | bytes 1048576 | tf_op jit(solution)/shard_map/all_to_all | solution.py:413
  208.9 2.2 copy-start.4
  295.7 0.8 copy-start
  296.5 24.4 %all-to-all-start.4 = ((bf16[16,128,128]{2,1,0:T(8,128)(2,1)}), bf16[16,128,128]{2,1,0:T(8,128)(2,1)S(1)}, u32[]{:S(2)}, u32[]{:S(2)}) async-start(bf16[16,128,128]{2,1,0:T(8,128)(2,1)} %copy-done), calls=%async_computation.4 | async-start | bytes 1048576 | tf_op jit(solution)/shard_map/all_to_all | solution.py:413

commit v4 on v3

v4 whole, which is shorter than its diff:
```python
import functools
import math

import jax
import jax.numpy as jnp
from jax import lax
from jax.experimental import pallas as pl
from jax.experimental.pallas import tpu as pltpu
from jax.sharding import PartitionSpec as P


HEAD = 128
SCALE = math.log2(math.e) / math.sqrt(HEAD)
SAFE = 100.0
LOWEST = -1e30
BF16 = jnp.bfloat16
F32 = jnp.float32


ANY = pl.BlockSpec(memory_space=pl.ANY)
SMEM = pl.BlockSpec(memory_space=pltpu.SMEM)


def blend_kernel(strength_ref, own_ref, partner_ref, *out_refs, heads):
    first = pl.program_id(0) * heads
    for head in range(heads):
        share = strength_ref[0, first + head]
        lanes = slice(head * HEAD, (head + 1) * HEAD)
        mixed = (
            (1.0 - share) * own_ref[:, :, lanes].astype(F32)
            + share * partner_ref[:, :, lanes].astype(F32)
        ).astype(BF16)
        if len(out_refs) == 1:
            out_refs[0][head] = mixed.reshape(-1, HEAD)
        else:
            for frame, out_ref in enumerate(out_refs):
                out_ref[head] = mixed[frame]


def blend_heads(strength, own, partner, split, steps=2):
    frames, rows, width = own.shape
    heads = width // HEAD
    group = heads // steps
    outs, count = (frames, rows) if split else (1, frames * rows)
    block = pl.BlockSpec((frames, rows, group * HEAD), lambda h: (0, 0, h))
    return pl.pallas_call(
        functools.partial(blend_kernel, heads=group),
        grid=(steps,),
        in_specs=[SMEM, block, block],
        out_specs=[pl.BlockSpec((group, count, HEAD), lambda h: (h, 0, 0))] * outs,
        out_shape=[jax.ShapeDtypeStruct((heads, count, HEAD), BF16)] * outs,
        cost_estimate=pl.CostEstimate(
            flops=3 * own.size, bytes_accessed=6 * own.size, transcendentals=0
        ),
        name="blend",
    )(strength, own, partner)


def split_kernel(source_ref, out_ref, sem):
    heads = out_ref.shape[0]
    copies = [
        pltpu.make_async_copy(
            source_ref.at[:, :, pl.ds(head * HEAD, HEAD)], out_ref.at[head], sem.at[head]
        )
        for head in range(heads)
    ]
    for copy in copies:
        copy.start()
    for copy in copies:
        copy.wait()


def split_heads(rows):
    frames, count, width = rows.shape
    heads = width // HEAD
    out = jax.ShapeDtypeStruct((heads, frames, count, HEAD), BF16)
    return pl.pallas_call(
        split_kernel,
        grid=(1,),
        in_specs=[ANY],
        out_specs=whole(out),
        out_shape=out,
        scratch_shapes=[pltpu.SemaphoreType.DMA((heads,))],
        cost_estimate=pl.CostEstimate(flops=0, bytes_accessed=4 * rows.size, transcendentals=0),
        name="split_heads",
    )(rows)


def dot_nt(a, b):
    return lax.dot_general(a, b, (((1,), (1,)), ((), ())), preferred_element_type=F32)


def scaled_split(query):
    scaled = query.astype(F32) * SCALE
    high = scaled.astype(BF16)
    low = (scaled - high.astype(F32)).astype(BF16)
    return jnp.concatenate([high, low], axis=1)


def score_tile(query_pair, key):
    return dot_nt(query_pair, jnp.concatenate([key, key], axis=1))


def with_ones(value):
    return jnp.concatenate([value, jnp.ones_like(value)], axis=1)


def weighted(weights, value):
    return jnp.dot(weights.astype(BF16), with_ones(value), preferred_element_type=F32)


def norm_max(rows):
    rows = rows.reshape(-1, HEAD)
    sums = jnp.dot(rows * rows, jnp.ones((HEAD, HEAD), BF16), preferred_element_type=F32)
    return jnp.max(sums)


def attend_kernel(valid_ref, *refs, frame, pieces, rows, mode):
    refs = list(refs)
    unsafe_in, acc_in = (refs.pop(0), refs.pop(0)) if mode == "more" else (None, None)
    query_in, key_ref, value_ref = refs[:3]
    key_extra, value_extra = refs[3 : 3 + pieces], refs[3 + pieces : 3 + 2 * pieces]
    refs = refs[3 + 2 * pieces :]
    if mode != "own":
        out_ref = refs.pop(0)
    acc, unsafe, keys, values, query_ref, top, key_sem, value_sem, sem = refs
    parts, cuts, blocks, cut_rows = keys.shape[:4]
    tile = blocks * cut_rows

    def fetch(part):
        for cut in range(cuts):
            if part == 0:
                span = pl.ds(frame * rows + cut * cut_rows, cut_rows)
                key, value = key_ref.at[:, span], value_ref.at[:, span]
            else:
                key, value = key_extra[cut].at[part - 1], value_extra[cut].at[part - 1]
            yield (
                pltpu.make_async_copy(key, keys.at[part, cut], key_sem.at[part, cut]),
                pltpu.make_async_copy(value, values.at[part, cut], value_sem.at[part, cut]),
            )

    def start(part):
        for key_copy, value_copy in fetch(part):
            key_copy.start()
            value_copy.start()

    def wait(target, sem, part):
        for cut in range(cuts):
            there = target.at[part, cut]
            pltpu.make_async_copy(there, there, sem.at[part, cut]).wait()

    def rows_of(target, part, cut):
        return target[part, cut].reshape(tile, HEAD)

    def add_part(part, pair, query_norm, assign):
        wait(keys, key_sem, part)
        safe = query_norm * norm_max(keys[part]) * (SCALE * SCALE) <= SAFE * SAFE
        wait(values, value_sem, part)

        @pl.when(safe)
        def _():
            for cut in range(cuts):
                weights = jnp.exp2(score_tile(pair, rows_of(keys, part, cut)))
                sums = weighted(weights, rows_of(values, part, cut))
                acc[...] = sums if assign and cut == 0 else acc[...] + sums

        @pl.when(jnp.logical_not(safe))
        def _():
            unsafe[0] = 1

    query_copy = pltpu.make_async_copy(query_in, query_ref, sem.at[0])
    query_copy.start()
    if mode == "more":
        acc_copy = pltpu.make_async_copy(acc_in, acc, sem.at[1])
        acc_copy.start()
    else:
        start(0)
    for part in range(1, parts):

        @pl.when(valid_ref[part] > 0)
        def _():
            start(part)

    query_copy.wait()
    query = query_ref[...].reshape(-1, HEAD)
    query_norm = norm_max(query)
    pair = scaled_split(query)
    if mode == "more":
        unsafe[0] = unsafe_in[0]
        acc_copy.wait()
    else:
        unsafe[0] = 0

    if mode == "own":
        add_part(0, pair, query_norm, True)
        return
    if mode == "all":
        acc[...] = jnp.zeros_like(acc)

    def one_part(part, carry):
        @pl.when(valid_ref[part] > 0)
        def _():
            add_part(part, pair, query_norm, False)

        return carry

    lax.fori_loop(1 if mode == "more" else 0, parts, one_part, 0)

    def finish(sums):
        return (sums[:, :HEAD] / sums[:, HEAD:]).astype(BF16)

    @pl.when(unsafe[0] == 0)
    def _():
        out_ref[...] = finish(acc[...]).reshape(out_ref.shape)

    @pl.when(unsafe[0] > 0)
    def _():
        if mode == "more":
            start(0)
            wait(keys, key_sem, 0)
            wait(values, value_sem, 0)

        def one_block(block, carry):
            pair = scaled_split(query_ref[block])
            sums = acc.at[pl.ds(0, rows)]
            sums[...] = jnp.zeros_like(sums)
            top[...] = jnp.full_like(top, LOWEST)

            def slow_part(part, carry):
                @pl.when(valid_ref[part] > 0)
                def _():
                    for cut in range(cuts):
                        scores = score_tile(pair, rows_of(keys, part, cut))
                        old_top = top[:, :1]
                        new_top = jnp.maximum(old_top, jnp.max(scores, axis=1, keepdims=True))
                        part_sums = weighted(
                            jnp.exp2(scores - new_top), rows_of(values, part, cut)
                        )
                        sums[...] = sums[...] * jnp.exp2(old_top - new_top) + part_sums
                        top[...] = jnp.broadcast_to(new_top, top.shape)

                return carry

            lax.fori_loop(0, parts, slow_part, 0)
            out_ref[block] = finish(sums[...])
            return carry

        lax.fori_loop(0, query_ref.shape[0], one_block, 0)


def whole(array):
    return pl.BlockSpec(
        array.shape, lambda i: (0,) * len(array.shape), pipeline_mode=pl.Buffered(1)
    )


def attend(mode, frame, valid, query, key, value, key_extra=(), value_extra=(), own=(), cuts=4):
    blocks, rows, _ = query.shape
    total = blocks * rows
    parts = valid.shape[0]
    pieces = len(key_extra)
    acc = jax.ShapeDtypeStruct((total, 2 * HEAD), F32)
    flag = jax.ShapeDtypeStruct((1,), jnp.int32)
    out = jax.ShapeDtypeStruct((blocks, rows, HEAD), BF16)
    kept = pltpu.VMEM((parts, cuts, blocks, rows // cuts, HEAD), BF16)
    sems = pltpu.SemaphoreType.DMA((parts, cuts))
    scratch = [
        kept, kept, pltpu.VMEM(query.shape, BF16), pltpu.VMEM((rows, HEAD), F32),
        sems, sems, pltpu.SemaphoreType.DMA((2,)),
    ]
    if mode == "own":
        out_shape, out_specs = [acc, flag], [whole(acc), SMEM]
    else:
        out_shape, out_specs = [out], [whole(out)]
        scratch = [pltpu.VMEM(acc.shape, F32), pltpu.SMEM((1,), jnp.int32)] + scratch
    work = {"own": 1, "more": parts - 1, "all": parts}[mode] * total * total
    result = pl.pallas_call(
        functools.partial(attend_kernel, frame=frame, pieces=pieces, rows=rows, mode=mode),
        grid=(1,),
        in_specs=[SMEM, *([SMEM, ANY] if own else []), *[ANY] * (3 + 2 * pieces)],
        out_specs=out_specs,
        out_shape=out_shape,
        scratch_shapes=scratch,
        compiler_params=pltpu.CompilerParams(vmem_limit_bytes=24 << 20),
        cost_estimate=pl.CostEstimate(
            flops=4 * work * HEAD, bytes_accessed=16 * total * HEAD, transcendentals=work
        ),
    )(valid, *own[::-1], query, key, value, *key_extra, *value_extra)
    return result if mode == "own" else result[0]


def piece_rows(keyframe, piece, shape):
    frames, rows, cuts = shape
    start = lax.rem(keyframe, frames) * rows + piece * (rows // cuts)
    return pl.ds(pl.multiple_of(start, rows // cuts), rows // cuts)


def run_copies(copies):
    for copy in copies:
        copy.start()
    for copy in copies:
        copy.wait()


def cut_kernel(place_ref, keyframes_ref, source_ref, *refs, shape):
    *out_refs, sem = refs
    x = place_ref[0] // 2
    copies = []
    for step, out_ref in enumerate(out_refs, 1):
        for j in range(out_ref.shape[0]):
            rows = piece_rows(keyframes_ref[j], lax.rem(x + step, shape[2]), shape)
            copies.append(
                pltpu.make_async_copy(source_ref.at[:, rows], out_ref.at[j], sem.at[len(copies)])
            )
    run_copies(copies)


def pick_x_kernel(place_ref, keyframes_ref, source_ref, *refs, shape, join):
    *got_refs, out_ref, sem = refs
    x = place_ref[0] // 2
    extras, _, cut_rows = got_refs[0].shape[:3]
    kept = source_ref.shape[1]
    if join:
        targets = [out_ref.at[:, pl.ds(kept + j * cut_rows, cut_rows)] for j in range(extras)]
        all_rows = pltpu.make_async_copy(source_ref, out_ref.at[:, pl.ds(0, kept)], sem.at[extras])
        all_rows.start()
    else:
        targets = [out_ref.at[j] for j in range(extras)]
    for j in range(extras):
        keyframe = keyframes_ref[j]
        step = lax.rem(x - keyframe // (2 * shape[0]) + shape[2], shape[2])

        @pl.when(step == 0)
        def _():
            rows = piece_rows(keyframe, x, shape)
            pltpu.make_async_copy(source_ref.at[:, rows], targets[j], sem.at[j]).start()

        for which, got_ref in enumerate(got_refs, 1):

            @pl.when(step == which)
            def _():
                pltpu.make_async_copy(got_ref.at[j], targets[j], sem.at[j]).start()

    for j in range(extras):
        pltpu.make_async_copy(got_refs[0].at[j], targets[j], sem.at[j]).wait()
    if join:
        all_rows.wait()


def pick_y_kernel(place_ref, keyframes_ref, mine_ref, other_ref, out_ref, sem, *, shape, kept):
    y = lax.rem(place_ref[0], 2)
    extras, _, cut_rows = out_ref.shape[:3]
    for j in range(extras):
        if kept is None:
            mine, other = mine_ref.at[j], other_ref.at[j]
        else:
            mine = mine_ref.at[:, pl.ds(kept + j * cut_rows, cut_rows)]
            other = other_ref.at[:, pl.ds(j * cut_rows, cut_rows)]
        same = lax.rem(keyframes_ref[j] // shape[0], 2) == y

        @pl.when(same)
        def _():
            pltpu.make_async_copy(mine, out_ref.at[j], sem.at[j]).start()

        @pl.when(jnp.logical_not(same))
        def _():
            pltpu.make_async_copy(other, out_ref.at[j], sem.at[j]).start()

    for j in range(extras):
        pltpu.make_async_copy(out_ref.at[j], out_ref.at[j], sem.at[j]).wait()


def move_call(kernel, out_shapes, place, keyframes, *arrays):
    moved = sum(math.prod(o.shape) for o in out_shapes)
    return pl.pallas_call(
        kernel,
        grid=(1,),
        in_specs=[SMEM, SMEM] + [ANY] * len(arrays),
        out_specs=[whole(o) for o in out_shapes],
        out_shape=out_shapes,
        scratch_shapes=[pltpu.SemaphoreType.DMA((len(out_shapes) * keyframes.shape[0] + 1,))],
        compiler_params=pltpu.CompilerParams(vmem_limit_bytes=8 << 20),
        cost_estimate=pl.CostEstimate(flops=0, bytes_accessed=4 * moved, transcendentals=0),
    )(place, keyframes, *arrays)


def swap_branch(value):
    return lax.ppermute(value, "branch", [(0, 1), (1, 0)])


def to_heads(value):
    return lax.all_to_all(value, "seq", split_axis=0, concat_axis=0, tiled=True)


def shift_x(value, step):
    size = lax.axis_size("mp")
    return lax.ppermute(value, "mp", [(m, (m + 2 * step) % size) for m in range(size)])


def flip_y(value):
    size = lax.axis_size("mp")
    return lax.ppermute(value, "mp", [(m, m ^ 1) for m in range(size)])


def spread_along_x(place, keyframes, source, shape, join):
    blocks = source.shape[0]
    extras, cut_rows = keyframes.shape[0], shape[1] // shape[2]
    piece = jax.ShapeDtypeStruct((extras, blocks, cut_rows, HEAD), BF16)
    cuts = move_call(
        functools.partial(cut_kernel, shape=shape),
        [piece] * (shape[2] - 1), place, keyframes, source,
    )
    got = [shift_x(cut, step) for step, cut in enumerate(cuts, 1)]
    if join:
        piece = jax.ShapeDtypeStruct((blocks, source.shape[1] + extras * cut_rows, HEAD), BF16)
    return move_call(
        functools.partial(pick_x_kernel, shape=shape, join=join),
        [piece], place, keyframes, source, *got,
    )[0]


def spread_from_x(place, keyframes, mine, shape, kept):
    extras, cut_rows = keyframes.shape[0], shape[1] // shape[2]
    other = flip_y(mine if kept is None else mine[:, kept:])
    blocks = mine.shape[1] if kept is None else mine.shape[0]
    (mine,) = move_call(
        functools.partial(pick_y_kernel, shape=shape, kept=kept),
        [jax.ShapeDtypeStruct((extras, blocks, cut_rows, HEAD), BF16)], place, keyframes, mine, other,
    )
    return [mine] + [shift_x(mine, step) for step in range(1, shape[2])]


def local(queries, keys, values, inject, keyframes, key_mask):
    queries, keys, values = queries[0], keys[0], values[0]
    frames, rows, _ = queries.shape
    shape = (frames, rows, lax.axis_size("mp") // 2)
    place = lax.axis_index("mp").astype(jnp.int32).reshape(1)
    partner_keys = swap_branch(keys)
    partner_queries = swap_branch(queries)

    value_rows = split_heads(values).reshape(-1, frames * rows, HEAD)
    value_heads = to_heads(value_rows)
    value_mine = spread_along_x(place, keyframes, value_heads, shape, False)
    value_extra = spread_from_x(place, keyframes, value_mine, shape, None)

    (key_rows,) = blend_heads(inject, keys, partner_keys, False)
    key_rows = spread_along_x(place, keyframes, key_rows, shape, True)
    key_heads = to_heads(key_rows)
    key_extra = spread_from_x(place, keyframes, key_heads, shape, frames * rows)

    query_rows = blend_heads(inject, queries, partner_queries, True)
    outs = []
    always = jnp.ones((1,), jnp.int32)
    for f in range(frames):
        query = to_heads(query_rows[f])
        masks = lax.dynamic_index_in_dim(key_mask, place[0] * frames + f, 0, keepdims=False)
        valid = jnp.concatenate([always, masks])
        extra = (key_extra, value_extra)
        if f == 0:
            own = attend("own", f, always, query, key_heads, value_heads)
            out = attend("more", f, valid, query, key_heads, value_heads, *extra, own)
        else:
            out = attend("all", f, valid, query, key_heads, value_heads, *extra)
        back = to_heads(out)
        outs.append(back.transpose(1, 0, 2).reshape(rows, -1))
    return jnp.stack(outs)[None]


def solution(mesh):
    return jax.shard_map(
        local,
        mesh=mesh,
        in_specs=(
            P("branch", "mp", "seq", None),
            P("branch", "mp", "seq", None),
            P("branch", "mp", "seq", None),
            P("branch", None),
            P(),
            P(),
        ),
        out_specs=P("branch", "mp", "seq", None),
        check_vma=False,
    )
```

time: 323 us -> 350 us (1.084)
  the two profiles are of different devices: /device:TPU:31 before, /device:TPU:23 now
where the time goes in v4:
time: 350 us; the launch traced here: 349 us
  Pallas kernels  159 us (45%)
  waiting for transfers between devices  120 us (34%)
  starting transfers between devices  62.3 us (18%)
  local copies, waits for them, and re-layouts  6.85 us (2%)
    pallas_call x3, Pallas kernels, attend(): pl.pallas_call(functools.partial(attend_kernel, frame=frame, pieces=piece...  145 us
    ppermute x2, waiting for transfers between devices, swap_branch(): return lax.ppermute(value, 'branch', [(0, 1), (1, 0)])  47.3 us
    all_to_all x6, starting transfers between devices, to_heads(): return lax.all_to_all(value, 'seq', split_axis=0, concat_axis=0, tiled=True)  45.3 us
    ppermute x12, waiting for transfers between devices, shift_x(): lax.ppermute(value, 'mp', [(m, (m + 2 * step) % size) for m in range(size)])  44.7 us
    all_to_all x6, waiting for transfers between devices, to_heads(): return lax.all_to_all(value, 'seq', split_axis=0, concat_axis=0, tiled=True)  22.9 us
    ppermute x12, starting transfers between devices, shift_x(): lax.ppermute(value, 'mp', [(m, (m + 2 * step) % size) for m in range(size)])  11.8 us
  transfers between devices with their start and end apart: 22, of which 16 were waited for; matrix products, arithmetic and copies ran while one was open for 0% of the time, Pallas kernels for 45%

profile of v4, /device:TPU:23, one launch (start us, length us, event | category | flops | bytes accessed | tf_op | source)
XLA Modules:
  0.0 348.6 jit_solution(105019818612660703)
XLA Ops:
  0.0 2.4 split_heads.1
  2.4 9.3 %all-to-all-start.2 = ((bf16[16,256,128]{2,1,0:T(8,128)(2,1)}), bf16[16,256,128]{2,1,0:T(8,128)(2,1)S(1)}, u32[]{:S(2)}, u32[]{:S(2)}) async-start(bf16[16,256,128]{2,1,0:T(8,128)(2,1)} %bitcast.11), calls=%async_computation.2 | async-start | bytes 2097152 | tf_op jit(solution)/shard_map/all_to_all | solution.py:392
  11.7 1.1 collective-permute-start.1
  12.8 23.6 %collective-permute-done.1.partner_ref = bf16[2,128,2048]{2,1,0:T(8,128)(2,1)S(1)} collective-permute-done((bf16[2,128,2048]{2,1,0:T(8,128)(2,1)S(1)}, bf16[2,128,2048]{2,1,0:T(8,128)(2,1)S(1)}, u32[]{:S(2)}, u32[]{:S(2)}) %collective-permute-start.1) | collective-permute-done | bytes 1048608 | tf_op jit(solution)/shard_map/ppermute | solution.py:388
  36.4 1.0 copy-done.6
  37.4 2.5 blend.3.source_ref
  39.9 1.2 copy-done
  41.2 0.7 shard_map.64
  42.2 2.1 collective-permute-start.3
  44.3 4.6 %collective-permute-done.2.refs_0_ = bf16[2,16,32,128]{3,2,1,0:T(8,128)(2,1)S(1)} collective-permute-done((bf16[2,16,32,128]{3,2,1,0:T(8,128)(2,1)S(1)}, bf16[2,16,32,128]{3,2,1,0:T(8,128)(2,1)S(1)}, u32[]{:S(2)}, u32[]{:S(2)}) %collective-permute-start.2) | collective-permute-done | bytes 262176 | tf_op jit(solution)/shard_map/ppermute | solution.py:397
  48.9 1.5 collective-permute-done.3.refs_1_
  50.4 7.2 %collective-permute-done.4.refs_2_ = bf16[2,16,32,128]{3,2,1,0:T(8,128)(2,1)S(1)} collective-permute-done((bf16[2,16,32,128]{3,2,1,0:T(8,128)(2,1)S(1)}, bf16[2,16,32,128]{3,2,1,0:T(8,128)(2,1)S(1)}, u32[]{:S(2)}, u32[]{:S(2)}) %collective-permute-start.4) | collective-permute-done | bytes 262176 | tf_op jit(solution)/shard_map/ppermute | solution.py:397
  58.3 1.1 copy-done.1
  59.4 7.2 %all-to-all-start.1 = ((bf16[16,320,128]{2,1,0:T(8,128)(2,1)}), bf16[16,320,128]{2,1,0:T(8,128)(2,1)S(1)}, u32[]{:S(2)}, u32[]{:S(2)}) async-start(bf16[16,320,128]{2,1,0:T(8,128)(2,1)} %copy-done.1), calls=%async_computation.1 | async-start | bytes 2621440 | tf_op jit(solution)/shard_map/all_to_all | solution.py:392
  66.5 1.1 collective-permute-start
  67.6 23.7 %collective-permute-done.partner_ref = bf16[2,128,2048]{2,1,0:T(8,128)(2,1)} collective-permute-done((bf16[2,128,2048]{2,1,0:T(8,128)(2,1)S(1)}, bf16[2,128,2048]{2,1,0:T(8,128)(2,1)}, u32[]{:S(2)}, u32[]{:S(2)}) %collective-permute-start) | collective-permute-done | bytes 1048608 | tf_op jit(solution)/shard_map/ppermute | solution.py:388
  91.4 2.5 blend.2
  93.9 5.9 %all-to-all-done.1.refs_1_.mine_ref.refs_3_ = bf16[16,320,128]{2,1,0:T(8,128)(2,1)S(1)} async-done(((bf16[16,320,128]{2,1,0:T(8,128)(2,1)}), bf16[16,320,128]{2,1,0:T(8,128)(2,1)S(1)}, u32[]{:S(2)}, u32[]{:S(2)}) %all-to-all-start.1) | async-done | bytes 1310752 | tf_op jit(solution)/shard_map/all_to_all | solution.py:392
  99.8 3.8 %all-to-all-start.4 = ((bf16[16,128,128]{2,1,0:T(8,128)(2,1)}), bf16[16,128,128]{2,1,0:T(8,128)(2,1)S(1)}, u32[]{:S(2)}, u32[]{:S(2)}) async-start(bf16[16,128,128]{2,1,0:T(8,128)(2,1)} %get-tuple-element.24), calls=%async_computation.4 | async-start | bytes 1048576 | tf_op jit(solution)/shard_map/all_to_all | solution.py:392
  103.6 0.7 shard_map.68
  104.3 0.8 collective-permute-start.9
  105.1 1.8 collective-permute-start.10
  106.9 5.3 %collective-permute-done.9.refs_0_ = bf16[2,16,32,128]{3,2,1,0:T(8,128)(2,1)S(1)} collective-permute-done((bf16[2,16,32,128]{3,2,1,0:T(8,128)(2,1)S(1)}, bf16[2,16,32,128]{3,2,1,0:T(8,128)(2,1)S(1)}, u32[]{:S(2)}, u32[]{:S(2)}) %collective-permute-start.9) | collective-permute-done | bytes 262176 | tf_op jit(solution)/shard_map/ppermute | solution.py:397
  112.2 2.0 collective-permute-done.10.refs_1_
  114.1 6.3 %collective-permute-done.11.refs_2_ = bf16[2,16,32,128]{3,2,1,0:T(8,128)(2,1)S(1)} collective-permute-done((bf16[2,16,32,128]{3,2,1,0:T(8,128)(2,1)S(1)}, bf16[2,16,32,128]{3,2,1,0:T(8,128)(2,1)S(1)}, u32[]{:S(2)}, u32[]{:S(2)}) %collective-permute-start.11) | collective-permute-done | bytes 262176 | tf_op jit(solution)/shard_map/ppermute | solution.py:397
  120.5 0.8 shard_map.69.mine_ref
  122.2 2.9 collective-permute-start.5
  125.1 5.2 %collective-permute-done.12.other_ref = bf16[2,16,32,128]{3,2,1,0:T(8,128)(2,1)S(1)} collective-permute-done((bf16[2,16,32,128]{3,2,1,0:T(8,128)(2,1)S(1)}, bf16[2,16,32,128]{3,2,1,0:T(8,128)(2,1)S(1)}, u32[]{:S(2)}, u32[]{:S(2)}) %collective-permute-start.12) | collective-permute-done | bytes 262176 | tf_op jit(solution)/shard_map/ppermute | solution.py:402
  130.3 1.6 shard_map.70.refs_9_.refs_7_
  132.0 10.0 %all-to-all-start = ((bf16[16,128,128]{2,1,0:T(8,128)(2,1)}), bf16[16,128,128]{2,1,0:T(8,128)(2,1)S(1)}, u32[]{:S(2)}, u32[]{:S(2)}) async-start(bf16[16,128,128]{2,1,0:T(8,128)(2,1)} %get-tuple-element.15), calls=%async_computation | async-start | bytes 1048576 | tf_op jit(solution)/shard_map/all_to_all | solution.py:392
  142.0 1.1 collective-permute-start.14
  143.0 2.2 collective-permute-start.13
  145.2 1.4 shard_map.67.refs_5_.refs_3_
  146.7 1.4 collective-permute-start.7
  148.1 2.0 collective-permute-start.6
  150.4 1.1 collective-permute-done.14.refs_11_.refs_9_
  151.5 5.5 %collective-permute-done.13.refs_10_.refs_8_ = bf16[2,16,32,128]{3,2,1,0:T(8,128)(2,1)} collective-permute-done((bf16[2,16,32,128]{3,2,1,0:T(8,128)(2,1)}, bf16[2,16,32,128]{3,2,1,0:T(8,128)(2,1)}, u32[]{:S(2)}, u32[]{:S(2)}) %collective-permute-start.13) | collective-permute-done | bytes 262176 | tf_op jit(solution)/shard_map/ppermute | solution.py:397
  157.0 0.8 collective-permute-done.8.refs_8_.refs_6_
  157.8 5.0 %collective-permute-done.7.refs_7_.refs_5_ = bf16[2,16,32,128]{3,2,1,0:T(8,128)(2,1)} collective-permute-done((bf16[2,16,32,128]{3,2,1,0:T(8,128)(2,1)}, bf16[2,16,32,128]{3,2,1,0:T(8,128)(2,1)}, u32[]{:S(2)}, u32[]{:S(2)}) %collective-permute-start.7) | collective-permute-done | bytes 262176 | tf_op jit(solution)/shard_map/ppermute | solution.py:397
  162.7 5.5 %collective-permute-done.6.refs_6_.refs_4_ = bf16[2,16,32,128]{3,2,1,0:T(8,128)(2,1)} collective-permute-done((bf16[2,16,32,128]{3,2,1,0:T(8,128)(2,1)}, bf16[2,16,32,128]{3,2,1,0:T(8,128)(2,1)}, u32[]{:S(2)}, u32[]{:S(2)}) %collective-permute-start.6) | collective-permute-done | bytes 262176 | tf_op jit(solution)/shard_map/ppermute | solution.py:397
  168.3 84.5 %shard_map.72 = bf16[16,128,128]{2,1,0:T(8,128)(2,1)S(1)} custom-call(s32[3]{0:T(128)S(1)} %pad_add_fusion.valid_ref, bf16[16,128,128]{2,1,0:T(8,128)(2,1)S(1)} %all-to-all-done.4.refs_0_, bf16[16,320,128]{2,1,0:T(8,128)(2,1)S(1)} %all-to-all-done.1.refs_1_.mine_ref.refs_3_, bf16[16,256,128]{2,1,0:T(8,128)(2,1)S(1)} %all-to-all-done.2.refs_2_.source_ref.refs_4_, ...), custom_call_target="tpu_custom_call" | custom-call | flops 6442450944 | bytes 4194304 | tf_op jit(solution)/shard_map/pallas_call | solution.py:277
  252.8 0.8 copy-done.2
  253.6 7.8 %all-to-all-start.5 = ((bf16[16,128,128]{2,1,0:T(8,128)(2,1)}), bf16[16,128,128]{2,1,0:T(8,128)(2,1)S(1)}, u32[]{:S(2)}, u32[]{:S(2)}) async-start(bf16[16,128,128]{2,1,0:T(8,128)(2,1)} %copy-done.2), calls=%async_computation.5 | async-start | bytes 1048576 | tf_op jit(solution)/shard_map/all_to_all | solution.py:392
  261.5 2.1 shard_map.66
  263.6 58.9 %shard_map.71 = bf16[16,128,128]{2,1,0:T(8,128)(2,1)} custom-call(s32[3]{0:T(128)S(1)} %pad_add_fusion.1.valid_ref, s32[1]{0:T(128)} %get-tuple-element.19.refs_0_, f32[2048,256]{1,0:T(8,128)S(1)} %get-tuple-element.20.refs_1_, bf16[16,128,128]{2,1,0:T(8,128)(2,1)S(1)} %all-to-all-done.refs_0_.refs_2_, ...), custom_call_target="tpu_custom_call" | custom-call | flops 4294967296 | bytes 4194304 | tf_op jit(solution)/shard_map/pallas_call | solution.py:277
  322.5 7.2 %all-to-all-start.3 = ((bf16[16,128,128]{2,1,0:T(8,128)(2,1)}), bf16[16,128,128]{2,1,0:T(8,128)(2,1)S(1)}, u32[]{:S(2)}, u32[]{:S(2)}) async-start(bf16[16,128,128]{2,1,0:T(8,128)(2,1)} %shard_map.71), calls=%async_computation.3 | async-start | bytes 1048576 | tf_op jit(solution)/shard_map/all_to_all | solution.py:392
  330.0 16.9 %all-to-all-done.3 = bf16[16,128,128]{2,1,0:T(8,128)(2,1)S(1)} async-done(((bf16[16,128,128]{2,1,0:T(8,128)(2,1)}), bf16[16,128,128]{2,1,0:T(8,128)(2,1)S(1)}, u32[]{:S(2)}, u32[]{:S(2)}) %all-to-all-start.3) | async-done | bytes 524320 | tf_op jit(solution)/shard_map/all_to_all | solution.py:392
  347.3 1.3 copy.9
  (32 shorter events, 3.1 us)
Async XLA Ops:
  2.4 9.3 %copy-start.5 = (bf16[1,2,128,2048]{3,2,1,0:T(8,128)(2,1)S(1)}, bf16[1,2,128,2048]{3,2,1,0:T(8,128)(2,1)}, u32[]{:S(2)}) copy-start(bf16[1,2,128,2048]{3,2,1,0:T(8,128)(2,1)} %param.7) | copy-start | bytes 3145732
  2.4 57.0 %all-to-all-start.2 = ((bf16[16,256,128]{2,1,0:T(8,128)(2,1)}), bf16[16,256,128]{2,1,0:T(8,128)(2,1)S(1)}, u32[]{:S(2)}, u32[]{:S(2)}) async-start(bf16[16,256,128]{2,1,0:T(8,128)(2,1)} %bitcast.11), calls=%async_computation.2 | async-start | bytes 2097152 | tf_op jit(solution)/shard_map/all_to_all | solution.py:392
  11.7 24.7 %collective-permute-start.1 = (bf16[2,128,2048]{2,1,0:T(8,128)(2,1)S(1)}, bf16[2,128,2048]{2,1,0:T(8,128)(2,1)S(1)}, u32[]{:S(2)}, u32[]{:S(2)}) collective-permute-start(bf16[2,128,2048]{2,1,0:T(8,128)(2,1)S(1)} %bitcast.20), channel_id=1, source_target_pairs={{0,128},{128,0},{1,129},{129,1},{2,130},{130,2},{3,131},{131,3},{4... | collective-permute-start | bytes 3145736 | tf_op jit(solution)/shard_map/ppermute | solution.py:388
  12.8 27.1 %copy-start.3 = (s32[2]{0:T(128)S(1)}, s32[2]{0:T(128)}, u32[]{:S(2)}) copy-start(s32[2]{0:T(128)} %keyframes_ref.11) | copy-start | bytes 28
  36.4 1.0 copy-start.6
  39.9 1.2 copy-start
  41.9 7.0 %collective-permute-start.2 = (bf16[2,16,32,128]{3,2,1,0:T(8,128)(2,1)S(1)}, bf16[2,16,32,128]{3,2,1,0:T(8,128)(2,1)S(1)}, u32[]{:S(2)}, u32[]{:S(2)}) collective-permute-start(bf16[2,16,32,128]{3,2,1,0:T(8,128)(2,1)S(1)} %get-tuple-element.16), channel_id=1, source_target_pairs={{0,2},{1,3},{2,4},{3,5},{4,6},{5,7},{6,0},{7,1},{8,10},{9,11},{10,... | collective-permute-start | bytes 786440 | tf_op jit(solution)/shard_map/ppermute | solution.py:397
  42.2 8.2 %collective-permute-start.3 = (bf16[2,16,32,128]{3,2,1,0:T(8,128)(2,1)S(1)}, bf16[2,16,32,128]{3,2,1,0:T(8,128)(2,1)S(1)}, u32[]{:S(2)}, u32[]{:S(2)}) collective-permute-start(bf16[2,16,32,128]{3,2,1,0:T(8,128)(2,1)S(1)} %get-tuple-element.17), channel_id=1, source_target_pairs={{0,4},{1,5},{2,6},{3,7},{4,0},{5,1},{6,2},{7,3},{8,12},{9,13},{10,... | collective-permute-start | bytes 786440 | tf_op jit(solution)/shard_map/ppermute | solution.py:397
  44.3 13.2 %collective-permute-start.4 = (bf16[2,16,32,128]{3,2,1,0:T(8,128)(2,1)S(1)}, bf16[2,16,32,128]{3,2,1,0:T(8,128)(2,1)S(1)}, u32[]{:S(2)}, u32[]{:S(2)}) collective-permute-start(bf16[2,16,32,128]{3,2,1,0:T(8,128)(2,1)S(1)} %get-tuple-element.18), channel_id=1, source_target_pairs={{0,6},{1,7},{2,0},{3,1},{4,2},{5,3},{6,4},{7,5},{8,14},{9,15},{10,... | collective-permute-start | bytes 786440 | tf_op jit(solution)/shard_map/ppermute | solution.py:397
  58.3 1.1 copy-start.1
  59.4 7.2 %copy-start.4 = (bf16[1,2,128,2048]{3,2,1,0:T(8,128)(2,1)S(1)}, bf16[1,2,128,2048]{3,2,1,0:T(8,128)(2,1)}, u32[]{:S(2)}) copy-start(bf16[1,2,128,2048]{3,2,1,0:T(8,128)(2,1)} %param.6) | copy-start | bytes 3145732
  59.4 40.4 %all-to-all-start.1 = ((bf16[16,320,128]{2,1,0:T(8,128)(2,1)}), bf16[16,320,128]{2,1,0:T(8,128)(2,1)S(1)}, u32[]{:S(2)}, u32[]{:S(2)}) async-start(bf16[16,320,128]{2,1,0:T(8,128)(2,1)} %copy-done.1), calls=%async_computation.1 | async-start | bytes 2621440 | tf_op jit(solution)/shard_map/all_to_all | solution.py:392
  66.5 24.8 %collective-permute-start = (bf16[2,128,2048]{2,1,0:T(8,128)(2,1)S(1)}, bf16[2,128,2048]{2,1,0:T(8,128)(2,1)}, u32[]{:S(2)}, u32[]{:S(2)}) collective-permute-start(bf16[2,128,2048]{2,1,0:T(8,128)(2,1)S(1)} %bitcast.17), channel_id=1, source_target_pairs={{0,128},{128,0},{1,129},{129,1},{2,130},{130,2},{3,131},{131,3},{4... | collective-permute-start | bytes 3145736 | tf_op jit(solution)/shard_map/ppermute | solution.py:388
  99.8 32.2 %all-to-all-start.4 = ((bf16[16,128,128]{2,1,0:T(8,128)(2,1)}), bf16[16,128,128]{2,1,0:T(8,128)(2,1)S(1)}, u32[]{:S(2)}, u32[]{:S(2)}) async-start(bf16[16,128,128]{2,1,0:T(8,128)(2,1)} %get-tuple-element.24), calls=%async_computation.4 | async-start | bytes 1048576 | tf_op jit(solution)/shard_map/all_to_all | solution.py:392
  104.3 7.8 %collective-permute-start.9 = (bf16[2,16,32,128]{3,2,1,0:T(8,128)(2,1)S(1)}, bf16[2,16,32,128]{3,2,1,0:T(8,128)(2,1)S(1)}, u32[]{:S(2)}, u32[]{:S(2)}) collective-permute-start(bf16[2,16,32,128]{3,2,1,0:T(8,128)(2,1)S(1)} %get-tuple-element.21), channel_id=1, source_target_pairs={{0,2},{1,3},{2,4},{3,5},{4,6},{5,7},{6,0},{7,1},{8,10},{9,11},{10,... | collective-permute-start | bytes 786440 | tf_op jit(solution)/shard_map/ppermute | solution.py:397
  105.1 9.0 %collective-permute-start.10 = (bf16[2,16,32,128]{3,2,1,0:T(8,128)(2,1)S(1)}, bf16[2,16,32,128]{3,2,1,0:T(8,128)(2,1)S(1)}, u32[]{:S(2)}, u32[]{:S(2)}) collective-permute-start(bf16[2,16,32,128]{3,2,1,0:T(8,128)(2,1)S(1)} %get-tuple-element.22), channel_id=1, source_target_pairs={{0,4},{1,5},{2,6},{3,7},{4,0},{5,1},{6,2},{7,3},{8,12},{9,13},{10,... | collective-permute-start | bytes 786440 | tf_op jit(solution)/shard_map/ppermute | solution.py:397
  106.9 13.6 %collective-permute-start.11 = (bf16[2,16,32,128]{3,2,1,0:T(8,128)(2,1)S(1)}, bf16[2,16,32,128]{3,2,1,0:T(8,128)(2,1)S(1)}, u32[]{:S(2)}, u32[]{:S(2)}) collective-permute-start(bf16[2,16,32,128]{3,2,1,0:T(8,128)(2,1)S(1)} %get-tuple-element.23), channel_id=1, source_target_pairs={{0,6},{1,7},{2,0},{3,1},{4,2},{5,3},{6,4},{7,5},{8,14},{9,15},{10,... | collective-permute-start | bytes 786440 | tf_op jit(solution)/shard_map/ppermute | solution.py:397
  121.3 9.0 %collective-permute-start.12 = (bf16[2,16,32,128]{3,2,1,0:T(8,128)(2,1)S(1)}, bf16[2,16,32,128]{3,2,1,0:T(8,128)(2,1)S(1)}, u32[]{:S(2)}, u32[]{:S(2)}) collective-permute-start(bf16[2,16,32,128]{3,2,1,0:T(8,128)(2,1)S(1)} %shard_map.69.mine_ref), channel_id=1, source_target_pairs={{0,1},{1,0},{2,3},{3,2},{4,5},{5,4},{6,7},{7,6},{8,9},{9,8},{10,11... | collective-permute-start | bytes 786440 | tf_op jit(solution)/shard_map/ppermute | solution.py:402
  122.2 23.1 %collective-permute-start.5 = (bf16[16,64,128]{2,1,0:T(8,128)(2,1)}, bf16[16,64,128]{2,1,0:T(8,128)(2,1)}, u32[]{:S(2)}, u32[]{:S(2)}) collective-permute-start(bf16[16,64,128]{2,1,0:T(8,128)(2,1)} %slice.4), channel_id=1, source_target_pairs={{0,1},{1,0},{2,3},{3,2},{4,5},{5,4},{6,7},{7,6},{8,9},{9,8},{10,11... | collective-permute-start | bytes 786440 | tf_op jit(solution)/shard_map/ppermute | solution.py:402
  131.9 16.2 %collective-permute-start.15 = (bf16[2,16,32,128]{3,2,1,0:T(8,128)(2,1)}, bf16[2,16,32,128]{3,2,1,0:T(8,128)(2,1)}, u32[]{:S(2)}, u32[]{:S(2)}) collective-permute-start(bf16[2,16,32,128]{3,2,1,0:T(8,128)(2,1)} %shard_map.70.refs_9_.refs_7_), channel_id=1, source_target_pairs={{0,6},{1,7},{2,0},{3,1},{4,2},{5,3},{6,4},{7,5},{8,14},{9,15},{10,... | collective-permute-start | bytes 786440 | tf_op jit(solution)/shard_map/ppermute | solution.py:397
  132.0 18.1 %copy-start.7 = (s32[16,2]{0,1:T(2,128)S(1)}, s32[16,2]{0,1:T(2,128)}, u32[]{:S(2)}) copy-start(s32[16,2]{0,1:T(2,128)} %param.11) | copy-start | bytes 388
  132.0 121.6 %all-to-all-start = ((bf16[16,128,128]{2,1,0:T(8,128)(2,1)}), bf16[16,128,128]{2,1,0:T(8,128)(2,1)S(1)}, u32[]{:S(2)}, u32[]{:S(2)}) async-start(bf16[16,128,128]{2,1,0:T(8,128)(2,1)} %get-tuple-element.15), calls=%async_computation | async-start | bytes 1048576 | tf_op jit(solution)/shard_map/all_to_all | solution.py:392
  142.0 9.5 %collective-permute-start.14 = (bf16[2,16,32,128]{3,2,1,0:T(8,128)(2,1)}, bf16[2,16,32,128]{3,2,1,0:T(8,128)(2,1)}, u32[]{:S(2)}, u32[]{:S(2)}) collective-permute-start(bf16[2,16,32,128]{3,2,1,0:T(8,128)(2,1)} %shard_map.70.refs_9_.refs_7_), channel_id=1, source_target_pairs={{0,4},{1,5},{2,6},{3,7},{4,0},{5,1},{6,2},{7,3},{8,12},{9,13},{10,... | collective-permute-start | bytes 786440 | tf_op jit(solution)/shard_map/ppermute | solution.py:397
  143.0 13.9 %collective-permute-start.13 = (bf16[2,16,32,128]{3,2,1,0:T(8,128)(2,1)}, bf16[2,16,32,128]{3,2,1,0:T(8,128)(2,1)}, u32[]{:S(2)}, u32[]{:S(2)}) collective-permute-start(bf16[2,16,32,128]{3,2,1,0:T(8,128)(2,1)} %shard_map.70.refs_9_.refs_7_), channel_id=1, source_target_pairs={{0,2},{1,3},{2,4},{3,5},{4,6},{5,7},{6,0},{7,1},{8,10},{9,11},{10,... | collective-permute-start | bytes 786440 | tf_op jit(solution)/shard_map/ppermute | solution.py:397
  146.6 11.2 %collective-permute-start.8 = (bf16[2,16,32,128]{3,2,1,0:T(8,128)(2,1)}, bf16[2,16,32,128]{3,2,1,0:T(8,128)(2,1)}, u32[]{:S(2)}, u32[]{:S(2)}) collective-permute-start(bf16[2,16,32,128]{3,2,1,0:T(8,128)(2,1)} %shard_map.67.refs_5_.refs_3_), channel_id=1, source_target_pairs={{0,6},{1,7},{2,0},{3,1},{4,2},{5,3},{6,4},{7,5},{8,14},{9,15},{10,... | collective-permute-start | bytes 786440 | tf_op jit(solution)/shard_map/ppermute | solution.py:397
  146.7 16.0 %collective-permute-start.7 = (bf16[2,16,32,128]{3,2,1,0:T(8,128)(2,1)}, bf16[2,16,32,128]{3,2,1,0:T(8,128)(2,1)}, u32[]{:S(2)}, u32[]{:S(2)}) collective-permute-start(bf16[2,16,32,128]{3,2,1,0:T(8,128)(2,1)} %shard_map.67.refs_5_.refs_3_), channel_id=1, source_target_pairs={{0,4},{1,5},{2,6},{3,7},{4,0},{5,1},{6,2},{7,3},{8,12},{9,13},{10,... | collective-permute-start | bytes 786440 | tf_op jit(solution)/shard_map/ppermute | solution.py:397
  148.1 20.1 %collective-permute-start.6 = (bf16[2,16,32,128]{3,2,1,0:T(8,128)(2,1)}, bf16[2,16,32,128]{3,2,1,0:T(8,128)(2,1)}, u32[]{:S(2)}, u32[]{:S(2)}) collective-permute-start(bf16[2,16,32,128]{3,2,1,0:T(8,128)(2,1)} %shard_map.67.refs_5_.refs_3_), channel_id=1, source_target_pairs={{0,2},{1,3},{2,4},{3,5},{4,6},{5,7},{6,0},{7,1},{8,10},{9,11},{10,... | collective-permute-start | bytes 786440 | tf_op jit(solution)/shard_map/ppermute | solution.py:397
  252.8 0.8 copy-start.2
  253.6 68.9 %all-to-all-start.5 = ((bf16[16,128,128]{2,1,0:T(8,128)(2,1)}), bf16[16,128,128]{2,1,0:T(8,128)(2,1)S(1)}, u32[]{:S(2)}, u32[]{:S(2)}) async-start(bf16[16,128,128]{2,1,0:T(8,128)(2,1)} %copy-done.2), calls=%async_computation.5 | async-start | bytes 1048576 | tf_op jit(solution)/shard_map/all_to_all | solution.py:392
  322.5 24.4 %all-to-all-start.3 = ((bf16[16,128,128]{2,1,0:T(8,128)(2,1)}), bf16[16,128,128]{2,1,0:T(8,128)(2,1)S(1)}, u32[]{:S(2)}, u32[]{:S(2)}) async-start(bf16[16,128,128]{2,1,0:T(8,128)(2,1)} %shard_map.71), calls=%async_computation.3 | async-start | bytes 1048576 | tf_op jit(solution)/shard_map/all_to_all | solution.py:392

commit v5 on v4

--- a/solution.py
+++ b/solution.py
@@ -21,34 +21,28 @@
 SMEM = pl.BlockSpec(memory_space=pltpu.SMEM)
 
 
-def blend_kernel(strength_ref, own_ref, partner_ref, *out_refs, heads):
+def blend_kernel(strength_ref, own_ref, partner_ref, out_ref, *, heads):
     first = pl.program_id(0) * heads
     for head in range(heads):
         share = strength_ref[0, first + head]
         lanes = slice(head * HEAD, (head + 1) * HEAD)
-        mixed = (
-            (1.0 - share) * own_ref[:, :, lanes].astype(F32)
-            + share * partner_ref[:, :, lanes].astype(F32)
-        ).astype(BF16)
-        if len(out_refs) == 1:
-            out_refs[0][head] = mixed.reshape(-1, HEAD)
-        else:
-            for frame, out_ref in enumerate(out_refs):
-                out_ref[head] = mixed[frame]
-
-
-def blend_heads(strength, own, partner, split, steps=2):
+        mixed = (1.0 - share) * own_ref[:, :, lanes].astype(F32) + share * partner_ref[
+            :, :, lanes
+        ].astype(F32)
+        out_ref[head] = mixed.astype(BF16).reshape(-1, HEAD)
+
+
+def blend_heads(strength, own, partner, steps=2):
     frames, rows, width = own.shape
     heads = width // HEAD
     group = heads // steps
-    outs, count = (frames, rows) if split else (1, frames * rows)
     block = pl.BlockSpec((frames, rows, group * HEAD), lambda h: (0, 0, h))
     return pl.pallas_call(
         functools.partial(blend_kernel, heads=group),
         grid=(steps,),
         in_specs=[SMEM, block, block],
-        out_specs=[pl.BlockSpec((group, count, HEAD), lambda h: (h, 0, 0))] * outs,
-        out_shape=[jax.ShapeDtypeStruct((heads, count, HEAD), BF16)] * outs,
+        out_specs=pl.BlockSpec((group, frames * rows, HEAD), lambda h: (h, 0, 0)),
+        out_shape=jax.ShapeDtypeStruct((heads, frames * rows, HEAD), BF16),
         cost_estimate=pl.CostEstimate(
             flops=3 * own.size, bytes_accessed=6 * own.size, transcendentals=0
         ),
@@ -168,7 +162,9 @@
         def _():
             unsafe[0] = 1
 
-    query_copy = pltpu.make_async_copy(query_in, query_ref, sem.at[0])
+    query_copy = pltpu.make_async_copy(
+        query_in.at[:, pl.ds(frame * rows, rows)], query_ref, sem.at[0]
+    )
     query_copy.start()
     if mode == "more":
         acc_copy = pltpu.make_async_copy(acc_in, acc, sem.at[1])
@@ -254,18 +250,18 @@
     )
 
 
-def attend(mode, frame, valid, query, key, value, key_extra=(), value_extra=(), own=(), cuts=4):
-    blocks, rows, _ = query.shape
+def attend(mode, frame, rows, valid, query, key, value, key_extra=(), value_extra=(), own=(), cuts=4):
+    blocks = query.shape[0]
     total = blocks * rows
     parts = valid.shape[0]
     pieces = len(key_extra)
     acc = jax.ShapeDtypeStruct((total, 2 * HEAD), F32)
     flag = jax.ShapeDtypeStruct((1,), jnp.int32)
-    out = jax.ShapeDtypeStruct((blocks, rows, HEAD), BF16)
+    out = pltpu.HBM((blocks, rows, HEAD), BF16)
     kept = pltpu.VMEM((parts, cuts, blocks, rows // cuts, HEAD), BF16)
     sems = pltpu.SemaphoreType.DMA((parts, cuts))
     scratch = [
-        kept, kept, pltpu.VMEM(query.shape, BF16), pltpu.VMEM((rows, HEAD), F32),
+        kept, kept, pltpu.VMEM(out.shape, BF16), pltpu.VMEM((rows, HEAD), F32),
         sems, sems, pltpu.SemaphoreType.DMA((2,)),
     ]
     if mode == "own":
@@ -315,17 +311,10 @@
     run_copies(copies)
 
 
-def pick_x_kernel(place_ref, keyframes_ref, source_ref, *refs, shape, join):
+def pick_x_kernel(place_ref, keyframes_ref, source_ref, *refs, shape):
     *got_refs, out_ref, sem = refs
     x = place_ref[0] // 2
-    extras, _, cut_rows = got_refs[0].shape[:3]
-    kept = source_ref.shape[1]
-    if join:
-        targets = [out_ref.at[:, pl.ds(kept + j * cut_rows, cut_rows)] for j in range(extras)]
-        all_rows = pltpu.make_async_copy(source_ref, out_ref.at[:, pl.ds(0, kept)], sem.at[extras])
-        all_rows.start()
-    else:
-        targets = [out_ref.at[j] for j in range(extras)]
+    extras = out_ref.shape[0]
     for j in range(extras):
         keyframe = keyframes_ref[j]
         step = lax.rem(x - keyframe // (2 * shape[0]) + shape[2], shape[2])
@@ -333,29 +322,23 @@
         @pl.when(step == 0)
         def _():
             rows = piece_rows(keyframe, x, shape)
-            pltpu.make_async_copy(source_ref.at[:, rows], targets[j], sem.at[j]).start()
+            pltpu.make_async_copy(source_ref.at[:, rows], out_ref.at[j], sem.at[j]).start()
 
         for which, got_ref in enumerate(got_refs, 1):
 
             @pl.when(step == which)
             def _():
-                pltpu.make_async_copy(got_ref.at[j], targets[j], sem.at[j]).start()
+                pltpu.make_async_copy(got_ref.at[j], out_ref.at[j], sem.at[j]).start()
 
     for j in range(extras):
-        pltpu.make_async_copy(got_refs[0].at[j], targets[j], sem.at[j]).wait()
-    if join:
-        all_rows.wait()
-
-
-def pick_y_kernel(place_ref, keyframes_ref, mine_ref, other_ref, out_ref, sem, *, shape, kept):
+        pltpu.make_async_copy(got_refs[0].at[j], out_ref.at[j], sem.at[j]).wait()
+
+
+def pick_y_kernel(place_ref, keyframes_ref, mine_ref, other_ref, out_ref, sem, *, shape):
     y = lax.rem(place_ref[0], 2)
-    extras, _, cut_rows = out_ref.shape[:3]
+    extras = out_ref.shape[0]
     for j in range(extras):
-        if kept is None:
-            mine, other = mine_ref.at[j], other_ref.at[j]
-        else:
-            mine = mine_ref.at[:, pl.ds(kept + j * cut_rows, cut_rows)]
-            other = other_ref.at[:, pl.ds(j * cut_rows, cut_rows)]
+        mine, other = mine_ref.at[j], other_ref.at[j]
         same = lax.rem(keyframes_ref[j] // shape[0], 2) == y
 
         @pl.when(same)
@@ -402,30 +385,25 @@
     return lax.ppermute(value, "mp", [(m, m ^ 1) for m in range(size)])
 
 
-def spread_along_x(place, keyframes, source, shape, join):
-    blocks = source.shape[0]
-    extras, cut_rows = keyframes.shape[0], shape[1] // shape[2]
-    piece = jax.ShapeDtypeStruct((extras, blocks, cut_rows, HEAD), BF16)
+def spread_along_x(place, keyframes, source, shape):
+    piece = (keyframes.shape[0], source.shape[0], shape[1] // shape[2], HEAD)
+    piece = jax.ShapeDtypeStruct(piece, BF16)
     cuts = move_call(
         functools.partial(cut_kernel, shape=shape),
         [piece] * (shape[2] - 1), place, keyframes, source,
     )
     got = [shift_x(cut, step) for step, cut in enumerate(cuts, 1)]
-    if join:
-        piece = jax.ShapeDtypeStruct((blocks, source.shape[1] + extras * cut_rows, HEAD), BF16)
     return move_call(
-        functools.partial(pick_x_kernel, shape=shape, join=join),
+        functools.partial(pick_x_kernel, shape=shape),
         [piece], place, keyframes, source, *got,
     )[0]
 
 
-def spread_from_x(place, keyframes, mine, shape, kept):
-    extras, cut_rows = keyframes.shape[0], shape[1] // shape[2]
-    other = flip_y(mine if kept is None else mine[:, kept:])
-    blocks = mine.shape[1] if kept is None else mine.shape[0]
+def spread_from_x(place, keyframes, mine, shape):
+    other = flip_y(mine)
     (mine,) = move_call(
-        functools.partial(pick_y_kernel, shape=shape, kept=kept),
-        [jax.ShapeDtypeStruct((extras, blocks, cut_rows, HEAD), BF16)], place, keyframes, mine, other,
+        functools.partial(pick_y_kernel, shape=shape),
+        [jax.ShapeDtypeStruct(mine.shape, BF16)], place, keyframes, mine, other,
     )
     return [mine] + [shift_x(mine, step) for step in range(1, shape[2])]
 
@@ -440,27 +418,28 @@
 
     value_rows = split_heads(values).reshape(-1, frames * rows, HEAD)
     value_heads = to_heads(value_rows)
-    value_mine = spread_along_x(place, keyframes, value_heads, shape, False)
-    value_extra = spread_from_x(place, keyframes, value_mine, shape, None)
-
-    (key_rows,) = blend_heads(inject, keys, partner_keys, False)
-    key_rows = spread_along_x(place, keyframes, key_rows, shape, True)
+    value_mine = spread_along_x(place, keyframes, value_heads, shape)
+    value_extra = spread_from_x(place, keyframes, value_mine, shape)
+
+    key_rows = blend_heads(inject, keys, partner_keys)
     key_heads = to_heads(key_rows)
-    key_extra = spread_from_x(place, keyframes, key_heads, shape, frames * rows)
-
-    query_rows = blend_heads(inject, queries, partner_queries, True)
+    key_mine = spread_along_x(place, keyframes, key_heads, shape)
+    key_extra = spread_from_x(place, keyframes, key_mine, shape)
+
+    query_rows = blend_heads(inject, queries, partner_queries)
+    query_heads = to_heads(query_rows)
     outs = []
     always = jnp.ones((1,), jnp.int32)
     for f in range(frames):
-        query = to_heads(query_rows[f])
         masks = lax.dynamic_index_in_dim(key_mask, place[0] * frames + f, 0, keepdims=False)
         valid = jnp.concatenate([always, masks])
+        heads = (query_heads, key_heads, value_heads)
         extra = (key_extra, value_extra)
         if f == 0:
-            own = attend("own", f, always, query, key_heads, value_heads)
-            out = attend("more", f, valid, query, key_heads, value_heads, *extra, own)
+            own = attend("own", f, rows, always, *heads)
+            out = attend("more", f, rows, valid, *heads, *extra, own)
         else:
-            out = attend("all", f, valid, query, key_heads, value_heads, *extra)
+            out = attend("all", f, rows, valid, *heads, *extra)
         back = to_heads(out)
         outs.append(back.transpose(1, 0, 2).reshape(rows, -1))
     return jnp.stack(outs)[None]

time: 350 us -> 319 us (0.911)
  the two profiles are of different devices: /device:TPU:23 before, /device:TPU:31 now
where the time goes in v5:
time: 319 us
  Pallas kernels  161 us (50%)
  waiting for transfers between devices  103 us (32%)
  starting transfers between devices  51 us (16%)
    pallas_call x3, Pallas kernels, attend(): pl.pallas_call(functools.partial(attend_kernel, frame=frame, pieces=piece...  147 us
    ppermute x2, waiting for transfers between devices, swap_branch(): return lax.ppermute(value, 'branch', [(0, 1), (1, 0)])  48.5 us
    all_to_all x5, starting transfers between devices, to_heads(): return lax.all_to_all(value, 'seq', split_axis=0, concat_axis=0, tiled=True)  38.1 us
    ppermute x12, waiting for transfers between devices, shift_x(): lax.ppermute(value, 'mp', [(m, (m + 2 * step) % size) for m in range(size)])  33.9 us
    all_to_all x5, waiting for transfers between devices, to_heads(): return lax.all_to_all(value, 'seq', split_axis=0, concat_axis=0, tiled=True)  17.1 us
    ppermute x12, starting transfers between devices, shift_x(): lax.ppermute(value, 'mp', [(m, (m + 2 * step) % size) for m in range(size)])  9.72 us
    pallas_call x6, Pallas kernels, move_call(): pl.pallas_call(kernel, grid=(1,), in_specs=[SMEM, SMEM] + [ANY] * len(arr...  6.45 us
  transfers between devices with their start and end apart: 21, of which 15 were waited for; matrix products, arithmetic and copies ran while one was open for 1% of the time, Pallas kernels for 31%

profile of v5, /device:TPU:31, one launch (start us, length us, event | category | flops | bytes accessed | tf_op | source)
XLA Modules:
  0.0 318.7 jit_solution(7093132769056918666)
XLA Ops:
  0.0 2.5 split_heads.1
  2.5 9.2 %all-to-all-start.2 = ((bf16[16,256,128]{2,1,0:T(8,128)(2,1)}), bf16[16,256,128]{2,1,0:T(8,128)(2,1)S(1)}, u32[]{:S(2)}, u32[]{:S(2)}) async-start(bf16[16,256,128]{2,1,0:T(8,128)(2,1)} %bitcast.11), calls=%async_computation.2 | async-start | bytes 2097152 | tf_op jit(solution)/shard_map/all_to_all | solution.py:375
  11.6 0.6 collective-permute-start.1
  12.2 24.3 %collective-permute-done.1.partner_ref = bf16[2,128,2048]{2,1,0:T(8,128)(2,1)} collective-permute-done((bf16[2,128,2048]{2,1,0:T(8,128)(2,1)S(1)}, bf16[2,128,2048]{2,1,0:T(8,128)(2,1)}, u32[]{:S(2)}, u32[]{:S(2)}) %collective-permute-start.1) | collective-permute-done | bytes 1048608 | tf_op jit(solution)/shard_map/ppermute | solution.py:371
  36.5 2.6 blend.3
  39.0 0.6 all-to-all-done.2.refs_2_.source_ref.refs_4_
  39.6 7.2 %all-to-all-start.1 = ((bf16[16,256,128]{2,1,0:T(8,128)(2,1)}), bf16[16,256,128]{2,1,0:T(8,128)(2,1)S(1)}, u32[]{:S(2)}, u32[]{:S(2)}) async-start(bf16[16,256,128]{2,1,0:T(8,128)(2,1)} %blend.3), calls=%async_computation.1 | async-start | bytes 2097152 | tf_op jit(solution)/shard_map/all_to_all | solution.py:375
  46.8 0.6 collective-permute-start
  47.4 24.3 %collective-permute-done.partner_ref = bf16[2,128,2048]{2,1,0:T(8,128)(2,1)} collective-permute-done((bf16[2,128,2048]{2,1,0:T(8,128)(2,1)S(1)}, bf16[2,128,2048]{2,1,0:T(8,128)(2,1)}, u32[]{:S(2)}, u32[]{:S(2)}) %collective-permute-start) | collective-permute-done | bytes 1048608 | tf_op jit(solution)/shard_map/ppermute | solution.py:371
  71.6 2.5 blend.2
  74.2 0.6 all-to-all-done.1.refs_1_.source_ref.refs_3_
  74.8 7.2 %all-to-all-start = ((bf16[16,256,128]{2,1,0:T(8,128)(2,1)}), bf16[16,256,128]{2,1,0:T(8,128)(2,1)S(1)}, u32[]{:S(2)}, u32[]{:S(2)}) async-start(bf16[16,256,128]{2,1,0:T(8,128)(2,1)} %blend.2), calls=%async_computation | async-start | bytes 2097152 | tf_op jit(solution)/shard_map/all_to_all | solution.py:375
  82.0 0.8 shard_map.68
  82.7 1.2 collective-permute-start.10
  83.9 2.7 collective-permute-start.9
  86.6 0.7 shard_map.65
  87.4 0.7 collective-permute-start.2
  88.0 0.1 collective-permute-start.3
  88.2 3.9 %collective-permute-done.10.refs_1_ = bf16[2,16,32,128]{3,2,1,0:T(8,128)(2,1)S(1)} collective-permute-done((bf16[2,16,32,128]{3,2,1,0:T(8,128)(2,1)S(1)}, bf16[2,16,32,128]{3,2,1,0:T(8,128)(2,1)S(1)}, u32[]{:S(2)}, u32[]{:S(2)}) %collective-permute-start.10) | collective-permute-done | bytes 262176 | tf_op jit(solution)/shard_map/ppermute | solution.py:380
  92.1 0.5 collective-permute-start.4
  92.7 6.0 %collective-permute-done.11.refs_2_ = bf16[2,16,32,128]{3,2,1,0:T(8,128)(2,1)S(1)} collective-permute-done((bf16[2,16,32,128]{3,2,1,0:T(8,128)(2,1)S(1)}, bf16[2,16,32,128]{3,2,1,0:T(8,128)(2,1)S(1)}, u32[]{:S(2)}, u32[]{:S(2)}) %collective-permute-start.11) | collective-permute-done | bytes 262176 | tf_op jit(solution)/shard_map/ppermute | solution.py:380
  98.6 0.8 shard_map.69.mine_ref
  99.4 1.0 collective-permute-start.12
  100.5 0.6 collective-permute-done.2.refs_0_
  101.1 2.3 collective-permute-done.3.refs_1_
  103.4 6.0 %collective-permute-done.4.refs_2_ = bf16[2,16,32,128]{3,2,1,0:T(8,128)(2,1)S(1)} collective-permute-done((bf16[2,16,32,128]{3,2,1,0:T(8,128)(2,1)S(1)}, bf16[2,16,32,128]{3,2,1,0:T(8,128)(2,1)S(1)}, u32[]{:S(2)}, u32[]{:S(2)}) %collective-permute-start.4) | collective-permute-done | bytes 262176 | tf_op jit(solution)/shard_map/ppermute | solution.py:380
  109.4 0.8 shard_map.66.mine_ref
  110.2 1.0 collective-permute-start.5
  111.3 1.7 shard_map.70.refs_9_.refs_7_
  113.1 0.2 dynamic-slice_reduce_fusion.1
  113.3 2.1 collective-permute-start.14
  115.5 3.9 %collective-permute-done.5.other_ref = bf16[2,16,32,128]{3,2,1,0:T(8,128)(2,1)} collective-permute-done((bf16[2,16,32,128]{3,2,1,0:T(8,128)(2,1)S(1)}, bf16[2,16,32,128]{3,2,1,0:T(8,128)(2,1)}, u32[]{:S(2)}, u32[]{:S(2)}) %collective-permute-start.5) | collective-permute-done | bytes 262176 | tf_op jit(solution)/shard_map/ppermute | solution.py:385
  119.3 1.6 shard_map.67.refs_5_.refs_3_
  121.1 1.5 collective-permute-start.7
  122.6 0.6 collective-permute-start.8
  123.3 1.8 shard_map.64
  125.1 5.5 %collective-permute-done.15.refs_12_.refs_10_ = bf16[2,16,32,128]{3,2,1,0:T(8,128)(2,1)} collective-permute-done((bf16[2,16,32,128]{3,2,1,0:T(8,128)(2,1)}, bf16[2,16,32,128]{3,2,1,0:T(8,128)(2,1)}, u32[]{:S(2)}, u32[]{:S(2)}) %collective-permute-start.15) | collective-permute-done | bytes 262176 | tf_op jit(solution)/shard_map/ppermute | solution.py:380
  130.7 1.7 collective-permute-done.6.refs_6_.refs_4_
  132.4 0.6 collective-permute-done.7.refs_7_.refs_5_
  133.0 7.2 %collective-permute-done.8.refs_8_.refs_6_ = bf16[2,16,32,128]{3,2,1,0:T(8,128)(2,1)} collective-permute-done((bf16[2,16,32,128]{3,2,1,0:T(8,128)(2,1)}, bf16[2,16,32,128]{3,2,1,0:T(8,128)(2,1)}, u32[]{:S(2)}, u32[]{:S(2)}) %collective-permute-start.8) | collective-permute-done | bytes 262176 | tf_op jit(solution)/shard_map/ppermute | solution.py:380
  140.2 59.3 %shard_map.71 = bf16[16,128,128]{2,1,0:T(8,128)(2,1)} custom-call(s32[3]{0:T(128)S(1)} %pad_add_fusion.1.valid_ref, s32[1]{0:T(128)} %get-tuple-element.13.refs_0_, f32[2048,256]{1,0:T(8,128)S(1)} %get-tuple-element.14.refs_1_, bf16[16,256,128]{2,1,0:T(8,128)(2,1)S(1)} %all-to-all-done.refs_0_.refs_2_, ...), custom_call_target="tpu_custom_call" | custom-call | flops 4294967296 | bytes 4194304 | tf_op jit(solution)/shard_map/pallas_call | solution.py:273
  199.5 7.4 %all-to-all-start.3 = ((bf16[16,128,128]{2,1,0:T(8,128)(2,1)}), bf16[16,128,128]{2,1,0:T(8,128)(2,1)}, u32[]{:S(2)}, u32[]{:S(2)}) async-start(bf16[16,128,128]{2,1,0:T(8,128)(2,1)} %shard_map.71), calls=%async_computation.3 | async-start | bytes 1048576 | tf_op jit(solution)/shard_map/all_to_all | solution.py:375
  206.9 85.6 %shard_map.72 = bf16[16,128,128]{2,1,0:T(8,128)(2,1)} custom-call(s32[3]{0:T(128)S(1)} %pad_add_fusion.valid_ref, bf16[16,256,128]{2,1,0:T(8,128)(2,1)S(1)} %all-to-all-done.refs_0_.refs_2_, bf16[16,256,128]{2,1,0:T(8,128)(2,1)S(1)} %all-to-all-done.1.refs_1_.source_ref.refs_3_, bf16[16,256,128]{2,1,0:T(8,128)(2,1)S(1)} %all-to-all-done.2.refs_2_.source_ref.refs_4_, ...), custom_call_target="tpu_custom_call" | custom-call | flops 6442450944 | bytes 4194304 | tf_op jit(solution)/shard_map/pallas_call | solution.py:273
  292.6 7.2 %all-to-all-start.4 = ((bf16[16,128,128]{2,1,0:T(8,128)(2,1)}), bf16[16,128,128]{2,1,0:T(8,128)(2,1)S(1)}, u32[]{:S(2)}, u32[]{:S(2)}) async-start(bf16[16,128,128]{2,1,0:T(8,128)(2,1)} %shard_map.72), calls=%async_computation.4 | async-start | bytes 1048576 | tf_op jit(solution)/shard_map/all_to_all | solution.py:375
  299.8 1.3 copy.7
  301.1 15.9 %all-to-all-done.4 = bf16[16,128,128]{2,1,0:T(8,128)(2,1)S(1)} async-done(((bf16[16,128,128]{2,1,0:T(8,128)(2,1)}), bf16[16,128,128]{2,1,0:T(8,128)(2,1)S(1)}, u32[]{:S(2)}, u32[]{:S(2)}) %all-to-all-start.4) | async-done | bytes 524320 | tf_op jit(solution)/shard_map/all_to_all | solution.py:375
  317.0 0.3 copy.8
  317.4 1.3 copy.9
  (21 shorter events, 0.5 us)
Async XLA Ops:
  0.0 11.6 %copy-start.1 = (bf16[1,2,128,2048]{3,2,1,0:T(8,128)(2,1)S(1)}, bf16[1,2,128,2048]{3,2,1,0:T(8,128)(2,1)}, u32[]{:S(2)}) copy-start(bf16[1,2,128,2048]{3,2,1,0:T(8,128)(2,1)} %param.7) | copy-start | bytes 3145732
  2.5 37.2 %all-to-all-start.2 = ((bf16[16,256,128]{2,1,0:T(8,128)(2,1)}), bf16[16,256,128]{2,1,0:T(8,128)(2,1)S(1)}, u32[]{:S(2)}, u32[]{:S(2)}) async-start(bf16[16,256,128]{2,1,0:T(8,128)(2,1)} %bitcast.11), calls=%async_computation.2 | async-start | bytes 2097152 | tf_op jit(solution)/shard_map/all_to_all | solution.py:375
  11.6 35.2 %copy-start.2 = (bf16[1,2,128,2048]{3,2,1,0:T(8,128)(2,1)S(1)}, bf16[1,2,128,2048]{3,2,1,0:T(8,128)(2,1)}, u32[]{:S(2)}) copy-start(bf16[1,2,128,2048]{3,2,1,0:T(8,128)(2,1)} %param.6) | copy-start | bytes 3145732
  11.6 24.8 %collective-permute-start.1 = (bf16[2,128,2048]{2,1,0:T(8,128)(2,1)S(1)}, bf16[2,128,2048]{2,1,0:T(8,128)(2,1)}, u32[]{:S(2)}, u32[]{:S(2)}) collective-permute-start(bf16[2,128,2048]{2,1,0:T(8,128)(2,1)S(1)} %bitcast.17), channel_id=1, source_target_pairs={{0,128},{128,0},{1,129},{129,1},{2,130},{130,2},{3,131},{131,3},{4... | collective-permute-start | bytes 3145736 | tf_op jit(solution)/shard_map/ppermute | solution.py:371
  39.6 35.2 %all-to-all-start.1 = ((bf16[16,256,128]{2,1,0:T(8,128)(2,1)}), bf16[16,256,128]{2,1,0:T(8,128)(2,1)S(1)}, u32[]{:S(2)}, u32[]{:S(2)}) async-start(bf16[16,256,128]{2,1,0:T(8,128)(2,1)} %blend.3), calls=%async_computation.1 | async-start | bytes 2097152 | tf_op jit(solution)/shard_map/all_to_all | solution.py:375
  46.8 35.1 %copy-start = (s32[2]{0:T(128)S(1)}, s32[2]{0:T(128)}, u32[]{:S(2)}) copy-start(s32[2]{0:T(128)} %keyframes_ref.11) | copy-start | bytes 28
  46.8 24.8 %collective-permute-start = (bf16[2,128,2048]{2,1,0:T(8,128)(2,1)S(1)}, bf16[2,128,2048]{2,1,0:T(8,128)(2,1)}, u32[]{:S(2)}, u32[]{:S(2)}) collective-permute-start(bf16[2,128,2048]{2,1,0:T(8,128)(2,1)S(1)} %bitcast.19), channel_id=1, source_target_pairs={{0,128},{128,0},{1,129},{129,1},{2,130},{130,2},{3,131},{131,3},{4... | collective-permute-start | bytes 3145736 | tf_op jit(solution)/shard_map/ppermute | solution.py:371
  74.8 48.5 %all-to-all-start = ((bf16[16,256,128]{2,1,0:T(8,128)(2,1)}), bf16[16,256,128]{2,1,0:T(8,128)(2,1)S(1)}, u32[]{:S(2)}, u32[]{:S(2)}) async-start(bf16[16,256,128]{2,1,0:T(8,128)(2,1)} %blend.2), calls=%async_computation | async-start | bytes 2097152 | tf_op jit(solution)/shard_map/all_to_all | solution.py:375
  82.7 9.4 %collective-permute-start.10 = (bf16[2,16,32,128]{3,2,1,0:T(8,128)(2,1)S(1)}, bf16[2,16,32,128]{3,2,1,0:T(8,128)(2,1)S(1)}, u32[]{:S(2)}, u32[]{:S(2)}) collective-permute-start(bf16[2,16,32,128]{3,2,1,0:T(8,128)(2,1)S(1)} %get-tuple-element.19), channel_id=1, source_target_pairs={{0,4},{1,5},{2,6},{3,7},{4,0},{5,1},{6,2},{7,3},{8,12},{9,13},{10,... | collective-permute-start | bytes 786440 | tf_op jit(solution)/shard_map/ppermute | solution.py:380
  83.9 14.7 %collective-permute-start.11 = (bf16[2,16,32,128]{3,2,1,0:T(8,128)(2,1)S(1)}, bf16[2,16,32,128]{3,2,1,0:T(8,128)(2,1)S(1)}, u32[]{:S(2)}, u32[]{:S(2)}) collective-permute-start(bf16[2,16,32,128]{3,2,1,0:T(8,128)(2,1)S(1)} %get-tuple-element.20), channel_id=1, source_target_pairs={{0,6},{1,7},{2,0},{3,1},{4,2},{5,3},{6,4},{7,5},{8,14},{9,15},{10,... | collective-permute-start | bytes 786440 | tf_op jit(solution)/shard_map/ppermute | solution.py:380
  83.9 14.7 %collective-permute-start.9 = (bf16[2,16,32,128]{3,2,1,0:T(8,128)(2,1)S(1)}, bf16[2,16,32,128]{3,2,1,0:T(8,128)(2,1)S(1)}, u32[]{:S(2)}, u32[]{:S(2)}) collective-permute-start(bf16[2,16,32,128]{3,2,1,0:T(8,128)(2,1)S(1)} %get-tuple-element.18), channel_id=1, source_target_pairs={{0,2},{1,3},{2,4},{3,5},{4,6},{5,7},{6,0},{7,1},{8,10},{9,11},{10,... | collective-permute-start | bytes 786440 | tf_op jit(solution)/shard_map/ppermute | solution.py:380
  87.4 13.8 %collective-permute-start.2 = (bf16[2,16,32,128]{3,2,1,0:T(8,128)(2,1)S(1)}, bf16[2,16,32,128]{3,2,1,0:T(8,128)(2,1)S(1)}, u32[]{:S(2)}, u32[]{:S(2)}) collective-permute-start(bf16[2,16,32,128]{3,2,1,0:T(8,128)(2,1)S(1)} %get-tuple-element.15), channel_id=1, source_target_pairs={{0,2},{1,3},{2,4},{3,5},{4,6},{5,7},{6,0},{7,1},{8,10},{9,11},{10,... | collective-permute-start | bytes 786440 | tf_op jit(solution)/shard_map/ppermute | solution.py:380
  88.0 15.3 %collective-permute-start.3 = (bf16[2,16,32,128]{3,2,1,0:T(8,128)(2,1)S(1)}, bf16[2,16,32,128]{3,2,1,0:T(8,128)(2,1)S(1)}, u32[]{:S(2)}, u32[]{:S(2)}) collective-permute-start(bf16[2,16,32,128]{3,2,1,0:T(8,128)(2,1)S(1)} %get-tuple-element.16), channel_id=1, source_target_pairs={{0,4},{1,5},{2,6},{3,7},{4,0},{5,1},{6,2},{7,3},{8,12},{9,13},{10,... | collective-permute-start | bytes 786440 | tf_op jit(solution)/shard_map/ppermute | solution.py:380
  92.1 20.9 %copy-start.3 = (s32[16,2]{0,1:T(2,128)S(1)}, s32[16,2]{0,1:T(2,128)}, u32[]{:S(2)}) copy-start(s32[16,2]{0,1:T(2,128)} %param.11) | copy-start | bytes 388
  92.1 17.3 %collective-permute-start.4 = (bf16[2,16,32,128]{3,2,1,0:T(8,128)(2,1)S(1)}, bf16[2,16,32,128]{3,2,1,0:T(8,128)(2,1)S(1)}, u32[]{:S(2)}, u32[]{:S(2)}) collective-permute-start(bf16[2,16,32,128]{3,2,1,0:T(8,128)(2,1)S(1)} %get-tuple-element.17), channel_id=1, source_target_pairs={{0,6},{1,7},{2,0},{3,1},{4,2},{5,3},{6,4},{7,5},{8,14},{9,15},{10,... | collective-permute-start | bytes 786440 | tf_op jit(solution)/shard_map/ppermute | solution.py:380
  99.4 11.8 %collective-permute-start.12 = (bf16[2,16,32,128]{3,2,1,0:T(8,128)(2,1)S(1)}, bf16[2,16,32,128]{3,2,1,0:T(8,128)(2,1)S(1)}, u32[]{:S(2)}, u32[]{:S(2)}) collective-permute-start(bf16[2,16,32,128]{3,2,1,0:T(8,128)(2,1)S(1)} %shard_map.69.mine_ref), channel_id=1, source_target_pairs={{0,1},{1,0},{2,3},{3,2},{4,5},{5,4},{6,7},{7,6},{8,9},{9,8},{10,11... | collective-permute-start | bytes 786440 | tf_op jit(solution)/shard_map/ppermute | solution.py:385
  110.2 9.1 %collective-permute-start.5 = (bf16[2,16,32,128]{3,2,1,0:T(8,128)(2,1)S(1)}, bf16[2,16,32,128]{3,2,1,0:T(8,128)(2,1)}, u32[]{:S(2)}, u32[]{:S(2)}) collective-permute-start(bf16[2,16,32,128]{3,2,1,0:T(8,128)(2,1)S(1)} %shard_map.66.mine_ref), channel_id=1, source_target_pairs={{0,1},{1,0},{2,3},{3,2},{4,5},{5,4},{6,7},{7,6},{8,9},{9,8},{10,11... | collective-permute-start | bytes 786440 | tf_op jit(solution)/shard_map/ppermute | solution.py:385
  112.9 9.7 %collective-permute-start.13 = (bf16[2,16,32,128]{3,2,1,0:T(8,128)(2,1)}, bf16[2,16,32,128]{3,2,1,0:T(8,128)(2,1)}, u32[]{:S(2)}, u32[]{:S(2)}) collective-permute-start(bf16[2,16,32,128]{3,2,1,0:T(8,128)(2,1)} %shard_map.70.refs_9_.refs_7_), channel_id=1, source_target_pairs={{0,2},{1,3},{2,4},{3,5},{4,6},{5,7},{6,0},{7,1},{8,10},{9,11},{10,... | collective-permute-start | bytes 786440 | tf_op jit(solution)/shard_map/ppermute | solution.py:380
  113.3 11.9 %collective-permute-start.14 = (bf16[2,16,32,128]{3,2,1,0:T(8,128)(2,1)}, bf16[2,16,32,128]{3,2,1,0:T(8,128)(2,1)}, u32[]{:S(2)}, u32[]{:S(2)}) collective-permute-start(bf16[2,16,32,128]{3,2,1,0:T(8,128)(2,1)} %shard_map.70.refs_9_.refs_7_), channel_id=1, source_target_pairs={{0,4},{1,5},{2,6},{3,7},{4,0},{5,1},{6,2},{7,3},{8,12},{9,13},{10,... | collective-permute-start | bytes 786440 | tf_op jit(solution)/shard_map/ppermute | solution.py:380
  115.4 15.3 %collective-permute-start.15 = (bf16[2,16,32,128]{3,2,1,0:T(8,128)(2,1)}, bf16[2,16,32,128]{3,2,1,0:T(8,128)(2,1)}, u32[]{:S(2)}, u32[]{:S(2)}) collective-permute-start(bf16[2,16,32,128]{3,2,1,0:T(8,128)(2,1)} %shard_map.70.refs_9_.refs_7_), channel_id=1, source_target_pairs={{0,6},{1,7},{2,0},{3,1},{4,2},{5,3},{6,4},{7,5},{8,14},{9,15},{10,... | collective-permute-start | bytes 786440 | tf_op jit(solution)/shard_map/ppermute | solution.py:380
  121.0 11.4 %collective-permute-start.6 = (bf16[2,16,32,128]{3,2,1,0:T(8,128)(2,1)}, bf16[2,16,32,128]{3,2,1,0:T(8,128)(2,1)S(1)}, u32[]{:S(2)}, u32[]{:S(2)}) collective-permute-start(bf16[2,16,32,128]{3,2,1,0:T(8,128)(2,1)} %shard_map.67.refs_5_.refs_3_), channel_id=1, source_target_pairs={{0,2},{1,3},{2,4},{3,5},{4,6},{5,7},{6,0},{7,1},{8,10},{9,11},{10,... | collective-permute-start | bytes 786440 | tf_op jit(solution)/shard_map/ppermute | solution.py:380
  121.1 11.9 %collective-permute-start.7 = (bf16[2,16,32,128]{3,2,1,0:T(8,128)(2,1)}, bf16[2,16,32,128]{3,2,1,0:T(8,128)(2,1)}, u32[]{:S(2)}, u32[]{:S(2)}) collective-permute-start(bf16[2,16,32,128]{3,2,1,0:T(8,128)(2,1)} %shard_map.67.refs_5_.refs_3_), channel_id=1, source_target_pairs={{0,4},{1,5},{2,6},{3,7},{4,0},{5,1},{6,2},{7,3},{8,12},{9,13},{10,... | collective-permute-start | bytes 786440 | tf_op jit(solution)/shard_map/ppermute | solution.py:380
  122.6 17.6 %collective-permute-start.8 = (bf16[2,16,32,128]{3,2,1,0:T(8,128)(2,1)}, bf16[2,16,32,128]{3,2,1,0:T(8,128)(2,1)}, u32[]{:S(2)}, u32[]{:S(2)}) collective-permute-start(bf16[2,16,32,128]{3,2,1,0:T(8,128)(2,1)} %shard_map.67.refs_5_.refs_3_), channel_id=1, source_target_pairs={{0,6},{1,7},{2,0},{3,1},{4,2},{5,3},{6,4},{7,5},{8,14},{9,15},{10,... | collective-permute-start | bytes 786440 | tf_op jit(solution)/shard_map/ppermute | solution.py:380
  199.5 93.1 %all-to-all-start.3 = ((bf16[16,128,128]{2,1,0:T(8,128)(2,1)}), bf16[16,128,128]{2,1,0:T(8,128)(2,1)}, u32[]{:S(2)}, u32[]{:S(2)}) async-start(bf16[16,128,128]{2,1,0:T(8,128)(2,1)} %shard_map.71), calls=%async_computation.3 | async-start | bytes 1048576 | tf_op jit(solution)/shard_map/all_to_all | solution.py:375
  292.6 24.4 %all-to-all-start.4 = ((bf16[16,128,128]{2,1,0:T(8,128)(2,1)}), bf16[16,128,128]{2,1,0:T(8,128)(2,1)S(1)}, u32[]{:S(2)}, u32[]{:S(2)}) async-start(bf16[16,128,128]{2,1,0:T(8,128)(2,1)} %shard_map.72), calls=%async_computation.4 | async-start | bytes 1048576 | tf_op jit(solution)/shard_map/all_to_all | solution.py:375

commit v6 on v5

--- a/solution.py
+++ b/solution.py
@@ -50,31 +50,34 @@
     )(strength, own, partner)
 
 
-def split_kernel(source_ref, out_ref, sem):
+def split_kernel(source_ref, out_ref, kept_ref, in_sem, out_sem):
     heads = out_ref.shape[0]
-    copies = [
-        pltpu.make_async_copy(
-            source_ref.at[:, :, pl.ds(head * HEAD, HEAD)], out_ref.at[head], sem.at[head]
-        )
-        for head in range(heads)
-    ]
-    for copy in copies:
-        copy.start()
-    for copy in copies:
-        copy.wait()
+    reads, writes = [], []
+    for head in range(heads):
+        lanes = pl.ds(head * HEAD, HEAD)
+        kept = kept_ref.at[head]
+        reads.append(pltpu.make_async_copy(source_ref.at[:, :, lanes], kept, in_sem.at[head]))
+        writes.append(pltpu.make_async_copy(kept, out_ref.at[head], out_sem.at[head]))
+    for read in reads:
+        read.start()
+    for read, write in zip(reads, writes):
+        read.wait()
+        write.start()
+    for write in writes:
+        write.wait()
 
 
 def split_heads(rows):
     frames, count, width = rows.shape
     heads = width // HEAD
-    out = jax.ShapeDtypeStruct((heads, frames, count, HEAD), BF16)
+    shape = (heads, frames, count, HEAD)
+    sems = pltpu.SemaphoreType.DMA((heads,))
     return pl.pallas_call(
         split_kernel,
-        grid=(1,),
         in_specs=[ANY],
-        out_specs=whole(out),
-        out_shape=out,
-        scratch_shapes=[pltpu.SemaphoreType.DMA((heads,))],
+        out_specs=ANY,
+        out_shape=pltpu.HBM(shape, BF16),
+        scratch_shapes=[pltpu.VMEM(shape, BF16), sems, sems],
         cost_estimate=pl.CostEstimate(flops=0, bytes_accessed=4 * rows.size, transcendentals=0),
         name="split_heads",
     )(rows)
@@ -117,6 +120,8 @@
     refs = refs[3 + 2 * pieces :]
     if mode != "own":
         out_ref = refs.pop(0)
+    if mode == "more":
+        own_sums = refs.pop()
     acc, unsafe, keys, values, query_ref, top, key_sem, value_sem, sem = refs
     parts, cuts, blocks, cut_rows = keys.shape[:4]
     tile = blocks * cut_rows
@@ -167,7 +172,7 @@
     )
     query_copy.start()
     if mode == "more":
-        acc_copy = pltpu.make_async_copy(acc_in, acc, sem.at[1])
+        acc_copy = pltpu.make_async_copy(acc_in, own_sums, sem.at[1])
         acc_copy.start()
     else:
         start(0)
@@ -183,15 +188,13 @@
     pair = scaled_split(query)
     if mode == "more":
         unsafe[0] = unsafe_in[0]
-        acc_copy.wait()
     else:
         unsafe[0] = 0
 
     if mode == "own":
         add_part(0, pair, query_norm, True)
         return
-    if mode == "all":
-        acc[...] = jnp.zeros_like(acc)
+    acc[...] = jnp.zeros_like(acc)
 
     def one_part(part, carry):
         @pl.when(valid_ref[part] > 0)
@@ -205,9 +208,13 @@
     def finish(sums):
         return (sums[:, :HEAD] / sums[:, HEAD:]).astype(BF16)
 
+    if mode == "more":
+        acc_copy.wait()
+
     @pl.when(unsafe[0] == 0)
     def _():
-        out_ref[...] = finish(acc[...]).reshape(out_ref.shape)
+        sums = acc[...] + own_sums[...] if mode == "more" else acc[...]
+        out_ref[...] = finish(sums).reshape(out_ref.shape)
 
     @pl.when(unsafe[0] > 0)
     def _():
@@ -269,6 +276,8 @@
     else:
         out_shape, out_specs = [out], [whole(out)]
         scratch = [pltpu.VMEM(acc.shape, F32), pltpu.SMEM((1,), jnp.int32)] + scratch
+    if mode == "more":
+        scratch.append(pltpu.VMEM(acc.shape, F32))
     work = {"own": 1, "more": parts - 1, "all": parts}[mode] * total * total
     result = pl.pallas_call(
         functools.partial(attend_kernel, frame=frame, pieces=pieces, rows=rows, mode=mode),
@@ -357,10 +366,9 @@
     moved = sum(math.prod(o.shape) for o in out_shapes)
     return pl.pallas_call(
         kernel,
-        grid=(1,),
         in_specs=[SMEM, SMEM] + [ANY] * len(arrays),
-        out_specs=[whole(o) for o in out_shapes],
-        out_shape=out_shapes,
+        out_specs=[pl.BlockSpec(memory_space=pltpu.VMEM)] * len(out_shapes),
+        out_shape=[pltpu.VMEM(o.shape, o.dtype) for o in out_shapes],
         scratch_shapes=[pltpu.SemaphoreType.DMA((len(out_shapes) * keyframes.shape[0] + 1,))],
         compiler_params=pltpu.CompilerParams(vmem_limit_bytes=8 << 20),
         cost_estimate=pl.CostEstimate(flops=0, bytes_accessed=4 * moved, transcendentals=0),

time: 319 us -> 319 us (level)
  no operation moved by 1% of the time
where the time goes in v6:
time: 319 us; the launch traced here: 318 us
  Pallas kernels  161 us (50%)
  waiting for transfers between devices  103 us (32%)
  starting transfers between devices  51 us (16%)
    pallas_call x3, Pallas kernels, attend(): pl.pallas_call(functools.partial(attend_kernel, frame=frame, pieces=piece...  147 us
    ppermute x2, waiting for transfers between devices, swap_branch(): return lax.ppermute(value, 'branch', [(0, 1), (1, 0)])  48.5 us
    all_to_all x5, starting transfers between devices, to_heads(): return lax.all_to_all(value, 'seq', split_axis=0, concat_axis=0, tiled=True)  38.1 us
    ppermute x12, waiting for transfers between devices, shift_x(): lax.ppermute(value, 'mp', [(m, (m + 2 * step) % size) for m in range(size)])  33.9 us
    all_to_all x5, waiting for transfers between devices, to_heads(): return lax.all_to_all(value, 'seq', split_axis=0, concat_axis=0, tiled=True)  17.1 us
    ppermute x12, starting transfers between devices, shift_x(): lax.ppermute(value, 'mp', [(m, (m + 2 * step) % size) for m in range(size)])  9.72 us
    pallas_call x6, Pallas kernels, move_call(): pl.pallas_call(kernel, in_specs=[SMEM, SMEM] + [ANY] * len(arrays), out_s...  6.45 us
  transfers between devices with their start and end apart: 21, of which 15 were waited for; matrix products, arithmetic and copies ran while one was open for 1% of the time, Pallas kernels for 31%

profile of v6, /device:TPU:31, one launch (start us, length us, event | category | flops | bytes accessed | tf_op | source)
XLA Modules:
  0.0 318.5 jit_solution(10211436994260324182)
XLA Ops:
  0.0 2.3 split_heads.1
  2.3 9.2 %all-to-all-start.2 = ((bf16[16,256,128]{2,1,0:T(8,128)(2,1)}), bf16[16,256,128]{2,1,0:T(8,128)(2,1)S(1)}, u32[]{:S(2)}, u32[]{:S(2)}) async-start(bf16[16,256,128]{2,1,0:T(8,128)(2,1)} %bitcast.11), calls=%async_computation.2 | async-start | bytes 2097152 | tf_op jit(solution)/shard_map/all_to_all | solution.py:383
  11.4 0.6 collective-permute-start.1
  12.0 24.3 %collective-permute-done.1.partner_ref = bf16[2,128,2048]{2,1,0:T(8,128)(2,1)} collective-permute-done((bf16[2,128,2048]{2,1,0:T(8,128)(2,1)S(1)}, bf16[2,128,2048]{2,1,0:T(8,128)(2,1)}, u32[]{:S(2)}, u32[]{:S(2)}) %collective-permute-start.1) | collective-permute-done | bytes 1048608 | tf_op jit(solution)/shard_map/ppermute | solution.py:379
  36.3 2.6 blend.3
  38.8 0.6 all-to-all-done.2.refs_2_.source_ref.refs_4_
  39.4 7.2 %all-to-all-start.1 = ((bf16[16,256,128]{2,1,0:T(8,128)(2,1)}), bf16[16,256,128]{2,1,0:T(8,128)(2,1)S(1)}, u32[]{:S(2)}, u32[]{:S(2)}) async-start(bf16[16,256,128]{2,1,0:T(8,128)(2,1)} %blend.3), calls=%async_computation.1 | async-start | bytes 2097152 | tf_op jit(solution)/shard_map/all_to_all | solution.py:383
  46.6 0.6 collective-permute-start
  47.2 24.3 %collective-permute-done.partner_ref = bf16[2,128,2048]{2,1,0:T(8,128)(2,1)} collective-permute-done((bf16[2,128,2048]{2,1,0:T(8,128)(2,1)S(1)}, bf16[2,128,2048]{2,1,0:T(8,128)(2,1)}, u32[]{:S(2)}, u32[]{:S(2)}) %collective-permute-start) | collective-permute-done | bytes 1048608 | tf_op jit(solution)/shard_map/ppermute | solution.py:379
  71.4 2.5 blend.2
  74.0 0.6 all-to-all-done.1.refs_1_.source_ref.refs_3_
  74.6 7.2 %all-to-all-start = ((bf16[16,256,128]{2,1,0:T(8,128)(2,1)}), bf16[16,256,128]{2,1,0:T(8,128)(2,1)S(1)}, u32[]{:S(2)}, u32[]{:S(2)}) async-start(bf16[16,256,128]{2,1,0:T(8,128)(2,1)} %blend.2), calls=%async_computation | async-start | bytes 2097152 | tf_op jit(solution)/shard_map/all_to_all | solution.py:383
  81.8 0.8 shard_map.68
  82.5 1.2 collective-permute-start.10
  83.7 2.7 collective-permute-start.9
  86.4 0.7 shard_map.65
  87.2 0.7 collective-permute-start.2
  87.8 0.1 collective-permute-start.3
  88.0 3.9 %collective-permute-done.10.refs_1_ = bf16[2,16,32,128]{3,2,1,0:T(8,128)(2,1)S(1)} collective-permute-done((bf16[2,16,32,128]{3,2,1,0:T(8,128)(2,1)S(1)}, bf16[2,16,32,128]{3,2,1,0:T(8,128)(2,1)S(1)}, u32[]{:S(2)}, u32[]{:S(2)}) %collective-permute-start.10) | collective-permute-done | bytes 262176 | tf_op jit(solution)/shard_map/ppermute | solution.py:388
  91.9 0.5 collective-permute-start.4
  92.5 6.0 %collective-permute-done.11.refs_2_ = bf16[2,16,32,128]{3,2,1,0:T(8,128)(2,1)S(1)} collective-permute-done((bf16[2,16,32,128]{3,2,1,0:T(8,128)(2,1)S(1)}, bf16[2,16,32,128]{3,2,1,0:T(8,128)(2,1)S(1)}, u32[]{:S(2)}, u32[]{:S(2)}) %collective-permute-start.11) | collective-permute-done | bytes 262176 | tf_op jit(solution)/shard_map/ppermute | solution.py:388
  98.4 0.8 shard_map.69.mine_ref
  99.2 1.0 collective-permute-start.12
  100.3 0.6 collective-permute-done.2.refs_0_
  100.9 2.3 collective-permute-done.3.refs_1_
  103.2 6.0 %collective-permute-done.4.refs_2_ = bf16[2,16,32,128]{3,2,1,0:T(8,128)(2,1)S(1)} collective-permute-done((bf16[2,16,32,128]{3,2,1,0:T(8,128)(2,1)S(1)}, bf16[2,16,32,128]{3,2,1,0:T(8,128)(2,1)S(1)}, u32[]{:S(2)}, u32[]{:S(2)}) %collective-permute-start.4) | collective-permute-done | bytes 262176 | tf_op jit(solution)/shard_map/ppermute | solution.py:388
  109.2 0.8 shard_map.66.mine_ref
  110.0 1.0 collective-permute-start.5
  111.1 1.7 shard_map.70.refs_9_.refs_7_
  112.9 0.2 dynamic-slice_reduce_fusion.1
  113.1 2.1 collective-permute-start.14
  115.3 3.9 %collective-permute-done.5.other_ref = bf16[2,16,32,128]{3,2,1,0:T(8,128)(2,1)} collective-permute-done((bf16[2,16,32,128]{3,2,1,0:T(8,128)(2,1)S(1)}, bf16[2,16,32,128]{3,2,1,0:T(8,128)(2,1)}, u32[]{:S(2)}, u32[]{:S(2)}) %collective-permute-start.5) | collective-permute-done | bytes 262176 | tf_op jit(solution)/shard_map/ppermute | solution.py:393
  119.1 1.6 shard_map.67.refs_5_.refs_3_
  120.9 1.5 collective-permute-start.7
  122.4 0.6 collective-permute-start.8
  123.1 1.8 shard_map.64
  124.9 5.5 %collective-permute-done.15.refs_12_.refs_10_ = bf16[2,16,32,128]{3,2,1,0:T(8,128)(2,1)} collective-permute-done((bf16[2,16,32,128]{3,2,1,0:T(8,128)(2,1)}, bf16[2,16,32,128]{3,2,1,0:T(8,128)(2,1)}, u32[]{:S(2)}, u32[]{:S(2)}) %collective-permute-start.15) | collective-permute-done | bytes 262176 | tf_op jit(solution)/shard_map/ppermute | solution.py:388
  130.5 1.7 collective-permute-done.6.refs_6_.refs_4_
  132.2 0.6 collective-permute-done.7.refs_7_.refs_5_
  132.8 7.2 %collective-permute-done.8.refs_8_.refs_6_ = bf16[2,16,32,128]{3,2,1,0:T(8,128)(2,1)} collective-permute-done((bf16[2,16,32,128]{3,2,1,0:T(8,128)(2,1)}, bf16[2,16,32,128]{3,2,1,0:T(8,128)(2,1)}, u32[]{:S(2)}, u32[]{:S(2)}) %collective-permute-start.8) | collective-permute-done | bytes 262176 | tf_op jit(solution)/shard_map/ppermute | solution.py:388
  140.0 59.3 %shard_map.71 = bf16[16,128,128]{2,1,0:T(8,128)(2,1)} custom-call(s32[3]{0:T(128)S(1)} %pad_add_fusion.1.valid_ref, s32[1]{0:T(128)} %get-tuple-element.13.refs_0_, f32[2048,256]{1,0:T(8,128)S(1)} %get-tuple-element.14.refs_1_, bf16[16,256,128]{2,1,0:T(8,128)(2,1)S(1)} %all-to-all-done.refs_0_.refs_2_, ...), custom_call_target="tpu_custom_call" | custom-call | flops 4294967296 | bytes 4194304 | tf_op jit(solution)/shard_map/pallas_call | solution.py:282
  199.3 7.3 %all-to-all-start.3 = ((bf16[16,128,128]{2,1,0:T(8,128)(2,1)}), bf16[16,128,128]{2,1,0:T(8,128)(2,1)}, u32[]{:S(2)}, u32[]{:S(2)}) async-start(bf16[16,128,128]{2,1,0:T(8,128)(2,1)} %shard_map.71), calls=%async_computation.3 | async-start | bytes 1048576 | tf_op jit(solution)/shard_map/all_to_all | solution.py:383
  206.7 85.6 %shard_map.72 = bf16[16,128,128]{2,1,0:T(8,128)(2,1)} custom-call(s32[3]{0:T(128)S(1)} %pad_add_fusion.valid_ref, bf16[16,256,128]{2,1,0:T(8,128)(2,1)S(1)} %all-to-all-done.refs_0_.refs_2_, bf16[16,256,128]{2,1,0:T(8,128)(2,1)S(1)} %all-to-all-done.1.refs_1_.source_ref.refs_3_, bf16[16,256,128]{2,1,0:T(8,128)(2,1)S(1)} %all-to-all-done.2.refs_2_.source_ref.refs_4_, ...), custom_call_target="tpu_custom_call" | custom-call | flops 6442450944 | bytes 4194304 | tf_op jit(solution)/shard_map/pallas_call | solution.py:282
  292.4 7.2 %all-to-all-start.4 = ((bf16[16,128,128]{2,1,0:T(8,128)(2,1)}), bf16[16,128,128]{2,1,0:T(8,128)(2,1)S(1)}, u32[]{:S(2)}, u32[]{:S(2)}) async-start(bf16[16,128,128]{2,1,0:T(8,128)(2,1)} %shard_map.72), calls=%async_computation.4 | async-start | bytes 1048576 | tf_op jit(solution)/shard_map/all_to_all | solution.py:383
  299.6 1.3 copy.7
  300.9 15.9 %all-to-all-done.4 = bf16[16,128,128]{2,1,0:T(8,128)(2,1)S(1)} async-done(((bf16[16,128,128]{2,1,0:T(8,128)(2,1)}), bf16[16,128,128]{2,1,0:T(8,128)(2,1)S(1)}, u32[]{:S(2)}, u32[]{:S(2)}) %all-to-all-start.4) | async-done | bytes 524320 | tf_op jit(solution)/shard_map/all_to_all | solution.py:383
  316.8 0.3 copy.8
  317.2 1.3 copy.9
  (21 shorter events, 0.5 us)
Async XLA Ops:
  0.0 11.4 %copy-start.1 = (bf16[1,2,128,2048]{3,2,1,0:T(8,128)(2,1)S(1)}, bf16[1,2,128,2048]{3,2,1,0:T(8,128)(2,1)}, u32[]{:S(2)}) copy-start(bf16[1,2,128,2048]{3,2,1,0:T(8,128)(2,1)} %param.7) | copy-start | bytes 3145732
  2.3 37.2 %all-to-all-start.2 = ((bf16[16,256,128]{2,1,0:T(8,128)(2,1)}), bf16[16,256,128]{2,1,0:T(8,128)(2,1)S(1)}, u32[]{:S(2)}, u32[]{:S(2)}) async-start(bf16[16,256,128]{2,1,0:T(8,128)(2,1)} %bitcast.11), calls=%async_computation.2 | async-start | bytes 2097152 | tf_op jit(solution)/shard_map/all_to_all | solution.py:383
  11.4 35.2 %copy-start.2 = (bf16[1,2,128,2048]{3,2,1,0:T(8,128)(2,1)S(1)}, bf16[1,2,128,2048]{3,2,1,0:T(8,128)(2,1)}, u32[]{:S(2)}) copy-start(bf16[1,2,128,2048]{3,2,1,0:T(8,128)(2,1)} %param.6) | copy-start | bytes 3145732
  11.4 24.8 %collective-permute-start.1 = (bf16[2,128,2048]{2,1,0:T(8,128)(2,1)S(1)}, bf16[2,128,2048]{2,1,0:T(8,128)(2,1)}, u32[]{:S(2)}, u32[]{:S(2)}) collective-permute-start(bf16[2,128,2048]{2,1,0:T(8,128)(2,1)S(1)} %bitcast.17), channel_id=1, source_target_pairs={{0,128},{128,0},{1,129},{129,1},{2,130},{130,2},{3,131},{131,3},{4... | collective-permute-start | bytes 3145736 | tf_op jit(solution)/shard_map/ppermute | solution.py:379
  39.4 35.2 %all-to-all-start.1 = ((bf16[16,256,128]{2,1,0:T(8,128)(2,1)}), bf16[16,256,128]{2,1,0:T(8,128)(2,1)S(1)}, u32[]{:S(2)}, u32[]{:S(2)}) async-start(bf16[16,256,128]{2,1,0:T(8,128)(2,1)} %blend.3), calls=%async_computation.1 | async-start | bytes 2097152 | tf_op jit(solution)/shard_map/all_to_all | solution.py:383
  46.6 35.1 %copy-start = (s32[2]{0:T(128)S(1)}, s32[2]{0:T(128)}, u32[]{:S(2)}) copy-start(s32[2]{0:T(128)} %keyframes_ref.11) | copy-start | bytes 28
  46.6 24.8 %collective-permute-start = (bf16[2,128,2048]{2,1,0:T(8,128)(2,1)S(1)}, bf16[2,128,2048]{2,1,0:T(8,128)(2,1)}, u32[]{:S(2)}, u32[]{:S(2)}) collective-permute-start(bf16[2,128,2048]{2,1,0:T(8,128)(2,1)S(1)} %bitcast.19), channel_id=1, source_target_pairs={{0,128},{128,0},{1,129},{129,1},{2,130},{130,2},{3,131},{131,3},{4... | collective-permute-start | bytes 3145736 | tf_op jit(solution)/shard_map/ppermute | solution.py:379
  74.6 48.5 %all-to-all-start = ((bf16[16,256,128]{2,1,0:T(8,128)(2,1)}), bf16[16,256,128]{2,1,0:T(8,128)(2,1)S(1)}, u32[]{:S(2)}, u32[]{:S(2)}) async-start(bf16[16,256,128]{2,1,0:T(8,128)(2,1)} %blend.2), calls=%async_computation | async-start | bytes 2097152 | tf_op jit(solution)/shard_map/all_to_all | solution.py:383
  82.5 9.4 %collective-permute-start.10 = (bf16[2,16,32,128]{3,2,1,0:T(8,128)(2,1)S(1)}, bf16[2,16,32,128]{3,2,1,0:T(8,128)(2,1)S(1)}, u32[]{:S(2)}, u32[]{:S(2)}) collective-permute-start(bf16[2,16,32,128]{3,2,1,0:T(8,128)(2,1)S(1)} %get-tuple-element.19), channel_id=1, source_target_pairs={{0,4},{1,5},{2,6},{3,7},{4,0},{5,1},{6,2},{7,3},{8,12},{9,13},{10,... | collective-permute-start | bytes 786440 | tf_op jit(solution)/shard_map/ppermute | solution.py:388
  83.7 14.7 %collective-permute-start.11 = (bf16[2,16,32,128]{3,2,1,0:T(8,128)(2,1)S(1)}, bf16[2,16,32,128]{3,2,1,0:T(8,128)(2,1)S(1)}, u32[]{:S(2)}, u32[]{:S(2)}) collective-permute-start(bf16[2,16,32,128]{3,2,1,0:T(8,128)(2,1)S(1)} %get-tuple-element.20), channel_id=1, source_target_pairs={{0,6},{1,7},{2,0},{3,1},{4,2},{5,3},{6,4},{7,5},{8,14},{9,15},{10,... | collective-permute-start | bytes 786440 | tf_op jit(solution)/shard_map/ppermute | solution.py:388
  83.7 14.7 %collective-permute-start.9 = (bf16[2,16,32,128]{3,2,1,0:T(8,128)(2,1)S(1)}, bf16[2,16,32,128]{3,2,1,0:T(8,128)(2,1)S(1)}, u32[]{:S(2)}, u32[]{:S(2)}) collective-permute-start(bf16[2,16,32,128]{3,2,1,0:T(8,128)(2,1)S(1)} %get-tuple-element.18), channel_id=1, source_target_pairs={{0,2},{1,3},{2,4},{3,5},{4,6},{5,7},{6,0},{7,1},{8,10},{9,11},{10,... | collective-permute-start | bytes 786440 | tf_op jit(solution)/shard_map/ppermute | solution.py:388
  87.2 13.8 %collective-permute-start.2 = (bf16[2,16,32,128]{3,2,1,0:T(8,128)(2,1)S(1)}, bf16[2,16,32,128]{3,2,1,0:T(8,128)(2,1)S(1)}, u32[]{:S(2)}, u32[]{:S(2)}) collective-permute-start(bf16[2,16,32,128]{3,2,1,0:T(8,128)(2,1)S(1)} %get-tuple-element.15), channel_id=1, source_target_pairs={{0,2},{1,3},{2,4},{3,5},{4,6},{5,7},{6,0},{7,1},{8,10},{9,11},{10,... | collective-permute-start | bytes 786440 | tf_op jit(solution)/shard_map/ppermute | solution.py:388
  87.8 15.3 %collective-permute-start.3 = (bf16[2,16,32,128]{3,2,1,0:T(8,128)(2,1)S(1)}, bf16[2,16,32,128]{3,2,1,0:T(8,128)(2,1)S(1)}, u32[]{:S(2)}, u32[]{:S(2)}) collective-permute-start(bf16[2,16,32,128]{3,2,1,0:T(8,128)(2,1)S(1)} %get-tuple-element.16), channel_id=1, source_target_pairs={{0,4},{1,5},{2,6},{3,7},{4,0},{5,1},{6,2},{7,3},{8,12},{9,13},{10,... | collective-permute-start | bytes 786440 | tf_op jit(solution)/shard_map/ppermute | solution.py:388
  91.9 20.9 %copy-start.3 = (s32[16,2]{0,1:T(2,128)S(1)}, s32[16,2]{0,1:T(2,128)}, u32[]{:S(2)}) copy-start(s32[16,2]{0,1:T(2,128)} %param.11) | copy-start | bytes 388
  91.9 17.3 %collective-permute-start.4 = (bf16[2,16,32,128]{3,2,1,0:T(8,128)(2,1)S(1)}, bf16[2,16,32,128]{3,2,1,0:T(8,128)(2,1)S(1)}, u32[]{:S(2)}, u32[]{:S(2)}) collective-permute-start(bf16[2,16,32,128]{3,2,1,0:T(8,128)(2,1)S(1)} %get-tuple-element.17), channel_id=1, source_target_pairs={{0,6},{1,7},{2,0},{3,1},{4,2},{5,3},{6,4},{7,5},{8,14},{9,15},{10,... | collective-permute-start | bytes 786440 | tf_op jit(solution)/shard_map/ppermute | solution.py:388
  99.2 11.8 %collective-permute-start.12 = (bf16[2,16,32,128]{3,2,1,0:T(8,128)(2,1)S(1)}, bf16[2,16,32,128]{3,2,1,0:T(8,128)(2,1)S(1)}, u32[]{:S(2)}, u32[]{:S(2)}) collective-permute-start(bf16[2,16,32,128]{3,2,1,0:T(8,128)(2,1)S(1)} %shard_map.69.mine_ref), channel_id=1, source_target_pairs={{0,1},{1,0},{2,3},{3,2},{4,5},{5,4},{6,7},{7,6},{8,9},{9,8},{10,11... | collective-permute-start | bytes 786440 | tf_op jit(solution)/shard_map/ppermute | solution.py:393
  110.0 9.1 %collective-permute-start.5 = (bf16[2,16,32,128]{3,2,1,0:T(8,128)(2,1)S(1)}, bf16[2,16,32,128]{3,2,1,0:T(8,128)(2,1)}, u32[]{:S(2)}, u32[]{:S(2)}) collective-permute-start(bf16[2,16,32,128]{3,2,1,0:T(8,128)(2,1)S(1)} %shard_map.66.mine_ref), channel_id=1, source_target_pairs={{0,1},{1,0},{2,3},{3,2},{4,5},{5,4},{6,7},{7,6},{8,9},{9,8},{10,11... | collective-permute-start | bytes 786440 | tf_op jit(solution)/shard_map/ppermute | solution.py:393
  112.7 9.7 %collective-permute-start.13 = (bf16[2,16,32,128]{3,2,1,0:T(8,128)(2,1)}, bf16[2,16,32,128]{3,2,1,0:T(8,128)(2,1)}, u32[]{:S(2)}, u32[]{:S(2)}) collective-permute-start(bf16[2,16,32,128]{3,2,1,0:T(8,128)(2,1)} %shard_map.70.refs_9_.refs_7_), channel_id=1, source_target_pairs={{0,2},{1,3},{2,4},{3,5},{4,6},{5,7},{6,0},{7,1},{8,10},{9,11},{10,... | collective-permute-start | bytes 786440 | tf_op jit(solution)/shard_map/ppermute | solution.py:388
  113.1 11.9 %collective-permute-start.14 = (bf16[2,16,32,128]{3,2,1,0:T(8,128)(2,1)}, bf16[2,16,32,128]{3,2,1,0:T(8,128)(2,1)}, u32[]{:S(2)}, u32[]{:S(2)}) collective-permute-start(bf16[2,16,32,128]{3,2,1,0:T(8,128)(2,1)} %shard_map.70.refs_9_.refs_7_), channel_id=1, source_target_pairs={{0,4},{1,5},{2,6},{3,7},{4,0},{5,1},{6,2},{7,3},{8,12},{9,13},{10,... | collective-permute-start | bytes 786440 | tf_op jit(solution)/shard_map/ppermute | solution.py:388
  115.2 15.3 %collective-permute-start.15 = (bf16[2,16,32,128]{3,2,1,0:T(8,128)(2,1)}, bf16[2,16,32,128]{3,2,1,0:T(8,128)(2,1)}, u32[]{:S(2)}, u32[]{:S(2)}) collective-permute-start(bf16[2,16,32,128]{3,2,1,0:T(8,128)(2,1)} %shard_map.70.refs_9_.refs_7_), channel_id=1, source_target_pairs={{0,6},{1,7},{2,0},{3,1},{4,2},{5,3},{6,4},{7,5},{8,14},{9,15},{10,... | collective-permute-start | bytes 786440 | tf_op jit(solution)/shard_map/ppermute | solution.py:388
  120.8 11.4 %collective-permute-start.6 = (bf16[2,16,32,128]{3,2,1,0:T(8,128)(2,1)}, bf16[2,16,32,128]{3,2,1,0:T(8,128)(2,1)S(1)}, u32[]{:S(2)}, u32[]{:S(2)}) collective-permute-start(bf16[2,16,32,128]{3,2,1,0:T(8,128)(2,1)} %shard_map.67.refs_5_.refs_3_), channel_id=1, source_target_pairs={{0,2},{1,3},{2,4},{3,5},{4,6},{5,7},{6,0},{7,1},{8,10},{9,11},{10,... | collective-permute-start | bytes 786440 | tf_op jit(solution)/shard_map/ppermute | solution.py:388
  120.9 11.9 %collective-permute-start.7 = (bf16[2,16,32,128]{3,2,1,0:T(8,128)(2,1)}, bf16[2,16,32,128]{3,2,1,0:T(8,128)(2,1)}, u32[]{:S(2)}, u32[]{:S(2)}) collective-permute-start(bf16[2,16,32,128]{3,2,1,0:T(8,128)(2,1)} %shard_map.67.refs_5_.refs_3_), channel_id=1, source_target_pairs={{0,4},{1,5},{2,6},{3,7},{4,0},{5,1},{6,2},{7,3},{8,12},{9,13},{10,... | collective-permute-start | bytes 786440 | tf_op jit(solution)/shard_map/ppermute | solution.py:388
  122.4 17.6 %collective-permute-start.8 = (bf16[2,16,32,128]{3,2,1,0:T(8,128)(2,1)}, bf16[2,16,32,128]{3,2,1,0:T(8,128)(2,1)}, u32[]{:S(2)}, u32[]{:S(2)}) collective-permute-start(bf16[2,16,32,128]{3,2,1,0:T(8,128)(2,1)} %shard_map.67.refs_5_.refs_3_), channel_id=1, source_target_pairs={{0,6},{1,7},{2,0},{3,1},{4,2},{5,3},{6,4},{7,5},{8,14},{9,15},{10,... | collective-permute-start | bytes 786440 | tf_op jit(solution)/shard_map/ppermute | solution.py:388
  199.3 93.1 %all-to-all-start.3 = ((bf16[16,128,128]{2,1,0:T(8,128)(2,1)}), bf16[16,128,128]{2,1,0:T(8,128)(2,1)}, u32[]{:S(2)}, u32[]{:S(2)}) async-start(bf16[16,128,128]{2,1,0:T(8,128)(2,1)} %shard_map.71), calls=%async_computation.3 | async-start | bytes 1048576 | tf_op jit(solution)/shard_map/all_to_all | solution.py:383
  292.4 24.4 %all-to-all-start.4 = ((bf16[16,128,128]{2,1,0:T(8,128)(2,1)}), bf16[16,128,128]{2,1,0:T(8,128)(2,1)S(1)}, u32[]{:S(2)}, u32[]{:S(2)}) async-start(bf16[16,128,128]{2,1,0:T(8,128)(2,1)} %shard_map.72), calls=%async_computation.4 | async-start | bytes 1048576 | tf_op jit(solution)/shard_map/all_to_all | solution.py:383

commit v7 on v6

--- a/solution.py
+++ b/solution.py
@@ -19,6 +19,7 @@
 
 ANY = pl.BlockSpec(memory_space=pl.ANY)
 SMEM = pl.BlockSpec(memory_space=pltpu.SMEM)
+VMEM = pl.BlockSpec(memory_space=pltpu.VMEM)
 
 
 def blend_kernel(strength_ref, own_ref, partner_ref, out_ref, *, heads):
@@ -323,51 +324,42 @@
 def pick_x_kernel(place_ref, keyframes_ref, source_ref, *refs, shape):
     *got_refs, out_ref, sem = refs
     x = place_ref[0] // 2
-    extras = out_ref.shape[0]
-    for j in range(extras):
+    for j in range(out_ref.shape[0]):
         keyframe = keyframes_ref[j]
         step = lax.rem(x - keyframe // (2 * shape[0]) + shape[2], shape[2])
 
         @pl.when(step == 0)
         def _():
             rows = piece_rows(keyframe, x, shape)
-            pltpu.make_async_copy(source_ref.at[:, rows], out_ref.at[j], sem.at[j]).start()
+            run_copies([pltpu.make_async_copy(source_ref.at[:, rows], out_ref.at[j], sem.at[j])])
 
         for which, got_ref in enumerate(got_refs, 1):
 
             @pl.when(step == which)
             def _():
-                pltpu.make_async_copy(got_ref.at[j], out_ref.at[j], sem.at[j]).start()
-
-    for j in range(extras):
-        pltpu.make_async_copy(got_refs[0].at[j], out_ref.at[j], sem.at[j]).wait()
+                out_ref[j] = got_ref[j]
 
 
 def pick_y_kernel(place_ref, keyframes_ref, mine_ref, other_ref, out_ref, sem, *, shape):
     y = lax.rem(place_ref[0], 2)
-    extras = out_ref.shape[0]
-    for j in range(extras):
-        mine, other = mine_ref.at[j], other_ref.at[j]
+    for j in range(out_ref.shape[0]):
         same = lax.rem(keyframes_ref[j] // shape[0], 2) == y
 
         @pl.when(same)
         def _():
-            pltpu.make_async_copy(mine, out_ref.at[j], sem.at[j]).start()
+            out_ref[j] = mine_ref[j]
 
         @pl.when(jnp.logical_not(same))
         def _():
-            pltpu.make_async_copy(other, out_ref.at[j], sem.at[j]).start()
-
-    for j in range(extras):
-        pltpu.make_async_copy(out_ref.at[j], out_ref.at[j], sem.at[j]).wait()
+            out_ref[j] = other_ref[j]
 
 
 def move_call(kernel, out_shapes, place, keyframes, *arrays):
     moved = sum(math.prod(o.shape) for o in out_shapes)
     return pl.pallas_call(
         kernel,
-        in_specs=[SMEM, SMEM] + [ANY] * len(arrays),
-        out_specs=[pl.BlockSpec(memory_space=pltpu.VMEM)] * len(out_shapes),
+        in_specs=[SMEM, SMEM] + [VMEM if a.ndim == 4 else ANY for a in arrays],
+        out_specs=[VMEM] * len(out_shapes),
         out_shape=[pltpu.VMEM(o.shape, o.dtype) for o in out_shapes],
         scratch_shapes=[pltpu.SemaphoreType.DMA((len(out_shapes) * keyframes.shape[0] + 1,))],
         compiler_params=pltpu.CompilerParams(vmem_limit_bytes=8 << 20),

time: 319 us -> 319 us (level)
  no operation moved by 1% of the time
where the time goes in v7:
time: 319 us; the launch traced here: 318 us
  Pallas kernels  160 us (50%)
  waiting for transfers between devices  104 us (33%)
  starting transfers between devices  50.6 us (16%)
    pallas_call x3, Pallas kernels, attend(): pl.pallas_call(functools.partial(attend_kernel, frame=frame, pieces=piece...  147 us
    ppermute x2, waiting for transfers between devices, swap_branch(): return lax.ppermute(value, 'branch', [(0, 1), (1, 0)])  48.5 us
    all_to_all x5, starting transfers between devices, to_heads(): return lax.all_to_all(value, 'seq', split_axis=0, concat_axis=0, tiled=True)  38 us
    ppermute x12, waiting for transfers between devices, shift_x(): lax.ppermute(value, 'mp', [(m, (m + 2 * step) % size) for m in range(size)])  33.8 us
    all_to_all x5, waiting for transfers between devices, to_heads(): return lax.all_to_all(value, 'seq', split_axis=0, concat_axis=0, tiled=True)  17.1 us
    ppermute x12, starting transfers between devices, shift_x(): lax.ppermute(value, 'mp', [(m, (m + 2 * step) % size) for m in range(size)])  9.4 us
  transfers between devices with their start and end apart: 21, of which 15 were waited for; matrix products, arithmetic and copies ran while one was open for 1% of the time, Pallas kernels for 31%

profile of v7, /device:TPU:31, one launch (start us, length us, event | category | flops | bytes accessed | tf_op | source)
XLA Modules:
  0.0 318.0 jit_solution(6534376464104431430)
XLA Ops:
  0.0 2.3 split_heads.1
  2.3 9.2 %all-to-all-start.2 = ((bf16[16,256,128]{2,1,0:T(8,128)(2,1)}), bf16[16,256,128]{2,1,0:T(8,128)(2,1)S(1)}, u32[]{:S(2)}, u32[]{:S(2)}) async-start(bf16[16,256,128]{2,1,0:T(8,128)(2,1)} %bitcast.11), calls=%async_computation.2 | async-start | bytes 2097152 | tf_op jit(solution)/shard_map/all_to_all | solution.py:375
  11.4 0.6 collective-permute-start.1
  12.0 24.3 %collective-permute-done.1.partner_ref = bf16[2,128,2048]{2,1,0:T(8,128)(2,1)} collective-permute-done((bf16[2,128,2048]{2,1,0:T(8,128)(2,1)S(1)}, bf16[2,128,2048]{2,1,0:T(8,128)(2,1)}, u32[]{:S(2)}, u32[]{:S(2)}) %collective-permute-start.1) | collective-permute-done | bytes 1048608 | tf_op jit(solution)/shard_map/ppermute | solution.py:371
  36.3 2.6 blend.3
  38.8 0.6 all-to-all-done.2.refs_2_.source_ref.refs_4_
  39.4 7.2 %all-to-all-start.1 = ((bf16[16,256,128]{2,1,0:T(8,128)(2,1)}), bf16[16,256,128]{2,1,0:T(8,128)(2,1)S(1)}, u32[]{:S(2)}, u32[]{:S(2)}) async-start(bf16[16,256,128]{2,1,0:T(8,128)(2,1)} %blend.3), calls=%async_computation.1 | async-start | bytes 2097152 | tf_op jit(solution)/shard_map/all_to_all | solution.py:375
  46.6 0.6 collective-permute-start
  47.2 24.3 %collective-permute-done.partner_ref = bf16[2,128,2048]{2,1,0:T(8,128)(2,1)} collective-permute-done((bf16[2,128,2048]{2,1,0:T(8,128)(2,1)S(1)}, bf16[2,128,2048]{2,1,0:T(8,128)(2,1)}, u32[]{:S(2)}, u32[]{:S(2)}) %collective-permute-start) | collective-permute-done | bytes 1048608 | tf_op jit(solution)/shard_map/ppermute | solution.py:371
  71.4 2.5 blend.2
  74.0 0.6 all-to-all-done.1.refs_1_.source_ref.refs_3_
  74.6 7.2 %all-to-all-start = ((bf16[16,256,128]{2,1,0:T(8,128)(2,1)}), bf16[16,256,128]{2,1,0:T(8,128)(2,1)S(1)}, u32[]{:S(2)}, u32[]{:S(2)}) async-start(bf16[16,256,128]{2,1,0:T(8,128)(2,1)} %blend.2), calls=%async_computation | async-start | bytes 2097152 | tf_op jit(solution)/shard_map/all_to_all | solution.py:375
  81.8 0.8 shard_map.68
  82.5 1.2 collective-permute-start.10
  83.7 2.7 collective-permute-start.9
  86.4 0.7 shard_map.65
  87.2 0.7 collective-permute-start.2
  87.8 0.1 collective-permute-start.3
  88.0 3.9 %collective-permute-done.10.refs_1_ = bf16[2,16,32,128]{3,2,1,0:T(8,128)(2,1)S(1)} collective-permute-done((bf16[2,16,32,128]{3,2,1,0:T(8,128)(2,1)S(1)}, bf16[2,16,32,128]{3,2,1,0:T(8,128)(2,1)S(1)}, u32[]{:S(2)}, u32[]{:S(2)}) %collective-permute-start.10) | collective-permute-done | bytes 262176 | tf_op jit(solution)/shard_map/ppermute | solution.py:380
  91.9 0.5 collective-permute-start.4
  92.5 6.0 %collective-permute-done.11.refs_2_ = bf16[2,16,32,128]{3,2,1,0:T(8,128)(2,1)S(1)} collective-permute-done((bf16[2,16,32,128]{3,2,1,0:T(8,128)(2,1)S(1)}, bf16[2,16,32,128]{3,2,1,0:T(8,128)(2,1)S(1)}, u32[]{:S(2)}, u32[]{:S(2)}) %collective-permute-start.11) | collective-permute-done | bytes 262176 | tf_op jit(solution)/shard_map/ppermute | solution.py:380
  98.4 0.7 shard_map.69.mine_ref
  99.1 1.0 collective-permute-start.12
  100.1 0.8 collective-permute-done.2.refs_0_
  100.9 2.3 collective-permute-done.3.refs_1_
  103.2 6.0 %collective-permute-done.4.refs_2_ = bf16[2,16,32,128]{3,2,1,0:T(8,128)(2,1)S(1)} collective-permute-done((bf16[2,16,32,128]{3,2,1,0:T(8,128)(2,1)S(1)}, bf16[2,16,32,128]{3,2,1,0:T(8,128)(2,1)S(1)}, u32[]{:S(2)}, u32[]{:S(2)}) %collective-permute-start.4) | collective-permute-done | bytes 262176 | tf_op jit(solution)/shard_map/ppermute | solution.py:380
  109.2 0.7 shard_map.66.mine_ref
  109.9 1.0 collective-permute-start.5
  110.9 1.3 shard_map.70.refs_9_.refs_7_
  112.4 0.2 dynamic-slice_reduce_fusion.1
  112.6 1.9 collective-permute-start.14
  114.6 4.4 %collective-permute-done.5.other_ref = bf16[2,16,32,128]{3,2,1,0:T(8,128)(2,1)} collective-permute-done((bf16[2,16,32,128]{3,2,1,0:T(8,128)(2,1)S(1)}, bf16[2,16,32,128]{3,2,1,0:T(8,128)(2,1)}, u32[]{:S(2)}, u32[]{:S(2)}) %collective-permute-start.5) | collective-permute-done | bytes 262176 | tf_op jit(solution)/shard_map/ppermute | solution.py:385
  119.0 1.7 shard_map.67.refs_5_.refs_3_
  120.8 1.4 collective-permute-start.7
  122.2 0.6 collective-permute-start.8
  122.8 1.8 shard_map.64
  124.7 5.3 %collective-permute-done.15.refs_12_.refs_10_ = bf16[2,16,32,128]{3,2,1,0:T(8,128)(2,1)} collective-permute-done((bf16[2,16,32,128]{3,2,1,0:T(8,128)(2,1)}, bf16[2,16,32,128]{3,2,1,0:T(8,128)(2,1)}, u32[]{:S(2)}, u32[]{:S(2)}) %collective-permute-start.15) | collective-permute-done | bytes 262176 | tf_op jit(solution)/shard_map/ppermute | solution.py:380
  130.0 1.6 collective-permute-done.6.refs_6_.refs_4_
  131.7 0.6 collective-permute-done.7.refs_7_.refs_5_
  132.3 7.3 %collective-permute-done.8.refs_8_.refs_6_ = bf16[2,16,32,128]{3,2,1,0:T(8,128)(2,1)} collective-permute-done((bf16[2,16,32,128]{3,2,1,0:T(8,128)(2,1)}, bf16[2,16,32,128]{3,2,1,0:T(8,128)(2,1)}, u32[]{:S(2)}, u32[]{:S(2)}) %collective-permute-start.8) | collective-permute-done | bytes 262176 | tf_op jit(solution)/shard_map/ppermute | solution.py:380
  139.6 59.3 %shard_map.71 = bf16[16,128,128]{2,1,0:T(8,128)(2,1)} custom-call(s32[3]{0:T(128)S(1)} %pad_add_fusion.1.valid_ref, s32[1]{0:T(128)} %get-tuple-element.13.refs_0_, f32[2048,256]{1,0:T(8,128)S(1)} %get-tuple-element.14.refs_1_, bf16[16,256,128]{2,1,0:T(8,128)(2,1)S(1)} %all-to-all-done.refs_0_.refs_2_, ...), custom_call_target="tpu_custom_call" | custom-call | flops 4294967296 | bytes 4194304 | tf_op jit(solution)/shard_map/pallas_call | solution.py:283
  198.9 7.3 %all-to-all-start.3 = ((bf16[16,128,128]{2,1,0:T(8,128)(2,1)}), bf16[16,128,128]{2,1,0:T(8,128)(2,1)}, u32[]{:S(2)}, u32[]{:S(2)}) async-start(bf16[16,128,128]{2,1,0:T(8,128)(2,1)} %shard_map.71), calls=%async_computation.3 | async-start | bytes 1048576 | tf_op jit(solution)/shard_map/all_to_all | solution.py:375
  206.2 85.6 %shard_map.72 = bf16[16,128,128]{2,1,0:T(8,128)(2,1)} custom-call(s32[3]{0:T(128)S(1)} %pad_add_fusion.valid_ref, bf16[16,256,128]{2,1,0:T(8,128)(2,1)S(1)} %all-to-all-done.refs_0_.refs_2_, bf16[16,256,128]{2,1,0:T(8,128)(2,1)S(1)} %all-to-all-done.1.refs_1_.source_ref.refs_3_, bf16[16,256,128]{2,1,0:T(8,128)(2,1)S(1)} %all-to-all-done.2.refs_2_.source_ref.refs_4_, ...), custom_call_target="tpu_custom_call" | custom-call | flops 6442450944 | bytes 4194304 | tf_op jit(solution)/shard_map/pallas_call | solution.py:283
  291.9 7.2 %all-to-all-start.4 = ((bf16[16,128,128]{2,1,0:T(8,128)(2,1)}), bf16[16,128,128]{2,1,0:T(8,128)(2,1)S(1)}, u32[]{:S(2)}, u32[]{:S(2)}) async-start(bf16[16,128,128]{2,1,0:T(8,128)(2,1)} %shard_map.72), calls=%async_computation.4 | async-start | bytes 1048576 | tf_op jit(solution)/shard_map/all_to_all | solution.py:375
  299.1 1.3 copy.7
  300.4 15.9 %all-to-all-done.4 = bf16[16,128,128]{2,1,0:T(8,128)(2,1)S(1)} async-done(((bf16[16,128,128]{2,1,0:T(8,128)(2,1)}), bf16[16,128,128]{2,1,0:T(8,128)(2,1)S(1)}, u32[]{:S(2)}, u32[]{:S(2)}) %all-to-all-start.4) | async-done | bytes 524320 | tf_op jit(solution)/shard_map/all_to_all | solution.py:375
  316.3 0.3 copy.8
  316.7 1.3 copy.9
  (21 shorter events, 0.5 us)
Async XLA Ops:
  0.0 11.4 %copy-start.1 = (bf16[1,2,128,2048]{3,2,1,0:T(8,128)(2,1)S(1)}, bf16[1,2,128,2048]{3,2,1,0:T(8,128)(2,1)}, u32[]{:S(2)}) copy-start(bf16[1,2,128,2048]{3,2,1,0:T(8,128)(2,1)} %param.7) | copy-start | bytes 3145732
  2.3 37.2 %all-to-all-start.2 = ((bf16[16,256,128]{2,1,0:T(8,128)(2,1)}), bf16[16,256,128]{2,1,0:T(8,128)(2,1)S(1)}, u32[]{:S(2)}, u32[]{:S(2)}) async-start(bf16[16,256,128]{2,1,0:T(8,128)(2,1)} %bitcast.11), calls=%async_computation.2 | async-start | bytes 2097152 | tf_op jit(solution)/shard_map/all_to_all | solution.py:375
  11.4 35.2 %copy-start.2 = (bf16[1,2,128,2048]{3,2,1,0:T(8,128)(2,1)S(1)}, bf16[1,2,128,2048]{3,2,1,0:T(8,128)(2,1)}, u32[]{:S(2)}) copy-start(bf16[1,2,128,2048]{3,2,1,0:T(8,128)(2,1)} %param.6) | copy-start | bytes 3145732
  11.4 24.8 %collective-permute-start.1 = (bf16[2,128,2048]{2,1,0:T(8,128)(2,1)S(1)}, bf16[2,128,2048]{2,1,0:T(8,128)(2,1)}, u32[]{:S(2)}, u32[]{:S(2)}) collective-permute-start(bf16[2,128,2048]{2,1,0:T(8,128)(2,1)S(1)} %bitcast.17), channel_id=1, source_target_pairs={{0,128},{128,0},{1,129},{129,1},{2,130},{130,2},{3,131},{131,3},{4... | collective-permute-start | bytes 3145736 | tf_op jit(solution)/shard_map/ppermute | solution.py:371
  39.4 35.2 %all-to-all-start.1 = ((bf16[16,256,128]{2,1,0:T(8,128)(2,1)}), bf16[16,256,128]{2,1,0:T(8,128)(2,1)S(1)}, u32[]{:S(2)}, u32[]{:S(2)}) async-start(bf16[16,256,128]{2,1,0:T(8,128)(2,1)} %blend.3), calls=%async_computation.1 | async-start | bytes 2097152 | tf_op jit(solution)/shard_map/all_to_all | solution.py:375
  46.6 35.1 %copy-start = (s32[2]{0:T(128)S(1)}, s32[2]{0:T(128)}, u32[]{:S(2)}) copy-start(s32[2]{0:T(128)} %keyframes_ref.11) | copy-start | bytes 28
  46.6 24.8 %collective-permute-start = (bf16[2,128,2048]{2,1,0:T(8,128)(2,1)S(1)}, bf16[2,128,2048]{2,1,0:T(8,128)(2,1)}, u32[]{:S(2)}, u32[]{:S(2)}) collective-permute-start(bf16[2,128,2048]{2,1,0:T(8,128)(2,1)S(1)} %bitcast.19), channel_id=1, source_target_pairs={{0,128},{128,0},{1,129},{129,1},{2,130},{130,2},{3,131},{131,3},{4... | collective-permute-start | bytes 3145736 | tf_op jit(solution)/shard_map/ppermute | solution.py:371
  74.6 48.2 %all-to-all-start = ((bf16[16,256,128]{2,1,0:T(8,128)(2,1)}), bf16[16,256,128]{2,1,0:T(8,128)(2,1)S(1)}, u32[]{:S(2)}, u32[]{:S(2)}) async-start(bf16[16,256,128]{2,1,0:T(8,128)(2,1)} %blend.2), calls=%async_computation | async-start | bytes 2097152 | tf_op jit(solution)/shard_map/all_to_all | solution.py:375
  82.5 9.4 %collective-permute-start.10 = (bf16[2,16,32,128]{3,2,1,0:T(8,128)(2,1)S(1)}, bf16[2,16,32,128]{3,2,1,0:T(8,128)(2,1)S(1)}, u32[]{:S(2)}, u32[]{:S(2)}) collective-permute-start(bf16[2,16,32,128]{3,2,1,0:T(8,128)(2,1)S(1)} %get-tuple-element.19), channel_id=1, source_target_pairs={{0,4},{1,5},{2,6},{3,7},{4,0},{5,1},{6,2},{7,3},{8,12},{9,13},{10,... | collective-permute-start | bytes 786440 | tf_op jit(solution)/shard_map/ppermute | solution.py:380
  83.7 14.7 %collective-permute-start.11 = (bf16[2,16,32,128]{3,2,1,0:T(8,128)(2,1)S(1)}, bf16[2,16,32,128]{3,2,1,0:T(8,128)(2,1)S(1)}, u32[]{:S(2)}, u32[]{:S(2)}) collective-permute-start(bf16[2,16,32,128]{3,2,1,0:T(8,128)(2,1)S(1)} %get-tuple-element.20), channel_id=1, source_target_pairs={{0,6},{1,7},{2,0},{3,1},{4,2},{5,3},{6,4},{7,5},{8,14},{9,15},{10,... | collective-permute-start | bytes 786440 | tf_op jit(solution)/shard_map/ppermute | solution.py:380
  83.7 14.7 %collective-permute-start.9 = (bf16[2,16,32,128]{3,2,1,0:T(8,128)(2,1)S(1)}, bf16[2,16,32,128]{3,2,1,0:T(8,128)(2,1)S(1)}, u32[]{:S(2)}, u32[]{:S(2)}) collective-permute-start(bf16[2,16,32,128]{3,2,1,0:T(8,128)(2,1)S(1)} %get-tuple-element.18), channel_id=1, source_target_pairs={{0,2},{1,3},{2,4},{3,5},{4,6},{5,7},{6,0},{7,1},{8,10},{9,11},{10,... | collective-permute-start | bytes 786440 | tf_op jit(solution)/shard_map/ppermute | solution.py:380
  87.2 13.8 %collective-permute-start.2 = (bf16[2,16,32,128]{3,2,1,0:T(8,128)(2,1)S(1)}, bf16[2,16,32,128]{3,2,1,0:T(8,128)(2,1)S(1)}, u32[]{:S(2)}, u32[]{:S(2)}) collective-permute-start(bf16[2,16,32,128]{3,2,1,0:T(8,128)(2,1)S(1)} %get-tuple-element.15), channel_id=1, source_target_pairs={{0,2},{1,3},{2,4},{3,5},{4,6},{5,7},{6,0},{7,1},{8,10},{9,11},{10,... | collective-permute-start | bytes 786440 | tf_op jit(solution)/shard_map/ppermute | solution.py:380
  87.8 15.3 %collective-permute-start.3 = (bf16[2,16,32,128]{3,2,1,0:T(8,128)(2,1)S(1)}, bf16[2,16,32,128]{3,2,1,0:T(8,128)(2,1)S(1)}, u32[]{:S(2)}, u32[]{:S(2)}) collective-permute-start(bf16[2,16,32,128]{3,2,1,0:T(8,128)(2,1)S(1)} %get-tuple-element.16), channel_id=1, source_target_pairs={{0,4},{1,5},{2,6},{3,7},{4,0},{5,1},{6,2},{7,3},{8,12},{9,13},{10,... | collective-permute-start | bytes 786440 | tf_op jit(solution)/shard_map/ppermute | solution.py:380
  91.9 20.4 %copy-start.3 = (s32[16,2]{0,1:T(2,128)S(1)}, s32[16,2]{0,1:T(2,128)}, u32[]{:S(2)}) copy-start(s32[16,2]{0,1:T(2,128)} %param.11) | copy-start | bytes 388
  91.9 17.3 %collective-permute-start.4 = (bf16[2,16,32,128]{3,2,1,0:T(8,128)(2,1)S(1)}, bf16[2,16,32,128]{3,2,1,0:T(8,128)(2,1)S(1)}, u32[]{:S(2)}, u32[]{:S(2)}) collective-permute-start(bf16[2,16,32,128]{3,2,1,0:T(8,128)(2,1)S(1)} %get-tuple-element.17), channel_id=1, source_target_pairs={{0,6},{1,7},{2,0},{3,1},{4,2},{5,3},{6,4},{7,5},{8,14},{9,15},{10,... | collective-permute-start | bytes 786440 | tf_op jit(solution)/shard_map/ppermute | solution.py:380
  99.1 11.8 %collective-permute-start.12 = (bf16[2,16,32,128]{3,2,1,0:T(8,128)(2,1)S(1)}, bf16[2,16,32,128]{3,2,1,0:T(8,128)(2,1)S(1)}, u32[]{:S(2)}, u32[]{:S(2)}) collective-permute-start(bf16[2,16,32,128]{3,2,1,0:T(8,128)(2,1)S(1)} %shard_map.69.mine_ref), channel_id=1, source_target_pairs={{0,1},{1,0},{2,3},{3,2},{4,5},{5,4},{6,7},{7,6},{8,9},{9,8},{10,11... | collective-permute-start | bytes 786440 | tf_op jit(solution)/shard_map/ppermute | solution.py:385
  109.9 9.1 %collective-permute-start.5 = (bf16[2,16,32,128]{3,2,1,0:T(8,128)(2,1)S(1)}, bf16[2,16,32,128]{3,2,1,0:T(8,128)(2,1)}, u32[]{:S(2)}, u32[]{:S(2)}) collective-permute-start(bf16[2,16,32,128]{3,2,1,0:T(8,128)(2,1)S(1)} %shard_map.66.mine_ref), channel_id=1, source_target_pairs={{0,1},{1,0},{2,3},{3,2},{4,5},{5,4},{6,7},{7,6},{8,9},{9,8},{10,11... | collective-permute-start | bytes 786440 | tf_op jit(solution)/shard_map/ppermute | solution.py:385
  112.3 9.9 %collective-permute-start.13 = (bf16[2,16,32,128]{3,2,1,0:T(8,128)(2,1)}, bf16[2,16,32,128]{3,2,1,0:T(8,128)(2,1)}, u32[]{:S(2)}, u32[]{:S(2)}) collective-permute-start(bf16[2,16,32,128]{3,2,1,0:T(8,128)(2,1)} %shard_map.70.refs_9_.refs_7_), channel_id=1, source_target_pairs={{0,2},{1,3},{2,4},{3,5},{4,6},{5,7},{6,0},{7,1},{8,10},{9,11},{10,... | collective-permute-start | bytes 786440 | tf_op jit(solution)/shard_map/ppermute | solution.py:380
  112.6 12.1 %collective-permute-start.14 = (bf16[2,16,32,128]{3,2,1,0:T(8,128)(2,1)}, bf16[2,16,32,128]{3,2,1,0:T(8,128)(2,1)}, u32[]{:S(2)}, u32[]{:S(2)}) collective-permute-start(bf16[2,16,32,128]{3,2,1,0:T(8,128)(2,1)} %shard_map.70.refs_9_.refs_7_), channel_id=1, source_target_pairs={{0,4},{1,5},{2,6},{3,7},{4,0},{5,1},{6,2},{7,3},{8,12},{9,13},{10,... | collective-permute-start | bytes 786440 | tf_op jit(solution)/shard_map/ppermute | solution.py:380
  114.5 15.5 %collective-permute-start.15 = (bf16[2,16,32,128]{3,2,1,0:T(8,128)(2,1)}, bf16[2,16,32,128]{3,2,1,0:T(8,128)(2,1)}, u32[]{:S(2)}, u32[]{:S(2)}) collective-permute-start(bf16[2,16,32,128]{3,2,1,0:T(8,128)(2,1)} %shard_map.70.refs_9_.refs_7_), channel_id=1, source_target_pairs={{0,6},{1,7},{2,0},{3,1},{4,2},{5,3},{6,4},{7,5},{8,14},{9,15},{10,... | collective-permute-start | bytes 786440 | tf_op jit(solution)/shard_map/ppermute | solution.py:380
  120.7 11.0 %collective-permute-start.6 = (bf16[2,16,32,128]{3,2,1,0:T(8,128)(2,1)}, bf16[2,16,32,128]{3,2,1,0:T(8,128)(2,1)S(1)}, u32[]{:S(2)}, u32[]{:S(2)}) collective-permute-start(bf16[2,16,32,128]{3,2,1,0:T(8,128)(2,1)} %shard_map.67.refs_5_.refs_3_), channel_id=1, source_target_pairs={{0,2},{1,3},{2,4},{3,5},{4,6},{5,7},{6,0},{7,1},{8,10},{9,11},{10,... | collective-permute-start | bytes 786440 | tf_op jit(solution)/shard_map/ppermute | solution.py:380
  120.8 11.5 %collective-permute-start.7 = (bf16[2,16,32,128]{3,2,1,0:T(8,128)(2,1)}, bf16[2,16,32,128]{3,2,1,0:T(8,128)(2,1)}, u32[]{:S(2)}, u32[]{:S(2)}) collective-permute-start(bf16[2,16,32,128]{3,2,1,0:T(8,128)(2,1)} %shard_map.67.refs_5_.refs_3_), channel_id=1, source_target_pairs={{0,4},{1,5},{2,6},{3,7},{4,0},{5,1},{6,2},{7,3},{8,12},{9,13},{10,... | collective-permute-start | bytes 786440 | tf_op jit(solution)/shard_map/ppermute | solution.py:380
  122.2 17.4 %collective-permute-start.8 = (bf16[2,16,32,128]{3,2,1,0:T(8,128)(2,1)}, bf16[2,16,32,128]{3,2,1,0:T(8,128)(2,1)}, u32[]{:S(2)}, u32[]{:S(2)}) collective-permute-start(bf16[2,16,32,128]{3,2,1,0:T(8,128)(2,1)} %shard_map.67.refs_5_.refs_3_), channel_id=1, source_target_pairs={{0,6},{1,7},{2,0},{3,1},{4,2},{5,3},{6,4},{7,5},{8,14},{9,15},{10,... | collective-permute-start | bytes 786440 | tf_op jit(solution)/shard_map/ppermute | solution.py:380
  198.9 93.0 %all-to-all-start.3 = ((bf16[16,128,128]{2,1,0:T(8,128)(2,1)}), bf16[16,128,128]{2,1,0:T(8,128)(2,1)}, u32[]{:S(2)}, u32[]{:S(2)}) async-start(bf16[16,128,128]{2,1,0:T(8,128)(2,1)} %shard_map.71), calls=%async_computation.3 | async-start | bytes 1048576 | tf_op jit(solution)/shard_map/all_to_all | solution.py:375
  291.9 24.4 %all-to-all-start.4 = ((bf16[16,128,128]{2,1,0:T(8,128)(2,1)}), bf16[16,128,128]{2,1,0:T(8,128)(2,1)S(1)}, u32[]{:S(2)}, u32[]{:S(2)}) async-start(bf16[16,128,128]{2,1,0:T(8,128)(2,1)} %shard_map.72), calls=%async_computation.4 | async-start | bytes 1048576 | tf_op jit(solution)/shard_map/all_to_all | solution.py:375
